TPU v7x, 32 devices: a whole 2x2x4 slice. The times are simulated.
32 devices in a mesh: blk: 8 (over z, x), table: 4 (over y, core).
Axes of the slice: x: 2, y: 2, z: 4, core: 2. Of those that a mesh axis runs over, the one named last changes fastest.
Arguments:
- hot_slab: bfloat16 [128, 128], P('blk'), may hold values from -1.5 to 1.5
- hot_ids: int32 [4096, 16], P(('blk', 'table')), may hold values from 0 to 127
- dense: bfloat16 [4096, 128], P(('blk', 'table')), may hold values from -6 to 6
- cold_ids: int32 [4096, 26], P(('blk', 'table')), may hold values from 0 to 511
- table_slot: int32 [26], replicated, may hold values from 0 to 27, as said below
- cold_tables: bfloat16 [28, 512, 128], P('table'), may hold values from -6 to 6
- down_rank: bfloat16 [3456, 512], replicated, may hold values from -0.109375 to 0.109375
- up_rank: bfloat16 [512, 3456], replicated, may hold values from -0.25 to 0.25
- cross_bias: float32 [3456], replicated, may hold values from -3 to 3
- cotangent: bfloat16 [4096, 3456], P(('blk', 'table')), may hold values from -6 to 6
Outputs:
- crossed: bfloat16 [4096, 3456], P(('blk', 'table'))
- table_grad: float32 [8, 28, 512, 128], P('blk', 'table')
Inputs may be any that keep to these rules, and one draw needn't show every extreme that they name: `table_slot`: distinct values; some owner has all 7 of its slots taken.
All inputs are finite; a program needn't handle non-finite values.
Results may differ from a plain program's by a relative error of at most 0.0052.
Values may be sent and summed in bfloat16 or wider, within the bound.
No kernel may reach another device: no remote copies, remote signals or barrier semaphores. Data moves between devices by JAX's collectives and lax.ppermute only.
A program may use at most 64 MiB of HBM per device.

v0:
```python
import jax
import jax.numpy as jnp
from jax import lax
from jax.sharding import PartitionSpec as P


def bag_counts(row_ids, width_rows):
    positions = lax.broadcasted_iota(jnp.int32, (row_ids.shape[0], width_rows), 1)
    counts = jnp.zeros((row_ids.shape[0], width_rows), jnp.float32)
    for bag_index in range(row_ids.shape[1]):
        local_ids = row_ids[:, bag_index : bag_index + 1]
        counts = counts + (local_ids == positions).astype(jnp.float32)
    return counts.astype(jnp.bfloat16)


def on_device(
    hot_slab,
    hot_ids,
    dense,
    cold_ids,
    table_slot,
    cold_tables,
    down_rank,
    up_rank,
    cross_bias,
    cotangent,
):
    batch_rows = dense.shape[0]
    width = hot_slab.shape[1]
    table_count = table_slot.shape[0]
    owners = lax.axis_size("table")
    slots = cold_tables.shape[0]
    table_rows = cold_tables.shape[1]
    slot_total = owners * slots
    block_rows = lax.all_gather(hot_slab, "blk", axis=0, tiled=True)
    counts = bag_counts(hot_ids, block_rows.shape[0])
    pooled = jnp.dot(counts, block_rows, preferred_element_type=jnp.float32)
    front_row = (dense.astype(jnp.float32) + pooled).astype(jnp.bfloat16)
    slot_match = (
        table_slot[:, None] == lax.broadcasted_iota(jnp.int32, (table_count, slot_total), 1)
    ).astype(jnp.int32)
    send_ids = jnp.sum(cold_ids[:, :, None] * slot_match[None, :, :], axis=1).reshape(
        batch_rows, owners, slots
    )
    ids_block = lax.all_to_all(send_ids, "table", split_axis=1, concat_axis=1, tiled=True)
    item_count = ids_block.shape[0]
    row_count = item_count * ids_block.shape[1]
    columns = lax.broadcasted_iota(jnp.int32, (row_count, table_rows), 1)
    pieces = []
    for lookup_slot_index in range(slots):
        lookup_slot_ids = ids_block[:, :, lookup_slot_index].reshape(row_count, 1)
        lookup_selector = (lookup_slot_ids == columns).astype(jnp.bfloat16)
        rows_out = jnp.dot(
            lookup_selector, cold_tables[lookup_slot_index], preferred_element_type=jnp.float32
        )
        pieces.append(rows_out.astype(jnp.bfloat16).reshape(item_count, ids_block.shape[1], width))
    fetched_rows = jnp.stack(pieces, axis=2)
    returned = lax.all_to_all(fetched_rows, "table", split_axis=1, concat_axis=1, tiled=True)
    slot_pick = slot_match.astype(jnp.bfloat16)
    cold_rows = jnp.einsum(
        "skd,tk->std",
        returned.reshape(batch_rows, slot_total, width),
        slot_pick,
        preferred_element_type=jnp.float32,
    ).astype(jnp.bfloat16)
    feat_count = (table_count + 1) * width
    features = jnp.concatenate([front_row[:, None, :], cold_rows], axis=1).reshape(
        batch_rows, feat_count
    )
    low_rank = jnp.dot(features, down_rank, preferred_element_type=jnp.float32).astype(jnp.bfloat16)
    gate = jnp.dot(low_rank, up_rank, preferred_element_type=jnp.float32) + cross_bias[None, :]
    feat_wide = features.astype(jnp.float32)
    crossed = (feat_wide * gate + feat_wide).astype(jnp.bfloat16)
    cot_wide = cotangent.astype(jnp.float32)
    mixed = (cot_wide * feat_wide).astype(jnp.bfloat16)
    grad_low = jnp.dot(mixed, up_rank.T, preferred_element_type=jnp.float32).astype(jnp.bfloat16)
    grad_in = cot_wide * (gate + 1.0) + jnp.dot(
        grad_low, down_rank.T, preferred_element_type=jnp.float32
    )
    grad_in = grad_in.astype(jnp.bfloat16)
    grad_cold = grad_in.reshape(batch_rows, table_count + 1, width)[:, 1:, :]
    grad_slots = jnp.einsum("std,tk->skd", grad_cold, slot_pick, preferred_element_type=jnp.float32)
    grad_slots = grad_slots.astype(jnp.bfloat16).reshape(batch_rows, owners, slots, width)
    arrived = lax.all_to_all(grad_slots, "table", split_axis=1, concat_axis=1, tiled=True)
    row_positions = lax.broadcasted_iota(jnp.int32, (table_rows, batch_rows * owners), 0)
    slot_grads = []
    for slot_index in range(slots):
        slot_ids = ids_block[:, :, slot_index].reshape(1, batch_rows * owners)
        slot_rows = arrived[:, :, slot_index, :].reshape(batch_rows * owners, width)
        selector = (row_positions == slot_ids).astype(jnp.bfloat16)
        slot_grads.append(jnp.dot(selector, slot_rows, preferred_element_type=jnp.float32))
    table_grad = jnp.stack(slot_grads, axis=0)[None]
    return (crossed, table_grad)


def solution(mesh):
    placed = (
        P("blk", None),
        P(("blk", "table"), None),
        P(("blk", "table"), None),
        P(("blk", "table"), None),
        P(),
        P("table", None, None),
        P(),
        P(),
        P(),
        P(("blk", "table"), None),
    )
    return jax.shard_map(
        on_device,
        mesh=mesh,
        in_specs=placed,
        out_specs=(P(("blk", "table"), None), P("blk", "table", None, None)),
        check_vma=False,
    )
```

profile of v0, /device:TPU:0, one launch (start us, length us, event | category | flops | bytes accessed | tf_op | source)
XLA Modules:
  0.0 134.0 jit_solution(799297158164035277)
XLA Ops:
  0.6 1.4 %fusion.62 = s32[26,28]{0,1:T(8,128)} fusion(s32[26]{0:T(128)} %param.14), kind=kLoop, calls=%fused_computation.124 | loop fusion | flops 1456 | bytes 3016 | tf_op jit(solution)/shard_map/convert_element_type | solution.py:41
  2.1 0.8 copy.51
  2.9 1.5 %multiply_reduce_fusion = s32[128,28]{0,1:T(8,128)} fusion(s32[26,28]{1,0:T(8,128)S(1)} %copy.51, s32[128,26]{0,1:T(8,128)} %param.13), kind=kLoop, calls=%fused_computation.68 | loop fusion | flops 182784 | bytes 30560 | tf_op jit(solution)/shard_map/reduce_sum | solution.py:42
  4.4 0.7 reshape.50
  5.1 7.9 %all_to_all.15 = s32[128,4,7]{0,2,1:T(8,128)S(1)} all-to-all(s32[128,4,7]{0,2,1:T(8,128)S(1)} %reshape.50), channel_id=1, replica_groups=mesh['blk'=8,'table'=4] {'table'}, dimensions={1} | all-to-all | bytes 28672 | tf_op jit(solution)/shard_map/all_to_all | solution.py:45
  13.6 1.4 %copy.58 = s32[128,4,1]{1,0,2:T(8,128)} copy(s32[128,4,1]{0,2,1:T(1,128)} %get-tuple-element.9) | data formatting | bytes 4096 | tf_op jit(solution)/shard_map/slice | solution.py:51
  15.0 1.5 %eq.366 = s32[512]{0:T(512)} reshape(s32[128,4,1]{1,0,2:T(8,128)} %copy.58) | data formatting | bytes 4096 | tf_op jit(solution)/shard_map/eq | solution.py:52
  16.5 1.4 %copy.57 = s32[128,4,1]{1,0,2:T(8,128)} copy(s32[128,4,1]{0,2,1:T(1,128)} %get-tuple-element.10) | data formatting | bytes 4096 | tf_op jit(solution)/shard_map/slice | solution.py:51
  17.9 1.5 %eq.363 = s32[512]{0:T(512)} reshape(s32[128,4,1]{1,0,2:T(8,128)} %copy.57) | data formatting | bytes 4096 | tf_op jit(solution)/shard_map/eq | solution.py:52
  19.5 1.4 %copy.56 = s32[128,4,1]{1,0,2:T(8,128)} copy(s32[128,4,1]{0,2,1:T(1,128)} %get-tuple-element.11) | data formatting | bytes 4096 | tf_op jit(solution)/shard_map/slice | solution.py:51
  20.9 1.5 %eq.360 = s32[512]{0:T(512)} reshape(s32[128,4,1]{1,0,2:T(8,128)} %copy.56) | data formatting | bytes 4096 | tf_op jit(solution)/shard_map/eq | solution.py:52
  22.4 0.7 copy.55
  23.1 1.5 %eq.357 = s32[512]{0:T(512)} reshape(s32[128,4,1]{1,0,2:T(8,128)} %copy.55) | data formatting | bytes 4096 | tf_op jit(solution)/shard_map/eq | solution.py:52
  24.7 0.7 copy.54
  25.4 1.5 %eq.354 = s32[512]{0:T(512)} reshape(s32[128,4,1]{1,0,2:T(8,128)} %copy.54) | data formatting | bytes 4096 | tf_op jit(solution)/shard_map/eq | solution.py:52
  26.9 0.7 copy.53
  27.7 0.9 eq.351
  28.6 0.7 copy.52
  29.4 1.5 %eq.348 = s32[512]{0:T(512)} reshape(s32[128,4,1]{1,0,2:T(8,128)} %copy.52) | data formatting | bytes 4096 | tf_op jit(solution)/shard_map/eq | solution.py:52
  30.9 1.3 convolution_convert_fusion.10
  32.2 1.3 convolution_convert_fusion.9
  33.4 1.3 convolution_convert_fusion.8
  34.7 1.3 convolution_convert_fusion.7
  36.0 1.3 convolution_convert_fusion.6
  37.3 1.3 convolution_convert_fusion.5
  38.6 1.3 convolution_convert_fusion.4
  39.8 0.7 copy_dynamic-update-slice_fusion.6
  41.9 0.7 copy_dynamic-update-slice_fusion.3
  42.5 0.7 copy_dynamic-update-slice_fusion.2
  43.2 0.7 copy_dynamic-update-slice_fusion.1
  43.9 0.7 copy_dynamic-update-slice_fusion
  44.6 4.2 %all-to-all-start.1 = ((bf16[128,4,7,128]{3,0,2,1:T(8,128)(2,1)}), bf16[128,4,7,128]{3,0,2,1:T(8,128)(2,1)}, u32[]{:S(2)}, u32[]{:S(2)}) async-start(bf16[128,4,7,128]{3,0,2,1:T(8,128)(2,1)} %copy_dynamic-update-slice_fusion), calls=%async_computation.1 | async-start | bytes 1835008 | tf_op jit(solution)/shard_map/all_to_all | solution.py:58
  48.8 1.5 %copy.50 = bf16[128,128]{0,1:T(8,128)(2,1)} copy(bf16[128,128]{1,0:T(8,128)(2,1)} %param.12) | data formatting | bytes 65536 | tf_op args[2]
  50.3 30.9 %all_gather.3 = bf16[128,128]{1,0:T(8,128)(2,1)S(1)} all-gather(bf16[16,128]{1,0:T(8,128)(2,1)S(1)} %copy-done.6), channel_id=1, replica_groups=mesh['blk'=8,'table'=4] {'blk'}, dimensions={0}, use_global_device_ids=true | all-gather | bytes 36864 | tf_op jit(solution)/shard_map/all_gather | solution.py:35
  81.2 1.9 %fusion.13 = bf16[128,1,128]{0,2,1:T(8,128)(2,1)} fusion(bf16[128,128]{1,0:T(8,128)(2,1)S(1)} %all_gather.3, bf16[128,128]{0,1:T(8,128)(2,1)} %copy.50, s32[128]{0:T(128)S(1)} %get-tuple-element.30, s32[128]{0:T(128)S(1)} %get-tuple-element.31, s32[128]{0:T(128)S(1)} %get-tuple-element.17, s32[128]{0:T(128)S(1)} %get-tuple-element.18, ...), kind=kOutput, calls=%fused_computation.37 | convolution fusion | flops 5029888 | bytes 106496 | tf_op jit(solution)/shard_map/dot_general | solution.py:37
  83.1 1.5 %copy.68 = bf16[128,1,128]{2,1,0:T(2,128)(2,1)} copy(bf16[128,1,128]{0,2,1:T(8,128)(2,1)} %fusion.13) | data formatting | bytes 65536 | tf_op jit(solution)/shard_map/broadcast_in_dim | solution.py:67
  84.6 1.9 %fusion.3 = bf16[128,26,128]{2,1,0:T(8,128)(2,1)S(1)} fusion(bf16[128,28,128]{2,0,1:T(8,128)(2,1)} %bitcast.32, s32[26]{0:T(128)S(1)} %copy-done.4), kind=kOutput, calls=%fused_computation.10 | convolution fusion | flops 24283272 | bytes 1769576 | tf_op jit(solution)/shard_map/skd,tk->std/dot_general | solution.py:60
  86.5 1.5 %pad_maximum_fusion = bf16[128,27,128]{2,1,0:T(8,128)(2,1)} fusion(bf16[128,26,128]{2,1,0:T(8,128)(2,1)S(1)} %fusion.3, bf16[128,1,128]{2,1,0:T(2,128)(2,1)S(1)} %copy-done.1), kind=kLoop, calls=%fused_computation.38 | loop fusion | flops 1769472 | bytes 1769472 | tf_op jit(solution)/shard_map/concatenate | solution.py:67
  88.0 2.6 %copy.69 = bf16[128,27,128]{0,2,1:T(8,128)(2,1)} copy(bf16[128,27,128]{2,1,0:T(8,128)(2,1)} %pad_maximum_fusion) | data formatting | bytes 1769472 | tf_op jit(solution)/shard_map/concatenate | solution.py:67
  90.6 2.2 %copy.70 = bf16[128,3456]{1,0:T(8,128)(2,1)} copy(bf16[128,3456]{0,1:T(8,128)(2,1)} %bitcast.142) | data formatting | bytes 1769472 | tf_op jit(solution)/shard_map/reshape | solution.py:67
  92.9 5.3 %fusion.2 = (bf16[128,3456]{1,0:T(8,128)(2,1)}, f32[128,3456]{1,0:T(8,128)}) fusion(bf16[128,3456]{1,0:T(8,128)(2,1)} %copy.70, f32[3456]{0:T(1024)S(1)} %copy-done.2, bf16[512,3456]{1,0:T(8,128)(2,1)S(1)} %copy-done, bf16[128,3456]{0,1:T(8,128)(2,1)} %bitcast.143, bf16[3456,512]{1,0:T(8,128)(2,1)} %param.16), kind=kOutput, calls=%fused_computation.7 | convolution fusion | flops 908247040 | bytes 11515392 | tf_op jit(solution)/shard_map/dot_general | solution.py:71
  98.2 6.3 %fusion = bf16[128,3456]{1,0:T(8,128)(2,1)} fusion(bf16[3456,512]{1,0:T(8,128)(2,1)} %param.16, bf16[128,3456]{1,0:T(8,128)(2,1)} %param.19, f32[128,3456]{1,0:T(8,128)} %get-tuple-element.33, bf16[512,3456]{1,0:T(8,128)(2,1)S(1)} %copy-done, bf16[128,3456]{1,0:T(8,128)(2,1)} %copy.70), kind=kOutput, calls=%fused_computation.2 | convolution fusion | flops 910016512 | bytes 11501568 | tf_op jit(solution)/shard_map/dot_general | solution.py:77
  104.5 2.2 %copy.71 = bf16[128,3456]{0,1:T(8,128)(2,1)} copy(bf16[128,3456]{1,0:T(8,128)(2,1)} %fusion) | data formatting | bytes 1769472 | tf_op jit(solution)/shard_map/convert_element_type | solution.py:80
  106.7 2.2 %slice.166 = bf16[128,26,128]{0,2,1:T(8,128)(2,1)} slice(bf16[128,27,128]{0,2,1:T(8,128)(2,1)} %bitcast.145), slice={[0:128], [1:27], [0:128]} | slice | bytes 1703936 | tf_op jit(solution)/shard_map/slice | solution.py:81
  108.9 2.6 %copy.83 = bf16[128,26,128]{2,1,0:T(8,128)(2,1)} copy(bf16[128,26,128]{0,2,1:T(8,128)(2,1)} %slice.166) | data formatting | bytes 1703936
  111.5 1.6 %fusion.4 = bf16[128,28,128]{2,1,0:T(8,128)(2,1)S(1)} fusion(bf16[128,26,128]{2,1,0:T(8,128)(2,1)} %copy.83, s32[26]{0:T(128)S(1)} %copy-done.5), kind=kOutput, calls=%fused_computation.11 | convolution fusion | flops 24316040 | bytes 1769576 | tf_op jit(solution)/shard_map/std,tk->skd/dot_general | solution.py:82
  113.5 16.1 %all_to_all.16 = bf16[128,4,7,128]{3,0,2,1:T(8,128)(2,1)S(1)} all-to-all(bf16[128,4,7,128]{3,0,2,1:T(8,128)(2,1)S(1)} %bitcast.144), channel_id=1, replica_groups=mesh['blk'=8,'table'=4] {'table'}, dimensions={1} | all-to-all | bytes 1835008 | tf_op jit(solution)/shard_map/all_to_all | solution.py:84
  132.8 1.2 copy-done.18
  (58 shorter events, 5.4 us)
Async XLA Ops:
  0.6 92.2 %copy-start = (bf16[512,3456]{1,0:T(8,128)(2,1)S(1)}, bf16[512,3456]{1,0:T(8,128)(2,1)}, u32[]{:S(2)}) copy-start(bf16[512,3456]{1,0:T(8,128)(2,1)} %param.17) | copy-start | bytes 10616836
  23.1 12.9 %copy-start.10 = (s32[512]{0:T(512)S(1)}, s32[512]{0:T(512)}, u32[]{:S(2)}) copy-start(s32[512]{0:T(512)} %eq.360) | copy-start | bytes 6148
  25.4 9.3 %copy-start.12 = (s32[512]{0:T(512)S(1)}, s32[512]{0:T(512)}, u32[]{:S(2)}) copy-start(s32[512]{0:T(512)} %eq.357) | copy-start | bytes 6148
  28.6 9.9 %copy-start.15 = (s32[512]{0:T(512)}, s32[512]{0:T(512)S(1)}, u32[]{:S(2)}) copy-start(s32[512]{0:T(512)S(1)} %eq.351) | copy-start | bytes 6148
  29.4 9.2 %copy-start.7 = (s32[512]{0:T(512)S(1)}, s32[512]{0:T(512)}, u32[]{:S(2)}) copy-start(s32[512]{0:T(512)} %eq.366) | copy-start | bytes 6148
  39.8 10.5 %copy-start.6 = (bf16[16,128]{1,0:T(8,128)(2,1)S(1)}, bf16[16,128]{1,0:T(8,128)(2,1)}, u32[]{:S(2)}) copy-start(bf16[16,128]{1,0:T(8,128)(2,1)} %param.10) | copy-start | bytes 12292
  39.8 41.4 %copy-start.3 = (s32[128,16]{0,1:T(8,128)S(1)}, s32[128,16]{0,1:T(8,128)}, u32[]{:S(2)}) copy-start(s32[128,16]{0,1:T(8,128)} %param.11) | copy-start | bytes 24580
  43.2 41.4 %copy-start.4 = (s32[26]{0:T(128)S(1)}, s32[26]{0:T(128)}, u32[]{:S(2)}) copy-start(s32[26]{0:T(128)} %param.14) | copy-start | bytes 316
  44.6 40.0 %all-to-all-start.1 = ((bf16[128,4,7,128]{3,0,2,1:T(8,128)(2,1)}), bf16[128,4,7,128]{3,0,2,1:T(8,128)(2,1)}, u32[]{:S(2)}, u32[]{:S(2)}) async-start(bf16[128,4,7,128]{3,0,2,1:T(8,128)(2,1)} %copy_dynamic-update-slice_fusion), calls=%async_computation.1 | async-start | bytes 1835008 | tf_op jit(solution)/shard_map/all_to_all | solution.py:58
  84.6 1.9 %copy-start.1 = (bf16[128,1,128]{2,1,0:T(2,128)(2,1)S(1)}, bf16[128,1,128]{2,1,0:T(2,128)(2,1)}, u32[]{:S(2)}) copy-start(bf16[128,1,128]{2,1,0:T(2,128)(2,1)} %copy.68) | copy-start | bytes 98308
  88.0 4.8 %copy-start.2 = (f32[3456]{0:T(1024)S(1)}, f32[3456]{0:T(1024)}, u32[]{:S(2)}) copy-start(f32[3456]{0:T(1024)} %param.18) | copy-start | bytes 41476
  106.7 4.8 %copy-start.5 = (s32[26]{0:T(128)S(1)}, s32[26]{0:T(128)}, u32[]{:S(2)}) copy-start(s32[26]{0:T(128)} %param.14) | copy-start | bytes 316
  129.6 0.9 copy-start.17
  129.6 1.3 copy-start.16
  129.7 1.5 %copy-start.14 = (s32[512]{0:T(512)S(1)}, s32[512]{0:T(512)}, u32[]{:S(2)}) copy-start(s32[512]{0:T(512)} %eq.354) | copy-start | bytes 6148
  129.7 1.8 %copy-start.13 = (s32[512]{0:T(512)S(1)}, s32[512]{0:T(512)}, u32[]{:S(2)}) copy-start(s32[512]{0:T(512)} %eq.357) | copy-start | bytes 6148
  129.9 1.9 %copy-start.11 = (s32[512]{0:T(512)S(1)}, s32[512]{0:T(512)}, u32[]{:S(2)}) copy-start(s32[512]{0:T(512)} %eq.360) | copy-start | bytes 6148
  130.2 2.0 %copy-start.9 = (s32[512]{0:T(512)S(1)}, s32[512]{0:T(512)}, u32[]{:S(2)}) copy-start(s32[512]{0:T(512)} %eq.363) | copy-start | bytes 6148
  130.4 2.0 %copy-start.8 = (s32[512]{0:T(512)S(1)}, s32[512]{0:T(512)}, u32[]{:S(2)}) copy-start(s32[512]{0:T(512)} %eq.366) | copy-start | bytes 6148
  132.8 1.2 copy-start.18
where the time goes:
time: 135 us; the launch traced here: 134 us
  blocking collectives  54.9 us (41%)
  local copies, waits for them, and re-layouts  41.4 us (31%)
  matrix products  28 us (21%)
  other arithmetic  4.39 us (3%)
  starting transfers between devices  4.22 us (3%)
    all_gather x1, blocking collectives, on_device(): block_rows = lax.all_gather(hot_slab, 'blk', axis=0, tiled=True)  30.9 us
    all_to_all x1, blocking collectives, on_device(): lax.all_to_all(grad_slots, 'table', split_axis=1, concat_axis=1, tiled=True)  16.1 us
    eq x7, local copies, waits for them, and re-layouts, on_device(): lookup_selector = (lookup_slot_ids == columns).astype(jnp.bfloat16)  10.1 us
    unnamed x46, local copies, waits for them, and re-layouts  9.46 us
    dot_general x7, matrix products, on_device(): jnp.dot(lookup_selector, cold_tables[lookup_slot_index], preferred_elemen...  8.85 us
    all_to_all x1, blocking collectives, on_device(): lax.all_to_all(send_ids, 'table', split_axis=1, concat_axis=1, tiled=True)  7.91 us
    slice x8, local copies, waits for them, and re-layouts, on_device(): lookup_slot_ids = ids_block[:, :, lookup_slot_index].reshape(row_count, 1)  7.77 us
    dot_general x1, matrix products, on_device(): jnp.dot(grad_low, down_rank.T, preferred_element_type=jnp.float32)  6.33 us
  transfers between devices with their start and end apart: 1, of which 0 were waited for; matrix products, arithmetic and copies ran while one was open for 4% of the time, Pallas kernels for 0%

commit v1 on v0

v1 whole, which is shorter than its diff:
```python
import functools

import jax
import jax.numpy as jnp
from jax import lax
from jax.experimental import pallas as pl
from jax.experimental.pallas import tpu as pltpu
from jax.sharding import PartitionSpec as P


BF16 = jnp.bfloat16
F32 = jnp.float32
ROW_PARTS = (4, 3)
GRAD_PARTS = (4, 3)
NEAR = 2
VMEM = pl.BlockSpec(memory_space=pltpu.VMEM)
SMEM = pl.BlockSpec(memory_space=pltpu.SMEM)
HBM = pl.BlockSpec(memory_space=pltpu.HBM)
OVER_LANES = (((1,), (1,)), ((), ()))


def peer(index, mask, count):
    return index ^ mask if count & (count - 1) == 0 else (index + mask) % count


def cut(slots, parts):
    whole = sum(parts)
    ends, total = [0], 0
    for part in parts:
        total += part
        ends.append(-(-slots * total // whole))
    return [(a, b - a) for a, b in zip(ends, ends[1:])]


def load_kernel(owners, slots, slot_hbm, tables_hbm, ids_hbm, tables, ids, meta, slot_ref, sems):
    copies = [
        pltpu.make_async_copy(slot_hbm, slot_ref, sems.at[0]),
        pltpu.make_async_copy(ids_hbm, ids, sems.at[1]),
        pltpu.make_async_copy(tables_hbm, tables, sems.at[2]),
    ]
    for copy in copies:
        copy.start()
    copies[0].wait()
    me = lax.axis_index("table")
    lane = lax.broadcasted_iota(jnp.int32, (1, meta.shape[1]), 1)
    spot = lane
    for k in range(owners):
        inside = (lane >= k * slots) & (lane < (k + 1) * slots)
        spot = jnp.where(inside, lane + ((me ^ k) - k) * slots, spot)
    table_at = jnp.full_like(lane, -1)
    place_of = jnp.zeros_like(lane)
    for table in range(slot_ref.shape[0]):
        slot = slot_ref[table]
        hit = (spot == slot) & (lane < owners * slots)
        table_at = jnp.where(hit, table, table_at)
        owner = slot // slots
        place_of = jnp.where(lane == table, slot + ((owner ^ me) - owner) * slots, place_of)
    meta[0:1, :] = table_at
    meta[1:2, :] = place_of
    for copy in copies[1:]:
        copy.wait()


def find(columns, tables, masks, span, pad, outs, batch):
    first, count = span
    rows = tables.shape[1]
    position = lax.broadcasted_iota(jnp.int32, (batch, rows), 1)
    for step in range(count):
        picks = [
            jnp.where(
                columns[:, k * pad + first + step : k * pad + first + step + 1] == position, 1.0, 0.0
            ).astype(BF16)
            for k in masks
        ]
        found = jnp.dot(
            jnp.concatenate(picks, axis=0), tables[first + step], preferred_element_type=F32
        ).astype(BF16)
        for i, out in enumerate(outs):
            out[step * batch : (step + 1) * batch, :] = found[i * batch : (i + 1) * batch]


def far_first_kernel(span, owners, slots, pad, *refs):
    meta = refs[0]
    ids = refs[1 : 1 + owners]
    tables, shard, lines = refs[1 + owners : 4 + owners]
    outs = refs[4 + owners :]
    batch = ids[0].shape[1]
    height = shard.shape[0]
    for slot in range(slots):
        table = meta[0, slot]
        for k in range(owners):
            line = ids[k][pl.ds(jnp.maximum(table, 0), 1), :]
            lines[k * pad + slot : k * pad + slot + 1, :] = jnp.where(table >= 0, line, -1)
    find(lines[...].T, tables, range(NEAR, owners), span, pad, outs, batch)
    for out in outs:
        out[span[1] * batch : span[1] * batch + height, :] = shard[...]


def far_kernel(span, owners, pad, lines, tables, again, *outs):
    again[...] = lines[0:8, :]
    find(lines[...].T, tables, range(NEAR, owners), span, pad, outs, lines.shape[1])


def near_kernel(owners, slots, pad, *refs):
    (meta, lines, _, tables, shard) = refs[:5]
    down_hbm, up_hbm, cot_hbm, bias_hbm, dense_hbm, hot_hbm = refs[5:11]
    outs = refs[11 : 11 + NEAR]
    down, up, cot, bias, dense, hot = refs[11 + NEAR : 17 + NEAR]
    bias_in, sems = refs[17 + NEAR :]
    batch, width = dense.shape
    height = shard.shape[0]
    total = owners * slots
    copies = [
        pltpu.make_async_copy(bias_hbm, bias_in, sems.at[3]),
        pltpu.make_async_copy(dense_hbm, dense, sems.at[4]),
        pltpu.make_async_copy(hot_hbm, hot, sems.at[5]),
    ]
    for copy in copies:
        copy.start()
    block = lambda index: pl.ds(pl.multiple_of(index * width, width), width)
    spots = [0] + [jnp.maximum(meta[0, i], 0) + 1 for i in range(total)]
    for i, spot in enumerate(spots):
        here = pl.ds(i * width, width)
        pltpu.make_async_copy(down_hbm.at[block(spot), :], down.at[here, :], sems.at[0]).start()
        pltpu.make_async_copy(up_hbm.at[:, block(spot)], up.at[:, here], sems.at[1]).start()
        pltpu.make_async_copy(cot_hbm.at[:, block(spot)], cot.at[:, here], sems.at[2]).start()
    find(lines[...].T, tables, range(NEAR), (0, slots), pad, outs, batch)
    outs[1][slots * batch : slots * batch + height, :] = shard[...]
    for copy in copies:
        copy.wait()
    for i, spot in enumerate(spots):
        bias[i : i + 1, :] = bias_in[pl.ds(spot, 1), :]
    pltpu.make_async_copy(down, down, sems.at[0]).wait()
    pltpu.make_async_copy(up, up, sems.at[1]).wait()
    pltpu.make_async_copy(cot, cot, sems.at[2]).wait()


def shards_kernel(owners, *refs):
    shard, near = refs[:2]
    far, out = refs[2:owners], refs[owners]
    height, _ = shard.shape
    parts = [shard[...], near[near.shape[0] - height :, :]]
    parts += [ref[ref.shape[0] - height :, :] for ref in far]
    out[...] = jnp.concatenate(parts, axis=0)


def wide(ref, count, batch):
    return jnp.concatenate([ref[i * batch : (i + 1) * batch, :] for i in range(count)], axis=1)


def add_up(x, begin, down, up, cot, low, grad):
    span = slice(begin, begin + x.shape[1])
    mixed = (cot[:, span].astype(F32) * x.astype(F32)).astype(BF16)
    more = jnp.dot(x, down[span, :], preferred_element_type=F32)
    more_grad = lax.dot_general(mixed, up[:, span], OVER_LANES, preferred_element_type=F32)
    return (more, more_grad) if low is None else (low + more, grad + more_grad)


def grads_to(out, begin, count, low, grad, down, up, bias, cot):
    batch = cot.shape[0]
    width = bias.shape[1]
    span = slice(begin * width, (begin + count) * width)
    b = jnp.concatenate([bias[begin + i : begin + i + 1, :] for i in range(count)], axis=1)
    gate = jnp.dot(low, up[:, span], preferred_element_type=F32) + b
    back = lax.dot_general(grad, down[span, :], OVER_LANES, preferred_element_type=F32)
    result = (cot[:, span].astype(F32) * (gate + 1.0) + back).astype(BF16)
    for i in range(count):
        out[i * batch : (i + 1) * batch, :] = result[:, i * width : (i + 1) * width]


def first_kernel(span, owners, slots, *refs):
    near, far = refs[:NEAR], refs[NEAR:owners]
    down, up, cot, low_out, grad_out = refs[owners:]
    batch = cot.shape[0]
    width = near[0].shape[1]
    low = grad = None
    for k, ref in enumerate(near):
        x = wide(ref, slots, batch)
        low, grad = add_up(x, (1 + k * slots) * width, down, up, cot, low, grad)
    for k, ref in enumerate(far, NEAR):
        x = wide(ref, span[1], batch)
        low, grad = add_up(x, (1 + k * slots + span[0]) * width, down, up, cot, low, grad)
    low_out[...] = low
    grad_out[...] = grad


def second_kernel(span, grad_span, owners, slots, blocks, *refs):
    far = refs[: owners - NEAR]
    refs = refs[owners - NEAR :]
    held = -(-blocks // owners)
    shards = refs[:held]
    hot_ids, dense, low_in, grad_in, down, up, bias, cot = refs[held : 8 + held]
    front_out, low_out, grad_out = refs[8 + held : 11 + held]
    outs = refs[11 + held :]
    batch, width = dense.shape
    me = lax.axis_index("table")
    mine = lax.axis_index("blk")
    height = shards[0].shape[0] // owners
    row = lax.broadcasted_iota(jnp.int32, (height, batch), 0)
    pooled = None
    for part in range(held):
        counts = []
        for k in range(owners):
            mask = part * owners + (me ^ k)
            base = jnp.where(mask < blocks, peer(mine, mask, blocks) * height, -height)
            total = jnp.zeros((height, batch), F32)
            for i in range(hot_ids.shape[0]):
                total += jnp.where(hot_ids[i : i + 1, :] - base == row, 1.0, 0.0)
            counts.append(total)
        counts = jnp.concatenate(counts, axis=0).astype(BF16)
        more = lax.dot_general(
            counts, shards[part][...], (((0,), (0,)), ((), ())), preferred_element_type=F32
        )
        pooled = more if pooled is None else pooled + more
    front = (dense[...].astype(F32) + pooled).astype(BF16)
    front_out[...] = front
    low, grad = add_up(front, 0, down, up, cot, low_in[...], grad_in[...])
    for k, ref in enumerate(far, NEAR):
        x = wide(ref, span[1], batch)
        low, grad = add_up(x, (1 + k * slots + span[0]) * width, down, up, cot, low, grad)
    low = low.astype(BF16)
    grad = grad.astype(BF16)
    low_out[...] = low
    grad_out[...] = grad
    for k, out in enumerate(outs, NEAR):
        begin = 1 + k * slots + grad_span[0]
        grads_to(out, begin, grad_span[1], low, grad, down, up, bias, cot)


def grads_kernel(span, masks, slots, low, grad, down, up, bias, cot, _, *outs):
    for k, out in zip(masks, outs):
        begin = 1 + k * slots + span[0]
        grads_to(out, begin, span[1], low[...], grad[...], down, up, bias, cot)


def crossed_kernel(spans, owners, slots, *refs):
    meta = refs[0]
    chunks = len(spans)
    near = refs[1 : 1 + NEAR]
    count = owners - NEAR
    far = [refs[1 + NEAR + c * count : 1 + NEAR + (c + 1) * count] for c in range(chunks)]
    front, low, up, bias, _, out, held = refs[1 + NEAR + chunks * count :]
    batch, width = front.shape

    def gated(xs, begin):
        span = slice(begin * width, (begin + len(xs)) * width)
        gate = jnp.dot(low[...], up[:, span], preferred_element_type=F32)
        for i, x in enumerate(xs):
            part = gate[:, i * width : (i + 1) * width] + bias[begin + i : begin + i + 1, :]
            x = x.astype(F32)
            xs[i] = (x * part + x).astype(BF16)
        return xs

    out[:, :width] = gated([front[...]], 0)[0]
    runs = [(ref, k, 0, slots) for k, ref in enumerate(near)]
    runs += [(ref, k, *spans[c]) for c in range(chunks) for k, ref in enumerate(far[c], NEAR)]
    for ref, k, first, steps in runs:
        xs = [ref[i * batch : (i + 1) * batch, :] for i in range(steps)]
        for i, value in enumerate(gated(xs, 1 + k * slots + first)):
            held[k * slots + first + i] = value
    for table in range(out.shape[1] // width - 1):
        out[:, (table + 1) * width : (table + 2) * width] = held[meta[1, table]]


def summed(lines, masks, slot, grads, pad, rows):
    batch = lines.shape[1]
    position = lax.broadcasted_iota(jnp.int32, (rows, batch), 0)
    picks = [
        jnp.where(position == lines[k * pad + slot : k * pad + slot + 1, :], 1.0, 0.0).astype(BF16)
        for k in masks
    ]
    return jnp.dot(
        jnp.concatenate(picks, axis=1), jnp.concatenate(grads, axis=0), preferred_element_type=F32
    )


def scatter_kernel(span, later, owners, pad, *refs):
    lines = refs[0]
    near = refs[1 : 1 + NEAR]
    far = refs[1 + NEAR : 1 + owners]
    out, rest, held, sems = refs[1 + owners :]
    rows = out.shape[2]
    batch = lines.shape[1]
    first, count = span
    copies = []
    for step in range(count):
        slot = first + step
        grads = [ref[slot * batch : (slot + 1) * batch, :] for ref in near]
        grads += [ref[step * batch : (step + 1) * batch, :] for ref in far]
        held[step] = summed(lines, range(owners), slot, grads, pad, rows)
        copies.append(pltpu.make_async_copy(held.at[step], out.at[0, slot], sems.at[step]))
        copies[-1].start()
    for step in range(later[1]):
        slot = later[0] + step
        grads = [ref[slot * batch : (slot + 1) * batch, :] for ref in near]
        rest[step] = summed(lines, range(NEAR), slot, grads, pad, rows)
    for copy in copies:
        copy.wait()


def last_kernel(span, owners, pad, *refs):
    lines, rest = refs[:2]
    far = refs[2 : 2 + owners - NEAR]
    out, held, sems = refs[3 + owners - NEAR :]
    rows = out.shape[2]
    batch = lines.shape[1]
    copies = []
    for step in range(span[1]):
        slot = span[0] + step
        grads = [ref[step * batch : (step + 1) * batch, :] for ref in far]
        held[step] = rest[step] + summed(lines, range(NEAR, owners), slot, grads, pad, rows)
        copies.append(pltpu.make_async_copy(held.at[step], out.at[0, slot], sems.at[step]))
        copies[-1].start()
    for copy in copies:
        copy.wait()


def on_device(
    hot_slab,
    hot_ids,
    dense,
    cold_ids,
    table_slot,
    cold_tables,
    down_rank,
    up_rank,
    cross_bias,
    cotangent,
):
    batch, width = dense.shape
    owners = lax.axis_size("table")
    blocks = lax.axis_size("blk")
    slots, table_rows = cold_tables.shape[:2]
    rank = down_rank.shape[1]
    height = hot_slab.shape[0]
    total = owners * slots
    pad = -(-slots // 8) * 8
    row_spans, grad_spans = cut(slots, ROW_PARTS), cut(slots, GRAD_PARTS)
    assert owners & (owners - 1) == 0 and owners > NEAR
    far_count = owners - NEAR

    def call(kernel, shapes, operands, specs=None, *, mib, scratch=(), flops=4e9):
        return pl.pallas_call(
            kernel,
            out_shape=shapes,
            in_specs=specs or [VMEM] * len(operands),
            out_specs=[VMEM] * len(shapes),
            scratch_shapes=list(scratch),
            compiler_params=pltpu.CompilerParams(vmem_limit_bytes=mib << 20),
            cost_estimate=pl.CostEstimate(flops=int(flops), transcendentals=0, bytes_accessed=1 << 20),
        )(*operands)

    def swap(array, k):
        return lax.ppermute(array, "table", [(i, i ^ k) for i in range(owners)])

    def far_swap(arrays):
        return [swap(array, k) for k, array in enumerate(arrays, NEAR)]

    def in_hbm(array):
        return pltpu.with_memory_space_constraint(array, pltpu.HBM)

    def shape(*dims, dtype=BF16):
        return jax.ShapeDtypeStruct(dims, dtype)

    ids = cold_ids.T
    far_ids = far_swap([ids] * far_count)
    near_ids = swap(ids, 1)
    shard = lax.ppermute(
        hot_slab,
        ("blk", "table"),
        [
            (peer(b, t, blocks) * owners + t, b * owners + t)
            for b in range(blocks)
            for t in range(owners)
        ],
    )
    tables, ids, meta = call(
        functools.partial(load_kernel, owners, slots),
        [shape(*cold_tables.shape), shape(*ids.shape, dtype=jnp.int32), shape(8, 128, dtype=jnp.int32)],
        [in_hbm(table_slot), in_hbm(cold_tables), in_hbm(ids)],
        [HBM] * 3,
        scratch=[pltpu.SMEM(table_slot.shape, jnp.int32), pltpu.SemaphoreType.DMA((3,))],
        mib=1,
    )
    lines, *sends = call(
        functools.partial(far_first_kernel, row_spans[0], owners, slots, pad),
        [shape(owners * pad, batch, dtype=jnp.int32)]
        + [shape(row_spans[0][1] * batch + height, width)] * far_count,
        [meta, ids, near_ids, *far_ids, tables, shard],
        [SMEM] + [VMEM] * (owners + 2),
        mib=4,
    )
    far = [far_swap(sends)]
    again, *sends = call(
        functools.partial(far_kernel, row_spans[1], owners, pad),
        [shape(8, batch, dtype=jnp.int32)] + [shape(row_spans[1][1] * batch, width)] * far_count,
        [lines, tables],
        mib=4,
    )
    far.append(far_swap(sends))
    features = (total + 1) * width
    *near, down, up, cot, bias, dense, hot_rows = call(
        functools.partial(near_kernel, owners, slots, pad),
        [shape(slots * batch, width), shape(slots * batch + height, width)]
        + [
            shape(features, rank),
            shape(rank, features),
            shape(batch, features),
            shape(-(-(total + 1) // 8) * 8, width, dtype=F32),
            shape(batch, width),
            shape(hot_ids.shape[1], batch, dtype=jnp.int32),
        ],
        [meta, lines, again, tables, shard]
        + [
            in_hbm(x)
            for x in (
                down_rank,
                up_rank,
                cotangent,
                cross_bias.reshape(-1, width),
                dense,
                hot_ids.T,
            )
        ],
        [SMEM] + [VMEM] * 4 + [HBM] * 6,
        scratch=[
            pltpu.VMEM((cross_bias.shape[0] // width, width), F32),
            pltpu.SemaphoreType.DMA((6,)),
        ],
        mib=6,
    )
    near[1] = swap(near[1], 1)

    (group,) = call(
        functools.partial(shards_kernel, owners),
        [shape(owners * height, width)],
        [shard, near[1], *far[0]],
        mib=1,
    )
    shards = [group]
    for mask in range(owners, blocks, owners):
        pairs = [(peer(b, mask, blocks), b) for b in range(blocks)]
        shards.append(lax.ppermute(group, "blk", pairs))

    low, grad = call(
        functools.partial(first_kernel, row_spans[0], owners, slots),
        [shape(batch, rank, dtype=F32)] * 2,
        [*near, *far[0], down, up, cot],
        mib=6,
    )
    front, low, grad, *sends = call(
        functools.partial(second_kernel, row_spans[1], grad_spans[0], owners, slots, blocks),
        [shape(batch, width), shape(batch, rank), shape(batch, rank)]
        + [shape(grad_spans[0][1] * batch, width)] * far_count,
        [*far[1], *shards, hot_rows, dense, low, grad, down, up, bias, cot],
        mib=6,
    )
    far_grads = [far_swap(sends)]
    sends = call(
        functools.partial(grads_kernel, grad_spans[1], range(NEAR, owners), slots),
        [shape(grad_spans[1][1] * batch, width)] * far_count,
        [low, grad, down, up, bias, cot, front],
        mib=6,
    )
    far_grads.append(far_swap(sends))
    near_grads = call(
        functools.partial(grads_kernel, (0, slots), range(NEAR), slots),
        [shape(slots * batch, width)] * NEAR,
        [low, grad, down, up, bias, cot, sends[0]],
        mib=6,
    )
    last_near = near_grads[0]
    near_grads = [near_grads[0], swap(near_grads[1], 1)]
    (crossed,) = call(
        functools.partial(crossed_kernel, row_spans, owners, slots),
        [shape(*cotangent.shape)],
        [meta, *near, *far[0], *far[1], front, low, up, bias, last_near],
        [SMEM] + [VMEM] * (NEAR + 2 * far_count + 5),
        scratch=[pltpu.VMEM((total, batch, width), BF16)],
        mib=6,
    )

    (first, count), later = grad_spans
    grads_shape = shape(1, slots, table_rows, width, dtype=F32)
    table_grad, rest = pl.pallas_call(
        functools.partial(scatter_kernel, grad_spans[0], later, owners, pad),
        out_shape=[grads_shape, shape(later[1], table_rows, width, dtype=F32)],
        in_specs=[VMEM] * (1 + owners),
        out_specs=[pl.BlockSpec(memory_space=pl.ANY), VMEM],
        scratch_shapes=[
            pltpu.VMEM((count, table_rows, width), F32),
            pltpu.SemaphoreType.DMA((count,)),
        ],
        compiler_params=pltpu.CompilerParams(vmem_limit_bytes=6 << 20),
        name="scatter",
    )(lines, *near_grads, *far_grads[0])
    table_grad = pl.pallas_call(
        functools.partial(last_kernel, later, owners, pad),
        out_shape=grads_shape,
        in_specs=[VMEM] * (2 + far_count) + [pl.BlockSpec(memory_space=pl.ANY)],
        out_specs=pl.BlockSpec(memory_space=pl.ANY),
        scratch_shapes=[
            pltpu.VMEM((later[1], table_rows, width), F32),
            pltpu.SemaphoreType.DMA((later[1],)),
        ],
        input_output_aliases={2 + far_count: 0},
        compiler_params=pltpu.CompilerParams(vmem_limit_bytes=6 << 20),
        name="last",
    )(lines, rest, *far_grads[1], table_grad)
    return crossed, table_grad


def solution(mesh):
    placed = (
        P("blk", None),
        P(("blk", "table"), None),
        P(("blk", "table"), None),
        P(("blk", "table"), None),
        P(),
        P("table", None, None),
        P(),
        P(),
        P(),
        P(("blk", "table"), None),
    )

    return jax.shard_map(
        on_device,
        mesh=mesh,
        in_specs=placed,
        out_specs=(P(("blk", "table"), None), P("blk", "table", None, None)),
        check_vma=False,
    )
```

time: 135 us -> 46 us (0.34)
  blocking collectives: 54.9 us -> 0 us
  local copies, waits for them, and re-layouts: 41.4 us -> 0 us
  matrix products: 28 us -> 0 us
  Pallas kernels: 0 us -> 17.3 us
  starting transfers between devices: 4.22 us -> 17.1 us
  waiting for transfers between devices: 0.01 us -> 10.4 us
  other arithmetic: 4.39 us -> 0 us
    all_gather x1 -> x0, blocking collectives: 30.9 us -> none  [on_device(): block_rows = lax.all_gather(hot_slab, 'blk', axis=0, tiled=True)]
    dot_general x19 -> x0, matrix products: 28 us -> none  [the longest x7 8.85 us: on_device(): jnp.dot(lookup_selector, cold_tables[lookup_slot_index], preferred_elemen...]
    all_to_all x2 -> x0, blocking collectives: 24 us -> none  [the longest x1 16.1 us: on_device(): lax.all_to_all(grad_slots, 'table', split_axis=1, concat_axis=1, tiled=True)]
    pallas_call x0 -> x12, Pallas kernels: none -> 17.3 us  [the longest x10 14.6 us: call(): pl.pallas_call(kernel, out_shape=shapes, in_specs=specs or [VMEM] * len(o...]
    ppermute x0 -> x15, starting transfers between devices: none -> 17.1 us  [the longest x13 13.1 us: swap(): return lax.ppermute(array, 'table', [(i, i ^ k) for i in range(owners)])]
    slice x17 -> x0, local copies, waits for them, and re-layouts: 10.8 us -> none  [the longest x8 7.77 us: on_device(): lookup_slot_ids = ids_block[:, :, lookup_slot_index].reshape(row_count, 1)]
    ppermute x0 -> x15, waiting for transfers between devices: none -> 10.4 us  [the longest x13 9.92 us: swap(): return lax.ppermute(array, 'table', [(i, i ^ k) for i in range(owners)])]
    eq x8 -> x0, local copies, waits for them, and re-layouts: 10.1 us -> none  [the longest x7 10.1 us: on_device(): lookup_selector = (lookup_slot_ids == columns).astype(jnp.bfloat16)]
  transfers between devices with their start and end apart: 1 -> 15, of which waited for: 0 -> 6; matrix products, arithmetic and copies ran while one was open for 4% -> 0% of each run, Pallas kernels for 0% -> 15%
where the time goes in v1:
time: 46 us; the launch traced here: 45.5 us
  Pallas kernels  17.3 us (38%)
  starting transfers between devices  17.1 us (37%)
  waiting for transfers between devices  10.4 us (23%)
  between operations  0.75 us (2%)
    pallas_call x10, Pallas kernels, call(): pl.pallas_call(kernel, out_shape=shapes, in_specs=specs or [VMEM] * len(o...  14.6 us
    ppermute x13, starting transfers between devices, swap(): return lax.ppermute(array, 'table', [(i, i ^ k) for i in range(owners)])  13.1 us
    ppermute x13, waiting for transfers between devices, swap(): return lax.ppermute(array, 'table', [(i, i ^ k) for i in range(owners)])  9.92 us
    ppermute x1, starting transfers between devices, on_device(): shards.append(lax.ppermute(group, 'blk', pairs))  2.61 us
    pallas_call x1, Pallas kernels, on_device(): pl.pallas_call(functools.partial(scatter_kernel, grad_spans[0], later, ow...  1.53 us
    ppermute x1, starting transfers between devices, on_device(): lax.ppermute(hot_slab, ('blk', 'table'), [(peer(b, t, blocks) * owners +...  1.33 us
    pallas_call x1, Pallas kernels, on_device(): pl.pallas_call(functools.partial(last_kernel, later, owners, pad), out_sh...  1.2 us
  transfers between devices with their start and end apart: 15, of which 6 were waited for; matrix products, arithmetic and copies ran while one was open for 0% of the time, Pallas kernels for 15%

profile of v1, /device:TPU:0, one launch (start us, length us, event | category | flops | bytes accessed | tf_op | source)
XLA Modules:
  0.0 45.5 jit_solution(3751158010616166677)
XLA Ops:
  0.6 2.5 %collective-permute-start.2 = (s32[26,128]{1,0:T(8,128)}, s32[26,128]{1,0:T(8,128)S(1)}, u32[]{:S(2)}, u32[]{:S(2)}) collective-permute-start(s32[26,128]{1,0:T(8,128)} %bitcast.3), channel_id=1, source_target_pairs={{0,3},{1,2},{2,1},{3,0},{4,7},{5,6},{6,5},{7,4},{8,11},{9,10},{10,... | collective-permute-start | bytes 39944 | tf_op jit(solution)/shard_map/ppermute | solution.py:354
  3.1 0.6 %collective-permute-start.1 = (s32[26,128]{1,0:T(8,128)}, s32[26,128]{1,0:T(8,128)S(1)}, u32[]{:S(2)}, u32[]{:S(2)}) collective-permute-start(s32[26,128]{1,0:T(8,128)} %bitcast.4), channel_id=1, source_target_pairs={{0,2},{1,3},{2,0},{3,1},{4,6},{5,7},{6,4},{7,5},{8,10},{9,11},{10,... | collective-permute-start | bytes 39944 | tf_op jit(solution)/shard_map/ppermute | solution.py:354
  3.8 0.0 collective-permute-start
  3.8 1.3 %collective-permute-start.3 = (bf16[16,128]{1,0:T(8,128)(2,1)}, bf16[16,128]{1,0:T(8,128)(2,1)S(1)}, u32[]{:S(2)}, u32[]{:S(2)}) collective-permute-start(bf16[16,128]{1,0:T(8,128)(2,1)} %param.10), channel_id=1, source_target_pairs={{0,0},{5,1},{10,2},{15,3},{4,4},{1,5},{14,6},{11,7},{8,8},{13,9},{... | collective-permute-start | bytes 12296 | tf_op jit(solution)/shard_map/ppermute | solution.py:368
  5.1 1.2 %shard_map.113 = (bf16[7,512,128]{2,1,0:T(8,128)(2,1)S(1)}, s32[26,128]{1,0:T(8,128)S(1)}, s32[8,128]{1,0:T(8,128)S(1)}) custom-call(s32[26]{0:T(128)} %slot_hbm.1, bf16[7,512,128]{2,1,0:T(8,128)(2,1)} %tables_hbm.1, s32[26,128]{1,0:T(8,128)} %bitcast.6), custom_call_target="tpu_custom_call" | custom-call | flops 4000000000 | bytes 1048576 | tf_op jit(solution)/shard_map/pallas_call | solution.py:343
  6.4 0.0 collective-permute-done.3.refs_6_.refs_4_.refs_0_
  6.4 0.0 collective-permute-done.2.refs_4_
  6.4 0.7 %collective-permute-done.1.refs_3_ = s32[26,128]{1,0:T(8,128)S(1)} collective-permute-done((s32[26,128]{1,0:T(8,128)}, s32[26,128]{1,0:T(8,128)S(1)}, u32[]{:S(2)}, u32[]{:S(2)}) %collective-permute-start.1) | collective-permute-done | bytes 13344 | tf_op jit(solution)/shard_map/ppermute | solution.py:354
  7.1 0.0 collective-permute-done.refs_2_
  7.1 1.2 %shard_map.114 = (s32[32,128]{1,0:T(8,128)S(1)}, bf16[528,128]{1,0:T(8,128)(2,1)S(1)}, bf16[528,128]{1,0:T(8,128)(2,1)S(1)}) custom-call(s32[8,128]{1,0:T(8,128)S(1)} %get-tuple-element.32.refs_0_, s32[26,128]{1,0:T(8,128)S(1)} %get-tuple-element.33.refs_1_, s32[26,128]{1,0:T(8,128)S(1)} %collective-permute-done.refs_2_, ...), custom_call_target="tpu_custom_call" | custom-call | flops 4000000000 | bytes 1048576 | tf_op jit(solution)/shard_map/pallas_call | solution.py:343
  8.3 0.5 %shard_map.115 = (s32[8,128]{1,0:T(8,128)S(1)}, bf16[384,128]{1,0:T(8,128)(2,1)S(1)}, bf16[384,128]{1,0:T(8,128)(2,1)S(1)}) custom-call(s32[32,128]{1,0:T(8,128)S(1)} %get-tuple-element.35.lines.refs_1_.refs_0_, bf16[7,512,128]{2,1,0:T(8,128)(2,1)S(1)} %get-tuple-element.34.refs_5_.tables.refs_3_), custom_call_target="tpu_custom_call" | custom-call | flops 4000000000 | bytes 1048576 | tf_op jit(solution)/shard_map/pallas_call | solution.py:343
  8.8 4.7 %shard_map.116 = (bf16[896,128]{1,0:T(8,128)(2,1)S(1)}, bf16[912,128]{1,0:T(8,128)(2,1)S(1)}, bf16[3712,512]{1,0:T(8,128)(2,1)S(1)}, bf16[512,3712]{1,0:T(8,128)...) custom-call(s32[8,128]{1,0:T(8,128)S(1)} %get-tuple-element.32.refs_, ...), custom_call_target="tpu_custom_call" | custom-call | flops 4000000000 | bytes 1048576 | tf_op jit(solution)/shard_map/pallas_call | solution.py:343
  13.5 1.8 %collective-permute-start.4 = (bf16[912,128]{1,0:T(8,128)(2,1)S(1)}, bf16[912,128]{1,0:T(8,128)(2,1)S(1)}, u32[]{:S(2)}, u32[]{:S(2)}) collective-permute-start(bf16[912,128]{1,0:T(8,128)(2,1)S(1)} %get-tuple-element.38), channel_id=1, source_target_pairs={{0,1},{1,0},{2,3},{3,2},{4,5},{5,4},{6,7},{7,6},{8,9},{9,8},{10,11... | collective-permute-start | bytes 700424 | tf_op jit(solution)/shard_map/ppermute | solution.py:354
  15.3 2.5 %collective-permute-start.5 = (bf16[528,128]{1,0:T(8,128)(2,1)S(1)}, bf16[528,128]{1,0:T(8,128)(2,1)S(1)}, u32[]{:S(2)}, u32[]{:S(2)}) collective-permute-start(bf16[528,128]{1,0:T(8,128)(2,1)S(1)} %get-tuple-element.39), channel_id=1, source_target_pairs={{0,2},{1,3},{2,0},{3,1},{4,6},{5,7},{6,4},{7,5},{8,10},{9,11},{10,... | collective-permute-start | bytes 405512 | tf_op jit(solution)/shard_map/ppermute | solution.py:354
  17.8 0.0 collective-permute-start.6
  17.9 1.7 %collective-permute-start.7 = (bf16[384,128]{1,0:T(8,128)(2,1)S(1)}, bf16[384,128]{1,0:T(8,128)(2,1)S(1)}, u32[]{:S(2)}, u32[]{:S(2)}) collective-permute-start(bf16[384,128]{1,0:T(8,128)(2,1)S(1)} %get-tuple-element.41), channel_id=1, source_target_pairs={{0,2},{1,3},{2,0},{3,1},{4,6},{5,7},{6,4},{7,5},{8,10},{9,11},{10,... | collective-permute-start | bytes 294920 | tf_op jit(solution)/shard_map/ppermute | solution.py:354
  19.6 0.0 collective-permute-start.8
  19.6 2.6 %collective-permute-done.5.refs_2_.refs_3_ = bf16[528,128]{1,0:T(8,128)(2,1)S(1)} collective-permute-done((bf16[528,128]{1,0:T(8,128)(2,1)S(1)}, bf16[528,128]{1,0:T(8,128)(2,1)S(1)}, u32[]{:S(2)}, u32[]{:S(2)}) %collective-permute-start.5) | collective-permute-done | bytes 135200 | tf_op jit(solution)/shard_map/ppermute | solution.py:354
  22.3 2.4 %collective-permute-done.6.refs_3_.refs_4_ = bf16[528,128]{1,0:T(8,128)(2,1)S(1)} collective-permute-done((bf16[528,128]{1,0:T(8,128)(2,1)S(1)}, bf16[528,128]{1,0:T(8,128)(2,1)S(1)}, u32[]{:S(2)}, u32[]{:S(2)}) %collective-permute-start.6) | collective-permute-done | bytes 135200 | tf_op jit(solution)/shard_map/ppermute | solution.py:354
  24.7 0.0 collective-permute-done.4.refs_1_.refs_2_
  24.7 2.6 %collective-permute-start.9 = (bf16[64,128]{1,0:T(8,128)(2,1)S(1)}, bf16[64,128]{1,0:T(8,128)(2,1)S(1)}, u32[]{:S(2)}, u32[]{:S(2)}) collective-permute-start(bf16[64,128]{1,0:T(8,128)(2,1)S(1)} %shard_map.117.refs_2_), channel_id=1, source_target_pairs={{16,0},{20,4},{24,8},{28,12},{0,16},{4,20},{8,24},{12,28},{17,1},{... | collective-permute-start | bytes 49160 | tf_op jit(solution)/shard_map/ppermute | solution.py:443
  27.3 1.5 %shard_map.118 = (f32[128,512]{1,0:T(8,128)S(1)}, f32[128,512]{1,0:T(8,128)S(1)}) custom-call(bf16[896,128]{1,0:T(8,128)(2,1)S(1)} %get-tuple-element.37.refs_0_.refs_1_, bf16[912,128]{1,0:T(8,128)(2,1)S(1)} %collective-permute-done.4.refs_1_.refs_2_, bf16[528,128]{1,0:T(8,128)(2,1)S(1)} %collective-permute-done.5.refs_2_.refs_3_, ...), custom_call_target="tpu_custom_call" | custom-call | flops 4000000000 | bytes 1048576 | tf_op jit(solution)/shard_map/pallas_call | solution.py:343
  28.9 0.0 collective-permute-done.7.refs_0_.refs_5_
  28.9 0.0 collective-permute-done.8.refs_1_.refs_6_
  28.9 0.5 %collective-permute-done.9.refs_3_ = bf16[64,128]{1,0:T(8,128)(2,1)S(1)} collective-permute-done((bf16[64,128]{1,0:T(8,128)(2,1)S(1)}, bf16[64,128]{1,0:T(8,128)(2,1)S(1)}, u32[]{:S(2)}, u32[]{:S(2)}) %collective-permute-start.9) | collective-permute-done | bytes 16416 | tf_op jit(solution)/shard_map/ppermute | solution.py:443
  29.4 1.4 %shard_map.119 = (bf16[128,128]{1,0:T(8,128)(2,1)S(1)}, bf16[128,512]{1,0:T(8,128)(2,1)S(1)}, bf16[128,512]{1,0:T(8,128)(2,1)S(1)}, bf16[512,128]{1,0:T(8,128)(2,1)S(1)}, bf16[512,128]{1,0:T(8,128)(2,1)S(1)}) custom-call(bf16[384,128]{1,0:T(8,128)(2,1)S(1)} %collective-permute-done.7.refs_0_.refs_5_, ...), custom_call_target="tpu_custom_call" | custom-call | flops 4000000000 | bytes 1048576 | tf_op jit(solution)/shard_map/pallas_call | solution.py:343
  30.8 0.5 %shard_map.120 = (bf16[384,128]{1,0:T(8,128)(2,1)S(1)}, bf16[384,128]{1,0:T(8,128)(2,1)S(1)}) custom-call(bf16[128,512]{1,0:T(8,128)(2,1)S(1)} %get-tuple-element.52.low.refs_8_, bf16[128,512]{1,0:T(8,128)(2,1)S(1)} %get-tuple-element.53.grad, bf16[3712,512]{1,0:T(8,128)(2,1)S(1)} %get-tuple-element.45.refs_4_.refs_8_.down, ...), custom_call_target="tpu_custom_call" | custom-call | flops 4000000000 | bytes 1048576 | tf_op jit(solution)/shard_map/pallas_call | solution.py:343
  31.3 1.1 %shard_map.121 = (bf16[896,128]{1,0:T(8,128)(2,1)S(1)}, bf16[896,128]{1,0:T(8,128)(2,1)S(1)}) custom-call(bf16[128,512]{1,0:T(8,128)(2,1)S(1)} %get-tuple-element.52.low.refs_8_, bf16[128,512]{1,0:T(8,128)(2,1)S(1)} %get-tuple-element.53.grad, bf16[3712,512]{1,0:T(8,128)(2,1)S(1)} %get-tuple-element.45.refs_4_.refs_8_.down, ...), custom_call_target="tpu_custom_call" | custom-call | flops 4000000000 | bytes 1048576 | tf_op jit(solution)/shard_map/pallas_call | solution.py:343
  32.4 1.6 %collective-permute-start.13 = (bf16[384,128]{1,0:T(8,128)(2,1)S(1)}, bf16[384,128]{1,0:T(8,128)(2,1)S(1)}, u32[]{:S(2)}, u32[]{:S(2)}) collective-permute-start(bf16[384,128]{1,0:T(8,128)(2,1)S(1)} %get-tuple-element.54._), channel_id=1, source_target_pairs={{0,2},{1,3},{2,0},{3,1},{4,6},{5,7},{6,4},{7,5},{8,10},{9,11},{10,... | collective-permute-start | bytes 294920 | tf_op jit(solution)/shard_map/ppermute | solution.py:354
  34.0 0.5 %collective-permute-start.11 = (bf16[512,128]{1,0:T(8,128)(2,1)S(1)}, bf16[512,128]{1,0:T(8,128)(2,1)S(1)}, u32[]{:S(2)}, u32[]{:S(2)}) collective-permute-start(bf16[512,128]{1,0:T(8,128)(2,1)S(1)} %get-tuple-element.57), channel_id=1, source_target_pairs={{0,2},{1,3},{2,0},{3,1},{4,6},{5,7},{6,4},{7,5},{8,10},{9,11},{10,... | collective-permute-start | bytes 393224 | tf_op jit(solution)/shard_map/ppermute | solution.py:354
  34.5 0.6 %collective-permute-start.12 = (bf16[512,128]{1,0:T(8,128)(2,1)S(1)}, bf16[512,128]{1,0:T(8,128)(2,1)S(1)}, u32[]{:S(2)}, u32[]{:S(2)}) collective-permute-start(bf16[512,128]{1,0:T(8,128)(2,1)S(1)} %get-tuple-element.58), channel_id=1, source_target_pairs={{0,3},{1,2},{2,1},{3,0},{4,7},{5,6},{6,5},{7,4},{8,11},{9,10},{10,... | collective-permute-start | bytes 393224 | tf_op jit(solution)/shard_map/ppermute | solution.py:354
  35.1 1.1 %collective-permute-start.14 = (bf16[384,128]{1,0:T(8,128)(2,1)S(1)}, bf16[384,128]{1,0:T(8,128)(2,1)S(1)}, u32[]{:S(2)}, u32[]{:S(2)}) collective-permute-start(bf16[384,128]{1,0:T(8,128)(2,1)S(1)} %get-tuple-element.60), channel_id=1, source_target_pairs={{0,3},{1,2},{2,1},{3,0},{4,7},{5,6},{6,5},{7,4},{8,11},{9,10},{10,... | collective-permute-start | bytes 294920 | tf_op jit(solution)/shard_map/ppermute | solution.py:354
  36.2 0.0 collective-permute-start.10
  36.2 2.4 %shard_map.122 = bf16[128,3456]{1,0:T(8,128)(2,1)} custom-call(s32[8,128]{1,0:T(8,128)S(1)} %get-tuple-element.32.refs_0_, bf16[896,128]{1,0:T(8,128)(2,1)S(1)} %get-tuple-element.37.refs_0_.refs_1_, bf16[912,128]{1,0:T(8,128)(2,1)S(1)} %collective-permute-done.4.refs_1_.refs_2_, bf16[528,128]{1,0:T(8,128)(2,1)S(1)} %collective-permute-done.5.refs_2_.refs_3_, ...), custom_call_target="tpu_custom_call" | custom-call | flops 4000000000 | bytes 1048576 | tf_op jit(solution)/shard_map/pallas_call | solution.py:343
  38.7 1.9 %collective-permute-done.11.refs_3_ = bf16[512,128]{1,0:T(8,128)(2,1)S(1)} collective-permute-done((bf16[512,128]{1,0:T(8,128)(2,1)S(1)}, bf16[512,128]{1,0:T(8,128)(2,1)S(1)}, u32[]{:S(2)}, u32[]{:S(2)}) %collective-permute-start.11) | collective-permute-done | bytes 131104 | tf_op jit(solution)/shard_map/ppermute | solution.py:354
  40.6 2.2 %collective-permute-done.12.refs_4_ = bf16[512,128]{1,0:T(8,128)(2,1)S(1)} collective-permute-done((bf16[512,128]{1,0:T(8,128)(2,1)S(1)}, bf16[512,128]{1,0:T(8,128)(2,1)S(1)}, u32[]{:S(2)}, u32[]{:S(2)}) %collective-permute-start.12) | collective-permute-done | bytes 131104 | tf_op jit(solution)/shard_map/ppermute | solution.py:354
  42.8 0.0 collective-permute-done.10.refs_2_
  42.8 1.5 %scatter.1 = (f32[1,7,512,128]{3,2,1,0:T(8,128)}, f32[3,512,128]{2,1,0:T(8,128)S(1)}) custom-call(s32[32,128]{1,0:T(8,128)S(1)} %get-tuple-element.35.lines.refs_1_.refs_0_, bf16[896,128]{1,0:T(8,128)(2,1)S(1)} %get-tuple-element.55.refs_11_.refs_1_, bf16[896,128]{1,0:T(8,128)(2,1)S(1)} %collective-permute-done.10.refs_2_, ...), custom_call_target="tpu_custom_call" | custom-call | tf_op jit(solution)/shard_map/scatter/pallas_call | solution.py:485
  44.3 0.0 collective-permute-done.14.refs_3_
  44.3 0.0 collective-permute-done.13.refs_2_
  44.4 1.2 %last.1 = f32[1,7,512,128]{3,2,1,0:T(8,128)} custom-call(s32[32,128]{1,0:T(8,128)S(1)} %get-tuple-element.35.lines.refs_1_.refs_0_, f32[3,512,128]{2,1,0:T(8,128)S(1)} %get-tuple-element.59.refs_1_, bf16[384,128]{1,0:T(8,128)(2,1)S(1)} %collective-permute-done.13.refs_2_, ...), custom_call_target="tpu_custom_call", output_to_operand_aliasing={{}: (4, {})} | custom-call | tf_op jit(solution)/shard_map/last/pallas_call | solution.py:497
  (1 shorter events, 0.0 us)
Async XLA Ops:
  0.6 5.8 %collective-permute-start.2 = (s32[26,128]{1,0:T(8,128)}, s32[26,128]{1,0:T(8,128)S(1)}, u32[]{:S(2)}, u32[]{:S(2)}) collective-permute-start(s32[26,128]{1,0:T(8,128)} %bitcast.3), channel_id=1, source_target_pairs={{0,3},{1,2},{2,1},{3,0},{4,7},{5,6},{6,5},{7,4},{8,11},{9,10},{10,... | collective-permute-start | bytes 39944 | tf_op jit(solution)/shard_map/ppermute | solution.py:354
  3.1 3.9 %collective-permute-start.1 = (s32[26,128]{1,0:T(8,128)}, s32[26,128]{1,0:T(8,128)S(1)}, u32[]{:S(2)}, u32[]{:S(2)}) collective-permute-start(s32[26,128]{1,0:T(8,128)} %bitcast.4), channel_id=1, source_target_pairs={{0,2},{1,3},{2,0},{3,1},{4,6},{5,7},{6,4},{7,5},{8,10},{9,11},{10,... | collective-permute-start | bytes 39944 | tf_op jit(solution)/shard_map/ppermute | solution.py:354
  3.8 3.3 %collective-permute-start = (s32[26,128]{1,0:T(8,128)}, s32[26,128]{1,0:T(8,128)S(1)}, u32[]{:S(2)}, u32[]{:S(2)}) collective-permute-start(s32[26,128]{1,0:T(8,128)} %bitcast.5), channel_id=1, source_target_pairs={{0,1},{1,0},{2,3},{3,2},{4,5},{5,4},{6,7},{7,6},{8,9},{9,8},{10,11... | collective-permute-start | bytes 39944 | tf_op jit(solution)/shard_map/ppermute | solution.py:354
  3.8 2.6 %collective-permute-start.3 = (bf16[16,128]{1,0:T(8,128)(2,1)}, bf16[16,128]{1,0:T(8,128)(2,1)S(1)}, u32[]{:S(2)}, u32[]{:S(2)}) collective-permute-start(bf16[16,128]{1,0:T(8,128)(2,1)} %param.10), channel_id=1, source_target_pairs={{0,0},{5,1},{10,2},{15,3},{4,4},{1,5},{14,6},{11,7},{8,8},{13,9},{... | collective-permute-start | bytes 12296 | tf_op jit(solution)/shard_map/ppermute | solution.py:368
  13.5 11.2 %collective-permute-start.4 = (bf16[912,128]{1,0:T(8,128)(2,1)S(1)}, bf16[912,128]{1,0:T(8,128)(2,1)S(1)}, u32[]{:S(2)}, u32[]{:S(2)}) collective-permute-start(bf16[912,128]{1,0:T(8,128)(2,1)S(1)} %get-tuple-element.38), channel_id=1, source_target_pairs={{0,1},{1,0},{2,3},{3,2},{4,5},{5,4},{6,7},{7,6},{8,9},{9,8},{10,11... | collective-permute-start | bytes 700424 | tf_op jit(solution)/shard_map/ppermute | solution.py:354
  15.3 6.9 %collective-permute-start.5 = (bf16[528,128]{1,0:T(8,128)(2,1)S(1)}, bf16[528,128]{1,0:T(8,128)(2,1)S(1)}, u32[]{:S(2)}, u32[]{:S(2)}) collective-permute-start(bf16[528,128]{1,0:T(8,128)(2,1)S(1)} %get-tuple-element.39), channel_id=1, source_target_pairs={{0,2},{1,3},{2,0},{3,1},{4,6},{5,7},{6,4},{7,5},{8,10},{9,11},{10,... | collective-permute-start | bytes 405512 | tf_op jit(solution)/shard_map/ppermute | solution.py:354
  17.8 6.9 %collective-permute-start.6 = (bf16[528,128]{1,0:T(8,128)(2,1)S(1)}, bf16[528,128]{1,0:T(8,128)(2,1)S(1)}, u32[]{:S(2)}, u32[]{:S(2)}) collective-permute-start(bf16[528,128]{1,0:T(8,128)(2,1)S(1)} %get-tuple-element.40), channel_id=1, source_target_pairs={{0,3},{1,2},{2,1},{3,0},{4,7},{5,6},{6,5},{7,4},{8,11},{9,10},{10,... | collective-permute-start | bytes 405512 | tf_op jit(solution)/shard_map/ppermute | solution.py:354
  17.9 11.0 %collective-permute-start.7 = (bf16[384,128]{1,0:T(8,128)(2,1)S(1)}, bf16[384,128]{1,0:T(8,128)(2,1)S(1)}, u32[]{:S(2)}, u32[]{:S(2)}) collective-permute-start(bf16[384,128]{1,0:T(8,128)(2,1)S(1)} %get-tuple-element.41), channel_id=1, source_target_pairs={{0,2},{1,3},{2,0},{3,1},{4,6},{5,7},{6,4},{7,5},{8,10},{9,11},{10,... | collective-permute-start | bytes 294920 | tf_op jit(solution)/shard_map/ppermute | solution.py:354
  19.6 9.3 %collective-permute-start.8 = (bf16[384,128]{1,0:T(8,128)(2,1)S(1)}, bf16[384,128]{1,0:T(8,128)(2,1)S(1)}, u32[]{:S(2)}, u32[]{:S(2)}) collective-permute-start(bf16[384,128]{1,0:T(8,128)(2,1)S(1)} %get-tuple-element.42), channel_id=1, source_target_pairs={{0,3},{1,2},{2,1},{3,0},{4,7},{5,6},{6,5},{7,4},{8,11},{9,10},{10,... | collective-permute-start | bytes 294920 | tf_op jit(solution)/shard_map/ppermute | solution.py:354
  24.7 4.7 %collective-permute-start.9 = (bf16[64,128]{1,0:T(8,128)(2,1)S(1)}, bf16[64,128]{1,0:T(8,128)(2,1)S(1)}, u32[]{:S(2)}, u32[]{:S(2)}) collective-permute-start(bf16[64,128]{1,0:T(8,128)(2,1)S(1)} %shard_map.117.refs_2_), channel_id=1, source_target_pairs={{16,0},{20,4},{24,8},{28,12},{0,16},{4,20},{8,24},{12,28},{17,1},{... | collective-permute-start | bytes 49160 | tf_op jit(solution)/shard_map/ppermute | solution.py:443
  32.4 12.0 %collective-permute-start.13 = (bf16[384,128]{1,0:T(8,128)(2,1)S(1)}, bf16[384,128]{1,0:T(8,128)(2,1)S(1)}, u32[]{:S(2)}, u32[]{:S(2)}) collective-permute-start(bf16[384,128]{1,0:T(8,128)(2,1)S(1)} %get-tuple-element.54._), channel_id=1, source_target_pairs={{0,2},{1,3},{2,0},{3,1},{4,6},{5,7},{6,4},{7,5},{8,10},{9,11},{10,... | collective-permute-start | bytes 294920 | tf_op jit(solution)/shard_map/ppermute | solution.py:354
  34.0 6.6 %collective-permute-start.11 = (bf16[512,128]{1,0:T(8,128)(2,1)S(1)}, bf16[512,128]{1,0:T(8,128)(2,1)S(1)}, u32[]{:S(2)}, u32[]{:S(2)}) collective-permute-start(bf16[512,128]{1,0:T(8,128)(2,1)S(1)} %get-tuple-element.57), channel_id=1, source_target_pairs={{0,2},{1,3},{2,0},{3,1},{4,6},{5,7},{6,4},{7,5},{8,10},{9,11},{10,... | collective-permute-start | bytes 393224 | tf_op jit(solution)/shard_map/ppermute | solution.py:354
  34.5 8.3 %collective-permute-start.12 = (bf16[512,128]{1,0:T(8,128)(2,1)S(1)}, bf16[512,128]{1,0:T(8,128)(2,1)S(1)}, u32[]{:S(2)}, u32[]{:S(2)}) collective-permute-start(bf16[512,128]{1,0:T(8,128)(2,1)S(1)} %get-tuple-element.58), channel_id=1, source_target_pairs={{0,3},{1,2},{2,1},{3,0},{4,7},{5,6},{6,5},{7,4},{8,11},{9,10},{10,... | collective-permute-start | bytes 393224 | tf_op jit(solution)/shard_map/ppermute | solution.py:354
  35.1 9.2 %collective-permute-start.14 = (bf16[384,128]{1,0:T(8,128)(2,1)S(1)}, bf16[384,128]{1,0:T(8,128)(2,1)S(1)}, u32[]{:S(2)}, u32[]{:S(2)}) collective-permute-start(bf16[384,128]{1,0:T(8,128)(2,1)S(1)} %get-tuple-element.60), channel_id=1, source_target_pairs={{0,3},{1,2},{2,1},{3,0},{4,7},{5,6},{6,5},{7,4},{8,11},{9,10},{10,... | collective-permute-start | bytes 294920 | tf_op jit(solution)/shard_map/ppermute | solution.py:354
  36.2 6.6 %collective-permute-start.10 = (bf16[896,128]{1,0:T(8,128)(2,1)S(1)}, bf16[896,128]{1,0:T(8,128)(2,1)S(1)}, u32[]{:S(2)}, u32[]{:S(2)}) collective-permute-start(bf16[896,128]{1,0:T(8,128)(2,1)S(1)} %get-tuple-element.56), channel_id=1, source_target_pairs={{0,1},{1,0},{2,3},{3,2},{4,5},{5,4},{6,7},{7,6},{8,9},{9,8},{10,11... | collective-permute-start | bytes 688136 | tf_op jit(solution)/shard_map/ppermute | solution.py:354

commit v2 on v1

--- a/solution.py
+++ b/solution.py
@@ -10,7 +10,7 @@
 
 BF16 = jnp.bfloat16
 F32 = jnp.float32
-ROW_PARTS = (4, 3)
+ROW_PARTS = (3, 4)
 GRAD_PARTS = (4, 3)
 NEAR = 2
 VMEM = pl.BlockSpec(memory_space=pltpu.VMEM)
@@ -101,38 +101,26 @@
     find(lines[...].T, tables, range(NEAR, owners), span, pad, outs, lines.shape[1])
 
 
+def partner_kernel(slots, pad, lines, _, tables, shard, out):
+    batch = lines.shape[1]
+    find(lines[...].T, tables, [1], (0, slots), pad, [out], batch)
+    out[slots * batch : slots * batch + shard.shape[0], :] = shard[...]
+
+
 def near_kernel(owners, slots, pad, *refs):
-    (meta, lines, _, tables, shard) = refs[:5]
-    down_hbm, up_hbm, cot_hbm, bias_hbm, dense_hbm, hot_hbm = refs[5:11]
-    outs = refs[11 : 11 + NEAR]
-    down, up, cot, bias, dense, hot = refs[11 + NEAR : 17 + NEAR]
-    bias_in, sems = refs[17 + NEAR :]
-    batch, width = dense.shape
-    height = shard.shape[0]
-    total = owners * slots
-    copies = [
-        pltpu.make_async_copy(bias_hbm, bias_in, sems.at[3]),
-        pltpu.make_async_copy(dense_hbm, dense, sems.at[4]),
-        pltpu.make_async_copy(hot_hbm, hot, sems.at[5]),
-    ]
-    for copy in copies:
-        copy.start()
-    block = lambda index: pl.ds(pl.multiple_of(index * width, width), width)
-    spots = [0] + [jnp.maximum(meta[0, i], 0) + 1 for i in range(total)]
-    for i, spot in enumerate(spots):
-        here = pl.ds(i * width, width)
-        pltpu.make_async_copy(down_hbm.at[block(spot), :], down.at[here, :], sems.at[0]).start()
-        pltpu.make_async_copy(up_hbm.at[:, block(spot)], up.at[:, here], sems.at[1]).start()
-        pltpu.make_async_copy(cot_hbm.at[:, block(spot)], cot.at[:, here], sems.at[2]).start()
-    find(lines[...].T, tables, range(NEAR), (0, slots), pad, outs, batch)
-    outs[1][slots * batch : slots * batch + height, :] = shard[...]
-    for copy in copies:
-        copy.wait()
-    for i, spot in enumerate(spots):
+    meta, lines, _, tables, down_in, up_in, cot_in, bias_in = refs[:8]
+    out, down, up, cot, bias = refs[8:]
+    batch = lines.shape[1]
+    width = bias.shape[1]
+    for i in range(owners * slots + 1):
+        spot = jnp.maximum(meta[0, i - 1], 0) + 1 if i else 0
+        block = pl.ds(pl.multiple_of(spot * width, width), width) if i else slice(0, width)
+        here = slice(i * width, (i + 1) * width)
+        down[here, :] = down_in[block, :]
+        up[:, here] = up_in[:, block]
+        cot[:, here] = cot_in[:, block]
         bias[i : i + 1, :] = bias_in[pl.ds(spot, 1), :]
-    pltpu.make_async_copy(down, down, sems.at[0]).wait()
-    pltpu.make_async_copy(up, up, sems.at[1]).wait()
-    pltpu.make_async_copy(cot, cot, sems.at[2]).wait()
+    find(lines[...].T, tables, [0], (0, slots), pad, [out], batch)
 
 
 def shards_kernel(owners, *refs):
@@ -168,16 +156,14 @@
         out[i * batch : (i + 1) * batch, :] = result[:, i * width : (i + 1) * width]
 
 
-def first_kernel(span, owners, slots, *refs):
-    near, far = refs[:NEAR], refs[NEAR:owners]
-    down, up, cot, low_out, grad_out = refs[owners:]
+def sums_kernel(span, masks, slots, *refs):
+    rows, refs = refs[: len(masks)], refs[len(masks) :]
+    down, up, cot = refs[:3]
+    low, grad = (ref[...] for ref in refs[3:5]) if len(refs) == 7 else (None, None)
+    low_out, grad_out = refs[-2:]
     batch = cot.shape[0]
-    width = near[0].shape[1]
-    low = grad = None
-    for k, ref in enumerate(near):
-        x = wide(ref, slots, batch)
-        low, grad = add_up(x, (1 + k * slots) * width, down, up, cot, low, grad)
-    for k, ref in enumerate(far, NEAR):
+    width = rows[0].shape[1]
+    for k, ref in zip(masks, rows):
         x = wide(ref, span[1], batch)
         low, grad = add_up(x, (1 + k * slots + span[0]) * width, down, up, cot, low, grad)
     low_out[...] = low
@@ -381,6 +367,7 @@
         [HBM] * 3,
         scratch=[pltpu.SMEM(table_slot.shape, jnp.int32), pltpu.SemaphoreType.DMA((3,))],
         mib=1,
+        flops=1e9,
     )
     lines, *sends = call(
         functools.partial(far_first_kernel, row_spans[0], owners, slots, pad),
@@ -389,6 +376,7 @@
         [meta, ids, near_ids, *far_ids, tables, shard],
         [SMEM] + [VMEM] * (owners + 2),
         mib=4,
+        flops=1e9,
     )
     far = [far_swap(sends)]
     again, *sends = call(
@@ -396,40 +384,33 @@
         [shape(8, batch, dtype=jnp.int32)] + [shape(row_spans[1][1] * batch, width)] * far_count,
         [lines, tables],
         mib=4,
+        flops=5e8,
     )
     far.append(far_swap(sends))
     features = (total + 1) * width
-    *near, down, up, cot, bias, dense, hot_rows = call(
+    (partner,) = call(
+        functools.partial(partner_kernel, slots, pad),
+        [shape(slots * batch + height, width)],
+        [lines, again, tables, shard],
+        mib=4,
+        flops=5e8,
+    )
+    mine, down, up, cot, bias = call(
         functools.partial(near_kernel, owners, slots, pad),
-        [shape(slots * batch, width), shape(slots * batch + height, width)]
-        + [
+        [
+            shape(slots * batch, width),
             shape(features, rank),
             shape(rank, features),
             shape(batch, features),
             shape(-(-(total + 1) // 8) * 8, width, dtype=F32),
-            shape(batch, width),
-            shape(hot_ids.shape[1], batch, dtype=jnp.int32),
         ],
-        [meta, lines, again, tables, shard]
-        + [
-            in_hbm(x)
-            for x in (
-                down_rank,
-                up_rank,
-                cotangent,
-                cross_bias.reshape(-1, width),
-                dense,
-                hot_ids.T,
-            )
-        ],
-        [SMEM] + [VMEM] * 4 + [HBM] * 6,
-        scratch=[
-            pltpu.VMEM((cross_bias.shape[0] // width, width), F32),
-            pltpu.SemaphoreType.DMA((6,)),
-        ],
-        mib=6,
-    )
-    near[1] = swap(near[1], 1)
+        [meta, lines, partner, tables]
+        + [down_rank, up_rank, cotangent, cross_bias.reshape(-1, width)],
+        [SMEM] + [VMEM] * 7,
+        mib=6,
+    )
+    hot_rows = hot_ids.T
+    near = [mine, swap(partner, 1)]
 
     (group,) = call(
         functools.partial(shards_kernel, owners),
@@ -442,10 +423,17 @@
         pairs = [(peer(b, mask, blocks), b) for b in range(blocks)]
         shards.append(lax.ppermute(group, "blk", pairs))
 
+    sums = [shape(batch, rank, dtype=F32)] * 2
     low, grad = call(
-        functools.partial(first_kernel, row_spans[0], owners, slots),
-        [shape(batch, rank, dtype=F32)] * 2,
-        [*near, *far[0], down, up, cot],
+        functools.partial(sums_kernel, (0, slots), range(NEAR), slots),
+        sums,
+        [*near, down, up, cot],
+        mib=6,
+    )
+    low, grad = call(
+        functools.partial(sums_kernel, row_spans[0], range(NEAR, owners), slots),
+        sums,
+        [*far[0], down, up, cot, low, grad],
         mib=6,
     )
     front, low, grad, *sends = call(

time: 46 us -> 40.2 us (0.87)
  the two profiles are of different devices: /device:TPU:0 before, /device:TPU:1 now
where the time goes in v2:
time: 40.2 us; the launch traced here: 40 us
  starting transfers between devices  17.9 us (45%)
  Pallas kernels  15.3 us (38%)
  waiting for transfers between devices  5.91 us (15%)
  between operations  0.84 us (2%)
    pallas_call x12, Pallas kernels, call(): pl.pallas_call(kernel, out_shape=shapes, in_specs=specs or [VMEM] * len(o...  12.6 us
    ppermute x13, starting transfers between devices, swap(): return lax.ppermute(array, 'table', [(i, i ^ k) for i in range(owners)])  12.4 us
    ppermute x13, waiting for transfers between devices, swap(): return lax.ppermute(array, 'table', [(i, i ^ k) for i in range(owners)])  5.79 us
    ppermute x1, starting transfers between devices, on_device(): lax.ppermute(hot_slab, ('blk', 'table'), [(peer(b, t, blocks) * owners +...  3.11 us
    ppermute x1, starting transfers between devices, on_device(): shards.append(lax.ppermute(group, 'blk', pairs))  2.37 us
    pallas_call x1, Pallas kernels, on_device(): pl.pallas_call(functools.partial(scatter_kernel, grad_spans[0], later, ow...  1.52 us
    pallas_call x1, Pallas kernels, on_device(): pl.pallas_call(functools.partial(last_kernel, later, owners, pad), out_sh...  1.2 us
  transfers between devices with their start and end apart: 15, of which 4 were waited for; matrix products, arithmetic and copies ran while one was open for 0% of the time, Pallas kernels for 25%

profile of v2, /device:TPU:1, one launch (start us, length us, event | category | flops | bytes accessed | tf_op | source)
XLA Modules:
  0.0 40.0 jit_solution(10281690192249835410)
XLA Ops:
  0.6 2.7 %collective-permute-start.2 = (s32[26,128]{1,0:T(8,128)}, s32[26,128]{1,0:T(8,128)S(1)}, u32[]{:S(2)}, u32[]{:S(2)}) collective-permute-start(s32[26,128]{1,0:T(8,128)} %bitcast.5), channel_id=1, source_target_pairs={{0,3},{1,2},{2,1},{3,0},{4,7},{5,6},{6,5},{7,4},{8,11},{9,10},{10,... | collective-permute-start | bytes 39944 | tf_op jit(solution)/shard_map/ppermute | solution.py:340
  3.3 0.0 collective-permute-start.1
  3.3 0.5 %collective-permute-start = (s32[26,128]{1,0:T(8,128)}, s32[26,128]{1,0:T(8,128)S(1)}, u32[]{:S(2)}, u32[]{:S(2)}) collective-permute-start(s32[26,128]{1,0:T(8,128)} %bitcast.7), channel_id=1, source_target_pairs={{0,1},{1,0},{2,3},{3,2},{4,5},{5,4},{6,7},{7,6},{8,9},{9,8},{10,11... | collective-permute-start | bytes 39944 | tf_op jit(solution)/shard_map/ppermute | solution.py:340
  3.8 3.1 %collective-permute-start.3 = (bf16[16,128]{1,0:T(8,128)(2,1)}, bf16[16,128]{1,0:T(8,128)(2,1)S(1)}, u32[]{:S(2)}, u32[]{:S(2)}) collective-permute-start(bf16[16,128]{1,0:T(8,128)(2,1)} %param.10), channel_id=1, source_target_pairs={{0,0},{5,1},{10,2},{15,3},{4,4},{1,5},{14,6},{11,7},{8,8},{13,9},{... | collective-permute-start | bytes 12296 | tf_op jit(solution)/shard_map/ppermute | solution.py:354
  6.9 1.3 %shard_map.113 = (bf16[7,512,128]{2,1,0:T(8,128)(2,1)S(1)}, s32[26,128]{1,0:T(8,128)S(1)}, s32[8,128]{1,0:T(8,128)S(1)}) custom-call(s32[26]{0:T(128)} %slot_hbm.1, bf16[7,512,128]{2,1,0:T(8,128)(2,1)} %tables_hbm.1, s32[26,128]{1,0:T(8,128)} %bitcast.8), custom_call_target="tpu_custom_call" | custom-call | flops 1000000000 | bytes 1048576 | tf_op jit(solution)/shard_map/pallas_call | solution.py:329
  8.2 0.1 collective-permute-done.3.refs_6_.shard.refs_0_
  8.3 0.0 collective-permute-done.2.refs_4_
  8.3 0.0 collective-permute-done.1.refs_3_
  8.3 0.0 collective-permute-done.refs_2_
  8.4 0.0 copy-start
  8.4 0.0 copy-start.1
  8.4 0.0 copy-start.4
  8.4 1.1 %shard_map.114 = (s32[32,128]{1,0:T(8,128)S(1)}, bf16[400,128]{1,0:T(8,128)(2,1)S(1)}, bf16[400,128]{1,0:T(8,128)(2,1)S(1)}) custom-call(s32[8,128]{1,0:T(8,128)S(1)} %get-tuple-element.31.refs_0_, s32[26,128]{1,0:T(8,128)S(1)} %get-tuple-element.32.refs_1_, s32[26,128]{1,0:T(8,128)S(1)} %collective-permute-done.refs_2_, ...), custom_call_target="tpu_custom_call" | custom-call | flops 1000000000 | bytes 1048576 | tf_op jit(solution)/shard_map/pallas_call | solution.py:329
  9.5 2.1 %collective-permute-start.5 = (bf16[400,128]{1,0:T(8,128)(2,1)S(1)}, bf16[400,128]{1,0:T(8,128)(2,1)S(1)}, u32[]{:S(2)}, u32[]{:S(2)}) collective-permute-start(bf16[400,128]{1,0:T(8,128)(2,1)S(1)} %get-tuple-element.37), channel_id=1, source_target_pairs={{0,2},{1,3},{2,0},{3,1},{4,6},{5,7},{6,4},{7,5},{8,10},{9,11},{10,... | collective-permute-start | bytes 307208 | tf_op jit(solution)/shard_map/ppermute | solution.py:340
  11.6 0.6 %collective-permute-start.6 = (bf16[400,128]{1,0:T(8,128)(2,1)S(1)}, bf16[400,128]{1,0:T(8,128)(2,1)S(1)}, u32[]{:S(2)}, u32[]{:S(2)}) collective-permute-start(bf16[400,128]{1,0:T(8,128)(2,1)S(1)} %get-tuple-element.38), channel_id=1, source_target_pairs={{0,3},{1,2},{2,1},{3,0},{4,7},{5,6},{6,5},{7,4},{8,11},{9,10},{10,... | collective-permute-start | bytes 307208 | tf_op jit(solution)/shard_map/ppermute | solution.py:340
  12.2 0.6 %shard_map.115 = (s32[8,128]{1,0:T(8,128)S(1)}, bf16[512,128]{1,0:T(8,128)(2,1)S(1)}, bf16[512,128]{1,0:T(8,128)(2,1)S(1)}) custom-call(s32[32,128]{1,0:T(8,128)S(1)} %get-tuple-element.34.lines.refs_1_.refs_0_, bf16[7,512,128]{2,1,0:T(8,128)(2,1)S(1)} %get-tuple-element.33.refs_5_.tables.refs_3_), custom_call_target="tpu_custom_call" | custom-call | flops 500000000 | bytes 1048576 | tf_op jit(solution)/shard_map/pallas_call | solution.py:329
  12.8 1.7 %collective-permute-start.7 = (bf16[512,128]{1,0:T(8,128)(2,1)S(1)}, bf16[512,128]{1,0:T(8,128)(2,1)S(1)}, u32[]{:S(2)}, u32[]{:S(2)}) collective-permute-start(bf16[512,128]{1,0:T(8,128)(2,1)S(1)} %get-tuple-element.39), channel_id=1, source_target_pairs={{0,2},{1,3},{2,0},{3,1},{4,6},{5,7},{6,4},{7,5},{8,10},{9,11},{10,... | collective-permute-start | bytes 393224 | tf_op jit(solution)/shard_map/ppermute | solution.py:340
  14.5 0.3 collective-permute-start.8
  14.8 0.5 %shard_map.116.refs_2_ = bf16[912,128]{1,0:T(8,128)(2,1)S(1)} custom-call(s32[32,128]{1,0:T(8,128)S(1)} %get-tuple-element.34.lines.refs_1_.refs_0_, s32[8,128]{1,0:T(8,128)S(1)} %get-tuple-element.35._, bf16[7,512,128]{2,1,0:T(8,128)(2,1)S(1)} %get-tuple-element.33.refs_5_.tables.refs_3_, bf16[16,128]{1,0:T(8,128)(2,1)S(1)} %collective-permute-done.3.refs_6_.shard.refs_0_), custom_call_target="tpu_custom_call" | custom-call | flops 500000000 | bytes 1048576 | tf_op jit(solution)/shard_map/pallas_call | solution.py:329
  15.3 0.3 collective-permute-start.4
  15.6 2.1 %shard_map.117 = (bf16[896,128]{1,0:T(8,128)(2,1)S(1)}, bf16[3712,512]{1,0:T(8,128)(2,1)S(1)}, bf16[512,3712]{1,0:T(8,128)(2,1)S(1)}, bf16[128,3712]{1,0:T(8,128)(2,1)S(1)}, f32[32,128]{1,0:T(8,128)S(1)}) custom-call(s32[8,128]{1,0:T(8,128)S(1)} %get-tuple-element.31.refs_0_, s32[32,128]{1,0:T(8,128)S(1)} %get-tuple-element.34.lines.refs_1_.refs_0_, ...), custom_call_target="tpu_custom_call" | custom-call | flops 4000000000 | bytes 1048576 | tf_op jit(solution)/shard_map/pallas_call | solution.py:329
  17.7 0.0 collective-permute-done.5.refs_2_.refs_0_.refs_3_
  17.7 0.0 collective-permute-done.6.refs_3_.refs_1_.refs_4_
  17.7 0.0 collective-permute-done.4.refs_1_.refs_2_
  17.7 2.4 %collective-permute-start.9 = (bf16[64,128]{1,0:T(8,128)(2,1)S(1)}, bf16[64,128]{1,0:T(8,128)(2,1)S(1)}, u32[]{:S(2)}, u32[]{:S(2)}) collective-permute-start(bf16[64,128]{1,0:T(8,128)(2,1)S(1)} %shard_map.118.refs_2_), channel_id=1, source_target_pairs={{16,0},{20,4},{24,8},{28,12},{0,16},{4,20},{8,24},{12,28},{17,1},{... | collective-permute-start | bytes 49160 | tf_op jit(solution)/shard_map/ppermute | solution.py:424
  20.1 1.0 %shard_map.119 = (f32[128,512]{1,0:T(8,128)S(1)}, f32[128,512]{1,0:T(8,128)S(1)}) custom-call(bf16[896,128]{1,0:T(8,128)(2,1)S(1)} %get-tuple-element.36.refs_0_.refs_1_, bf16[912,128]{1,0:T(8,128)(2,1)S(1)} %collective-permute-done.4.refs_1_.refs_2_, bf16[3712,512]{1,0:T(8,128)(2,1)S(1)} %get-tuple-element.41.refs_2_.refs_8_.down, ...), custom_call_target="tpu_custom_call" | custom-call | flops 4000000000 | bytes 1048576 | tf_op jit(solution)/shard_map/pallas_call | solution.py:329
  21.1 0.0 copy-start.3
  21.1 0.0 copy-start.5
  21.1 0.6 %shard_map.120 = (f32[128,512]{1,0:T(8,128)S(1)}, f32[128,512]{1,0:T(8,128)S(1)}) custom-call(bf16[400,128]{1,0:T(8,128)(2,1)S(1)} %collective-permute-done.5.refs_2_.refs_0_.refs_3_, bf16[400,128]{1,0:T(8,128)(2,1)S(1)} %collective-permute-done.6.refs_3_.refs_1_.refs_4_, bf16[3712,512]{1,0:T(8,128)(2,1)S(1)} %get-tuple-element.41.refs_2_.refs_8_.down, ...), custom_call_target="tpu_custom_call" | custom-call | flops 4000000000 | bytes 1048576 | tf_op jit(solution)/shard_map/pallas_call | solution.py:329
  21.7 0.0 collective-permute-done.7.refs_0_.refs_5_
  21.7 1.1 %collective-permute-done.8.refs_1_.refs_6_ = bf16[512,128]{1,0:T(8,128)(2,1)S(1)} collective-permute-done((bf16[512,128]{1,0:T(8,128)(2,1)S(1)}, bf16[512,128]{1,0:T(8,128)(2,1)S(1)}, u32[]{:S(2)}, u32[]{:S(2)}) %collective-permute-start.8) | collective-permute-done | bytes 131104 | tf_op jit(solution)/shard_map/ppermute | solution.py:340
  22.8 0.0 collective-permute-done.9.refs_3_
  22.8 1.5 %shard_map.121 = (bf16[128,128]{1,0:T(8,128)(2,1)S(1)}, bf16[128,512]{1,0:T(8,128)(2,1)S(1)}, bf16[128,512]{1,0:T(8,128)(2,1)S(1)}, bf16[512,128]{1,0:T(8,128)(2,1)S(1)}, bf16[512,128]{1,0:T(8,128)(2,1)S(1)}) custom-call(bf16[512,128]{1,0:T(8,128)(2,1)S(1)} %collective-permute-done.7.refs_0_.refs_5_, ...), custom_call_target="tpu_custom_call" | custom-call | flops 4000000000 | bytes 1048576 | tf_op jit(solution)/shard_map/pallas_call | solution.py:329
  24.4 0.5 %shard_map.122 = (bf16[384,128]{1,0:T(8,128)(2,1)S(1)}, bf16[384,128]{1,0:T(8,128)(2,1)S(1)}) custom-call(bf16[128,512]{1,0:T(8,128)(2,1)S(1)} %get-tuple-element.50.low.refs_8_, bf16[128,512]{1,0:T(8,128)(2,1)S(1)} %get-tuple-element.51.grad, bf16[3712,512]{1,0:T(8,128)(2,1)S(1)} %get-tuple-element.41.refs_2_.refs_8_.down, ...), custom_call_target="tpu_custom_call" | custom-call | flops 4000000000 | bytes 1048576 | tf_op jit(solution)/shard_map/pallas_call | solution.py:329
  24.9 1.0 %shard_map.123 = (bf16[896,128]{1,0:T(8,128)(2,1)S(1)}, bf16[896,128]{1,0:T(8,128)(2,1)S(1)}) custom-call(bf16[128,512]{1,0:T(8,128)(2,1)S(1)} %get-tuple-element.50.low.refs_8_, bf16[128,512]{1,0:T(8,128)(2,1)S(1)} %get-tuple-element.51.grad, bf16[3712,512]{1,0:T(8,128)(2,1)S(1)} %get-tuple-element.41.refs_2_.refs_8_.down, ...), custom_call_target="tpu_custom_call" | custom-call | flops 4000000000 | bytes 1048576 | tf_op jit(solution)/shard_map/pallas_call | solution.py:329
  25.9 1.3 %collective-permute-start.13 = (bf16[384,128]{1,0:T(8,128)(2,1)S(1)}, bf16[384,128]{1,0:T(8,128)(2,1)S(1)}, u32[]{:S(2)}, u32[]{:S(2)}) collective-permute-start(bf16[384,128]{1,0:T(8,128)(2,1)S(1)} %get-tuple-element.52._), channel_id=1, source_target_pairs={{0,2},{1,3},{2,0},{3,1},{4,6},{5,7},{6,4},{7,5},{8,10},{9,11},{10,... | collective-permute-start | bytes 294920 | tf_op jit(solution)/shard_map/ppermute | solution.py:340
  27.2 0.2 collective-permute-start.11
  27.4 1.5 %collective-permute-start.12 = (bf16[512,128]{1,0:T(8,128)(2,1)S(1)}, bf16[512,128]{1,0:T(8,128)(2,1)S(1)}, u32[]{:S(2)}, u32[]{:S(2)}) collective-permute-start(bf16[512,128]{1,0:T(8,128)(2,1)S(1)} %get-tuple-element.56), channel_id=1, source_target_pairs={{0,3},{1,2},{2,1},{3,0},{4,7},{5,6},{6,5},{7,4},{8,11},{9,10},{10,... | collective-permute-start | bytes 393224 | tf_op jit(solution)/shard_map/ppermute | solution.py:340
  29.0 0.2 collective-permute-start.14
  29.2 1.0 %collective-permute-start.10 = (bf16[896,128]{1,0:T(8,128)(2,1)S(1)}, bf16[896,128]{1,0:T(8,128)(2,1)S(1)}, u32[]{:S(2)}, u32[]{:S(2)}) collective-permute-start(bf16[896,128]{1,0:T(8,128)(2,1)S(1)} %get-tuple-element.54), channel_id=1, source_target_pairs={{0,1},{1,0},{2,3},{3,2},{4,5},{5,4},{6,7},{7,6},{8,9},{9,8},{10,11... | collective-permute-start | bytes 688136 | tf_op jit(solution)/shard_map/ppermute | solution.py:340
  30.2 2.4 %shard_map.124 = bf16[128,3456]{1,0:T(8,128)(2,1)} custom-call(s32[8,128]{1,0:T(8,128)S(1)} %get-tuple-element.31.refs_0_, bf16[896,128]{1,0:T(8,128)(2,1)S(1)} %get-tuple-element.36.refs_0_.refs_1_, bf16[912,128]{1,0:T(8,128)(2,1)S(1)} %collective-permute-done.4.refs_1_.refs_2_, bf16[400,128]{1,0:T(8,128)(2,1)S(1)} %collective-permute-done.5.refs_2_.refs_0_.refs_3_, ...), custom_call_target="tpu_custom_call" | custom-call | flops 4000000000 | bytes 1048576 | tf_op jit(solution)/shard_map/pallas_call | solution.py:329
  32.6 0.1 collective-permute-done.11.refs_3_
  32.7 4.6 %collective-permute-done.12.refs_4_ = bf16[512,128]{1,0:T(8,128)(2,1)S(1)} collective-permute-done((bf16[512,128]{1,0:T(8,128)(2,1)S(1)}, bf16[512,128]{1,0:T(8,128)(2,1)S(1)}, u32[]{:S(2)}, u32[]{:S(2)}) %collective-permute-start.12) | collective-permute-done | bytes 131104 | tf_op jit(solution)/shard_map/ppermute | solution.py:340
  37.3 0.0 collective-permute-done.10.refs_2_
  37.3 1.5 %scatter.1 = (f32[1,7,512,128]{3,2,1,0:T(8,128)}, f32[3,512,128]{2,1,0:T(8,128)S(1)}) custom-call(s32[32,128]{1,0:T(8,128)S(1)} %get-tuple-element.34.lines.refs_1_.refs_0_, bf16[896,128]{1,0:T(8,128)(2,1)S(1)} %get-tuple-element.53.refs_11_.refs_1_, bf16[896,128]{1,0:T(8,128)(2,1)S(1)} %collective-permute-done.10.refs_2_, ...), custom_call_target="tpu_custom_call" | custom-call | tf_op jit(solution)/shard_map/scatter/pallas_call | solution.py:473
  38.8 0.0 collective-permute-done.14.refs_3_
  38.8 0.0 collective-permute-done.13.refs_2_
  38.8 1.2 %last.1 = f32[1,7,512,128]{3,2,1,0:T(8,128)} custom-call(s32[32,128]{1,0:T(8,128)S(1)} %get-tuple-element.34.lines.refs_1_.refs_0_, f32[3,512,128]{2,1,0:T(8,128)S(1)} %get-tuple-element.57.refs_1_, bf16[384,128]{1,0:T(8,128)(2,1)S(1)} %collective-permute-done.13.refs_2_, ...), custom_call_target="tpu_custom_call", output_to_operand_aliasing={{}: (4, {})} | custom-call | tf_op jit(solution)/shard_map/last/pallas_call | solution.py:485
  (8 shorter events, 0.0 us)
Async XLA Ops:
  0.6 7.7 %collective-permute-start.2 = (s32[26,128]{1,0:T(8,128)}, s32[26,128]{1,0:T(8,128)S(1)}, u32[]{:S(2)}, u32[]{:S(2)}) collective-permute-start(s32[26,128]{1,0:T(8,128)} %bitcast.5), channel_id=1, source_target_pairs={{0,3},{1,2},{2,1},{3,0},{4,7},{5,6},{6,5},{7,4},{8,11},{9,10},{10,... | collective-permute-start | bytes 39944 | tf_op jit(solution)/shard_map/ppermute | solution.py:340
  3.3 5.0 %collective-permute-start.1 = (s32[26,128]{1,0:T(8,128)}, s32[26,128]{1,0:T(8,128)S(1)}, u32[]{:S(2)}, u32[]{:S(2)}) collective-permute-start(s32[26,128]{1,0:T(8,128)} %bitcast.6), channel_id=1, source_target_pairs={{0,2},{1,3},{2,0},{3,1},{4,6},{5,7},{6,4},{7,5},{8,10},{9,11},{10,... | collective-permute-start | bytes 39944 | tf_op jit(solution)/shard_map/ppermute | solution.py:340
  3.3 5.0 %collective-permute-start = (s32[26,128]{1,0:T(8,128)}, s32[26,128]{1,0:T(8,128)S(1)}, u32[]{:S(2)}, u32[]{:S(2)}) collective-permute-start(s32[26,128]{1,0:T(8,128)} %bitcast.7), channel_id=1, source_target_pairs={{0,1},{1,0},{2,3},{3,2},{4,5},{5,4},{6,7},{7,6},{8,9},{9,8},{10,11... | collective-permute-start | bytes 39944 | tf_op jit(solution)/shard_map/ppermute | solution.py:340
  3.8 4.5 %collective-permute-start.3 = (bf16[16,128]{1,0:T(8,128)(2,1)}, bf16[16,128]{1,0:T(8,128)(2,1)S(1)}, u32[]{:S(2)}, u32[]{:S(2)}) collective-permute-start(bf16[16,128]{1,0:T(8,128)(2,1)} %param.10), channel_id=1, source_target_pairs={{0,0},{5,1},{10,2},{15,3},{4,4},{1,5},{14,6},{11,7},{8,8},{13,9},{... | collective-permute-start | bytes 12296 | tf_op jit(solution)/shard_map/ppermute | solution.py:354
  6.9 8.7 %copy-start.2 = (bf16[128,3456]{1,0:T(8,128)(2,1)S(1)}, bf16[128,3456]{1,0:T(8,128)(2,1)}, u32[]{:S(2)}) copy-start(bf16[128,3456]{1,0:T(8,128)(2,1)} %refs_6_.1) | copy-start | bytes 2654212
  8.4 7.2 %copy-start = (bf16[3456,512]{1,0:T(8,128)(2,1)S(1)}, bf16[3456,512]{1,0:T(8,128)(2,1)}, u32[]{:S(2)}) copy-start(bf16[3456,512]{1,0:T(8,128)(2,1)} %refs_4_.1) | copy-start | bytes 10616836
  8.4 7.2 %copy-start.1 = (bf16[512,3456]{1,0:T(8,128)(2,1)S(1)}, bf16[512,3456]{1,0:T(8,128)(2,1)}, u32[]{:S(2)}) copy-start(bf16[512,3456]{1,0:T(8,128)(2,1)} %refs_5_.2) | copy-start | bytes 10616836
  8.4 7.2 %copy-start.4 = (f32[3456]{0:T(1024)S(1)}, f32[3456]{0:T(1024)}, u32[]{:S(2)}) copy-start(f32[3456]{0:T(1024)} %param.18) | copy-start | bytes 41476
  9.5 8.2 %collective-permute-start.5 = (bf16[400,128]{1,0:T(8,128)(2,1)S(1)}, bf16[400,128]{1,0:T(8,128)(2,1)S(1)}, u32[]{:S(2)}, u32[]{:S(2)}) collective-permute-start(bf16[400,128]{1,0:T(8,128)(2,1)S(1)} %get-tuple-element.37), channel_id=1, source_target_pairs={{0,2},{1,3},{2,0},{3,1},{4,6},{5,7},{6,4},{7,5},{8,10},{9,11},{10,... | collective-permute-start | bytes 307208 | tf_op jit(solution)/shard_map/ppermute | solution.py:340
  11.6 6.1 %collective-permute-start.6 = (bf16[400,128]{1,0:T(8,128)(2,1)S(1)}, bf16[400,128]{1,0:T(8,128)(2,1)S(1)}, u32[]{:S(2)}, u32[]{:S(2)}) collective-permute-start(bf16[400,128]{1,0:T(8,128)(2,1)S(1)} %get-tuple-element.38), channel_id=1, source_target_pairs={{0,3},{1,2},{2,1},{3,0},{4,7},{5,6},{6,5},{7,4},{8,11},{9,10},{10,... | collective-permute-start | bytes 307208 | tf_op jit(solution)/shard_map/ppermute | solution.py:340
  12.8 8.9 %collective-permute-start.7 = (bf16[512,128]{1,0:T(8,128)(2,1)S(1)}, bf16[512,128]{1,0:T(8,128)(2,1)S(1)}, u32[]{:S(2)}, u32[]{:S(2)}) collective-permute-start(bf16[512,128]{1,0:T(8,128)(2,1)S(1)} %get-tuple-element.39), channel_id=1, source_target_pairs={{0,2},{1,3},{2,0},{3,1},{4,6},{5,7},{6,4},{7,5},{8,10},{9,11},{10,... | collective-permute-start | bytes 393224 | tf_op jit(solution)/shard_map/ppermute | solution.py:340
  14.5 8.3 %collective-permute-start.8 = (bf16[512,128]{1,0:T(8,128)(2,1)S(1)}, bf16[512,128]{1,0:T(8,128)(2,1)S(1)}, u32[]{:S(2)}, u32[]{:S(2)}) collective-permute-start(bf16[512,128]{1,0:T(8,128)(2,1)S(1)} %get-tuple-element.40), channel_id=1, source_target_pairs={{0,3},{1,2},{2,1},{3,0},{4,7},{5,6},{6,5},{7,4},{8,11},{9,10},{10,... | collective-permute-start | bytes 393224 | tf_op jit(solution)/shard_map/ppermute | solution.py:340
  15.3 2.4 %collective-permute-start.4 = (bf16[912,128]{1,0:T(8,128)(2,1)S(1)}, bf16[912,128]{1,0:T(8,128)(2,1)S(1)}, u32[]{:S(2)}, u32[]{:S(2)}) collective-permute-start(bf16[912,128]{1,0:T(8,128)(2,1)S(1)} %shard_map.116.refs_2_), channel_id=1, source_target_pairs={{0,1},{1,0},{2,3},{3,2},{4,5},{5,4},{6,7},{7,6},{8,9},{9,8},{10,11... | collective-permute-start | bytes 700424 | tf_op jit(solution)/shard_map/ppermute | solution.py:340
  17.7 5.1 %collective-permute-start.9 = (bf16[64,128]{1,0:T(8,128)(2,1)S(1)}, bf16[64,128]{1,0:T(8,128)(2,1)S(1)}, u32[]{:S(2)}, u32[]{:S(2)}) collective-permute-start(bf16[64,128]{1,0:T(8,128)(2,1)S(1)} %shard_map.118.refs_2_), channel_id=1, source_target_pairs={{16,0},{20,4},{24,8},{28,12},{0,16},{4,20},{8,24},{12,28},{17,1},{... | collective-permute-start | bytes 49160 | tf_op jit(solution)/shard_map/ppermute | solution.py:424
  21.1 1.7 %copy-start.3 = (bf16[128,128]{1,0:T(8,128)(2,1)S(1)}, bf16[128,128]{1,0:T(8,128)(2,1)}, u32[]{:S(2)}) copy-start(bf16[128,128]{1,0:T(8,128)(2,1)} %refs_5_.3) | copy-start | bytes 98308
  21.1 1.7 %copy-start.5 = (s32[128,16]{0,1:T(8,128)S(1)}, s32[128,16]{0,1:T(8,128)}, u32[]{:S(2)}) copy-start(s32[128,16]{0,1:T(8,128)} %param.11) | copy-start | bytes 24580
  25.9 12.9 %collective-permute-start.13 = (bf16[384,128]{1,0:T(8,128)(2,1)S(1)}, bf16[384,128]{1,0:T(8,128)(2,1)S(1)}, u32[]{:S(2)}, u32[]{:S(2)}) collective-permute-start(bf16[384,128]{1,0:T(8,128)(2,1)S(1)} %get-tuple-element.52._), channel_id=1, source_target_pairs={{0,2},{1,3},{2,0},{3,1},{4,6},{5,7},{6,4},{7,5},{8,10},{9,11},{10,... | collective-permute-start | bytes 294920 | tf_op jit(solution)/shard_map/ppermute | solution.py:340
  27.2 5.5 %collective-permute-start.11 = (bf16[512,128]{1,0:T(8,128)(2,1)S(1)}, bf16[512,128]{1,0:T(8,128)(2,1)S(1)}, u32[]{:S(2)}, u32[]{:S(2)}) collective-permute-start(bf16[512,128]{1,0:T(8,128)(2,1)S(1)} %get-tuple-element.55), channel_id=1, source_target_pairs={{0,2},{1,3},{2,0},{3,1},{4,6},{5,7},{6,4},{7,5},{8,10},{9,11},{10,... | collective-permute-start | bytes 393224 | tf_op jit(solution)/shard_map/ppermute | solution.py:340
  27.4 9.8 %collective-permute-start.12 = (bf16[512,128]{1,0:T(8,128)(2,1)S(1)}, bf16[512,128]{1,0:T(8,128)(2,1)S(1)}, u32[]{:S(2)}, u32[]{:S(2)}) collective-permute-start(bf16[512,128]{1,0:T(8,128)(2,1)S(1)} %get-tuple-element.56), channel_id=1, source_target_pairs={{0,3},{1,2},{2,1},{3,0},{4,7},{5,6},{6,5},{7,4},{8,11},{9,10},{10,... | collective-permute-start | bytes 393224 | tf_op jit(solution)/shard_map/ppermute | solution.py:340
  29.0 9.8 %collective-permute-start.14 = (bf16[384,128]{1,0:T(8,128)(2,1)S(1)}, bf16[384,128]{1,0:T(8,128)(2,1)S(1)}, u32[]{:S(2)}, u32[]{:S(2)}) collective-permute-start(bf16[384,128]{1,0:T(8,128)(2,1)S(1)} %get-tuple-element.58), channel_id=1, source_target_pairs={{0,3},{1,2},{2,1},{3,0},{4,7},{5,6},{6,5},{7,4},{8,11},{9,10},{10,... | collective-permute-start | bytes 294920 | tf_op jit(solution)/shard_map/ppermute | solution.py:340
  29.2 8.1 %collective-permute-start.10 = (bf16[896,128]{1,0:T(8,128)(2,1)S(1)}, bf16[896,128]{1,0:T(8,128)(2,1)S(1)}, u32[]{:S(2)}, u32[]{:S(2)}) collective-permute-start(bf16[896,128]{1,0:T(8,128)(2,1)S(1)} %get-tuple-element.54), channel_id=1, source_target_pairs={{0,1},{1,0},{2,3},{3,2},{4,5},{5,4},{6,7},{7,6},{8,9},{9,8},{10,11... | collective-permute-start | bytes 688136 | tf_op jit(solution)/shard_map/ppermute | solution.py:340

commit v3 on v2

--- a/solution.py
+++ b/solution.py
@@ -32,33 +32,8 @@
     return [(a, b - a) for a, b in zip(ends, ends[1:])]
 
 
-def load_kernel(owners, slots, slot_hbm, tables_hbm, ids_hbm, tables, ids, meta, slot_ref, sems):
-    copies = [
-        pltpu.make_async_copy(slot_hbm, slot_ref, sems.at[0]),
-        pltpu.make_async_copy(ids_hbm, ids, sems.at[1]),
-        pltpu.make_async_copy(tables_hbm, tables, sems.at[2]),
-    ]
-    for copy in copies:
-        copy.start()
-    copies[0].wait()
-    me = lax.axis_index("table")
-    lane = lax.broadcasted_iota(jnp.int32, (1, meta.shape[1]), 1)
-    spot = lane
-    for k in range(owners):
-        inside = (lane >= k * slots) & (lane < (k + 1) * slots)
-        spot = jnp.where(inside, lane + ((me ^ k) - k) * slots, spot)
-    table_at = jnp.full_like(lane, -1)
-    place_of = jnp.zeros_like(lane)
-    for table in range(slot_ref.shape[0]):
-        slot = slot_ref[table]
-        hit = (spot == slot) & (lane < owners * slots)
-        table_at = jnp.where(hit, table, table_at)
-        owner = slot // slots
-        place_of = jnp.where(lane == table, slot + ((owner ^ me) - owner) * slots, place_of)
-    meta[0:1, :] = table_at
-    meta[1:2, :] = place_of
-    for copy in copies[1:]:
-        copy.wait()
+def cover_kernel(out):
+    out[...] = jnp.zeros_like(out)
 
 
 def find(columns, tables, masks, span, pad, outs, batch):
@@ -80,20 +55,39 @@
 
 
 def far_first_kernel(span, owners, slots, pad, *refs):
-    meta = refs[0]
-    ids = refs[1 : 1 + owners]
-    tables, shard, lines = refs[1 + owners : 4 + owners]
-    outs = refs[4 + owners :]
+    slot_ref = refs[0]
+    ids = refs[2 : 2 + owners]
+    tables, lines, meta = refs[2 + owners : 5 + owners]
+    outs, spots = refs[5 + owners : -1], refs[-1]
     batch = ids[0].shape[1]
-    height = shard.shape[0]
     for slot in range(slots):
-        table = meta[0, slot]
+        spots[slot] = -1
+    me = lax.axis_index("table")
+    lane = lax.broadcasted_iota(jnp.int32, (1, meta.shape[1]), 1)
+    table_at = jnp.full_like(lane, -1)
+    place_of = jnp.zeros_like(lane)
+    for table in range(slot_ref.shape[0]):
+        slot = slot_ref[table]
+        owner = slot // slots
+        place = slot + ((owner ^ me) - owner) * slots
+        spots[jnp.minimum(place, slots)] = table
+        table_at = jnp.where(lane == place, table, table_at)
+        place_of = jnp.where(lane == table, place, place_of)
+    meta[0:1, :] = table_at
+    meta[1:2, :] = place_of
+    for slot in range(slots):
+        table = spots[slot]
         for k in range(owners):
             line = ids[k][pl.ds(jnp.maximum(table, 0), 1), :]
             lines[k * pad + slot : k * pad + slot + 1, :] = jnp.where(table >= 0, line, -1)
     find(lines[...].T, tables, range(NEAR, owners), span, pad, outs, batch)
-    for out in outs:
-        out[span[1] * batch : span[1] * batch + height, :] = shard[...]
+
+
+def tail_kernel(*refs):
+    count = len(refs) // 2
+    for out in refs[count + 1 :]:
+        height = refs[0].shape[0]
+        out[out.shape[0] - height :, :] = refs[0][...]
 
 
 def far_kernel(span, owners, pad, lines, tables, again, *outs):
@@ -325,13 +319,14 @@
     assert owners & (owners - 1) == 0 and owners > NEAR
     far_count = owners - NEAR
 
-    def call(kernel, shapes, operands, specs=None, *, mib, scratch=(), flops=4e9):
+    def call(kernel, shapes, operands, specs=None, *, mib, scratch=(), aliases=None, flops=4e9):
         return pl.pallas_call(
             kernel,
             out_shape=shapes,
-            in_specs=specs or [VMEM] * len(operands),
+            in_specs=[VMEM] * len(operands) if specs is None else specs,
             out_specs=[VMEM] * len(shapes),
             scratch_shapes=list(scratch),
+            input_output_aliases=aliases or {},
             compiler_params=pltpu.CompilerParams(vmem_limit_bytes=mib << 20),
             cost_estimate=pl.CostEstimate(flops=int(flops), transcendentals=0, bytes_accessed=1 << 20),
         )(*operands)
@@ -341,9 +336,6 @@
 
     def far_swap(arrays):
         return [swap(array, k) for k, array in enumerate(arrays, NEAR)]
-
-    def in_hbm(array):
-        return pltpu.with_memory_space_constraint(array, pltpu.HBM)
 
     def shape(*dims, dtype=BF16):
         return jax.ShapeDtypeStruct(dims, dtype)
@@ -360,23 +352,25 @@
             for t in range(owners)
         ],
     )
-    tables, ids, meta = call(
-        functools.partial(load_kernel, owners, slots),
-        [shape(*cold_tables.shape), shape(*ids.shape, dtype=jnp.int32), shape(8, 128, dtype=jnp.int32)],
-        [in_hbm(table_slot), in_hbm(cold_tables), in_hbm(ids)],
-        [HBM] * 3,
-        scratch=[pltpu.SMEM(table_slot.shape, jnp.int32), pltpu.SemaphoreType.DMA((3,))],
-        mib=1,
-        flops=1e9,
-    )
-    lines, *sends = call(
+    (cover,) = call(cover_kernel, [shape(8, 128, dtype=jnp.int32)], [], mib=1)
+    tables = cold_tables
+    lines, meta, *sends = call(
         functools.partial(far_first_kernel, row_spans[0], owners, slots, pad),
-        [shape(owners * pad, batch, dtype=jnp.int32)]
+        [shape(owners * pad, batch, dtype=jnp.int32), shape(8, 128, dtype=jnp.int32)]
         + [shape(row_spans[0][1] * batch + height, width)] * far_count,
-        [meta, ids, near_ids, *far_ids, tables, shard],
+        [table_slot, cover, ids, near_ids, *far_ids, tables],
         [SMEM] + [VMEM] * (owners + 2),
+        scratch=[pltpu.SMEM((slots + 1,), jnp.int32)],
         mib=4,
         flops=1e9,
+    )
+    sends = call(
+        tail_kernel,
+        [shape(*array.shape) for array in sends],
+        [shard, *sends],
+        aliases={1 + i: i for i in range(far_count)},
+        mib=1,
+        flops=1e8,
     )
     far = [far_swap(sends)]
     again, *sends = call(

time: 40.2 us -> 39.1 us (0.973)
  Pallas kernels: 15.3 us -> 14.3 us
    pallas_call x12 -> x13, Pallas kernels: 12.6 us -> 11.5 us  [call(): pl.pallas_call(kernel, out_shape=shapes, in_specs=[VMEM] * len(operands)...]
  transfers between devices with their start and end apart: 15 -> 15, of which waited for: 4 -> 4; matrix products, arithmetic and copies ran while one was open for 0% -> 0% of each run, Pallas kernels for 25% -> 26%
where the time goes in v3:
time: 39.1 us; the launch traced here: 38.9 us
  starting transfers between devices  17.8 us (46%)
  Pallas kernels  14.3 us (37%)
  waiting for transfers between devices  5.98 us (15%)
  between operations  0.91 us (2%)
    ppermute x13, starting transfers between devices, swap(): return lax.ppermute(array, 'table', [(i, i ^ k) for i in range(owners)])  12.3 us
    pallas_call x13, Pallas kernels, call(): pl.pallas_call(kernel, out_shape=shapes, in_specs=[VMEM] * len(operands)...  11.5 us
    ppermute x13, waiting for transfers between devices, swap(): return lax.ppermute(array, 'table', [(i, i ^ k) for i in range(owners)])  5.92 us
    ppermute x1, starting transfers between devices, on_device(): lax.ppermute(hot_slab, ('blk', 'table'), [(peer(b, t, blocks) * owners +...  3.11 us
    ppermute x1, starting transfers between devices, on_device(): shards.append(lax.ppermute(group, 'blk', pairs))  2.37 us
    pallas_call x1, Pallas kernels, on_device(): pl.pallas_call(functools.partial(scatter_kernel, grad_spans[0], later, ow...  1.52 us
    pallas_call x1, Pallas kernels, on_device(): pl.pallas_call(functools.partial(last_kernel, later, owners, pad), out_sh...  1.2 us
  transfers between devices with their start and end apart: 15, of which 4 were waited for; matrix products, arithmetic and copies ran while one was open for 0% of the time, Pallas kernels for 26%

profile of v3, /device:TPU:1, one launch (start us, length us, event | category | flops | bytes accessed | tf_op | source)
XLA Modules:
  0.0 38.9 jit_solution(6284969977528037143)
XLA Ops:
  0.7 2.7 %collective-permute-start.2 = (s32[26,128]{1,0:T(8,128)}, s32[26,128]{1,0:T(8,128)S(1)}, u32[]{:S(2)}, u32[]{:S(2)}) collective-permute-start(s32[26,128]{1,0:T(8,128)} %bitcast.3), channel_id=1, source_target_pairs={{0,3},{1,2},{2,1},{3,0},{4,7},{5,6},{6,5},{7,4},{8,11},{9,10},{10,... | collective-permute-start | bytes 39944 | tf_op jit(solution)/shard_map/ppermute | solution.py:335
  3.3 0.0 collective-permute-start.1
  3.3 0.5 %collective-permute-start = (s32[26,128]{1,0:T(8,128)}, s32[26,128]{1,0:T(8,128)S(1)}, u32[]{:S(2)}, u32[]{:S(2)}) collective-permute-start(s32[26,128]{1,0:T(8,128)} %bitcast.5), channel_id=1, source_target_pairs={{0,1},{1,0},{2,3},{3,2},{4,5},{5,4},{6,7},{7,6},{8,9},{9,8},{10,11... | collective-permute-start | bytes 39944 | tf_op jit(solution)/shard_map/ppermute | solution.py:335
  3.8 3.1 %collective-permute-start.3 = (bf16[16,128]{1,0:T(8,128)(2,1)}, bf16[16,128]{1,0:T(8,128)(2,1)S(1)}, u32[]{:S(2)}, u32[]{:S(2)}) collective-permute-start(bf16[16,128]{1,0:T(8,128)(2,1)} %param.10), channel_id=1, source_target_pairs={{0,0},{5,1},{10,2},{15,3},{4,4},{1,5},{14,6},{11,7},{8,8},{13,9},{... | collective-permute-start | bytes 12296 | tf_op jit(solution)/shard_map/ppermute | solution.py:346
  7.0 0.0 copy-start
  7.0 0.0 copy-start.1
  7.0 0.0 copy-start.6
  7.0 0.0 collective-permute-done.2.refs_5_
  7.0 0.0 collective-permute-done.1.refs_4_
  7.0 0.0 collective-permute-done.refs_3_
  7.1 1.3 %shard_map.114 = (s32[32,128]{1,0:T(8,128)S(1)}, s32[8,128]{1,0:T(8,128)S(1)}, bf16[400,128]{1,0:T(8,128)(2,1)S(1)}, bf16[400,128]{1,0:T(8,128)(2,1)S(1)}) custom-call(s32[26]{0:T(128)S(1)} %copy-done.8, s32[8,128]{1,0:T(8,128)S(1)} %shard_map.113.refs_1_, s32[26,128]{1,0:T(8,128)S(1)} %bitcast.6, s32[26,128]{1,0:T(8,128)S(1)} %collective-permute-done.refs_3_, ...), custom_call_target="tpu_custom_call" | custom-call | flops 1000000000 | bytes 1048576 | tf_op jit(solution)/shard_map/pallas_call | solution.py:323
  8.3 0.1 collective-permute-done.3.shard.refs_0_
  8.4 2.2 %collective-permute-start.5 = (bf16[400,128]{1,0:T(8,128)(2,1)S(1)}, bf16[400,128]{1,0:T(8,128)(2,1)S(1)}, u32[]{:S(2)}, u32[]{:S(2)}) collective-permute-start(bf16[400,128]{1,0:T(8,128)(2,1)S(1)} %get-tuple-element.37), channel_id=1, source_target_pairs={{0,2},{1,3},{2,0},{3,1},{4,6},{5,7},{6,4},{7,5},{8,10},{9,11},{10,... | collective-permute-start | bytes 307208 | tf_op jit(solution)/shard_map/ppermute | solution.py:335
  10.5 0.4 %collective-permute-start.6 = (bf16[400,128]{1,0:T(8,128)(2,1)S(1)}, bf16[400,128]{1,0:T(8,128)(2,1)S(1)}, u32[]{:S(2)}, u32[]{:S(2)}) collective-permute-start(bf16[400,128]{1,0:T(8,128)(2,1)S(1)} %get-tuple-element.38), channel_id=1, source_target_pairs={{0,3},{1,2},{2,1},{3,0},{4,7},{5,6},{6,5},{7,4},{8,11},{9,10},{10,... | collective-permute-start | bytes 307208 | tf_op jit(solution)/shard_map/ppermute | solution.py:335
  10.9 0.6 %shard_map.115 = (s32[8,128]{1,0:T(8,128)S(1)}, bf16[512,128]{1,0:T(8,128)(2,1)S(1)}, bf16[512,128]{1,0:T(8,128)(2,1)S(1)}) custom-call(s32[32,128]{1,0:T(8,128)S(1)} %get-tuple-element.32.lines.refs_1_.refs_0_, bf16[7,512,128]{2,1,0:T(8,128)(2,1)S(1)} %copy-done.2), custom_call_target="tpu_custom_call" | custom-call | flops 500000000 | bytes 1048576 | tf_op jit(solution)/shard_map/pallas_call | solution.py:323
  11.5 1.8 %collective-permute-start.7 = (bf16[512,128]{1,0:T(8,128)(2,1)S(1)}, bf16[512,128]{1,0:T(8,128)(2,1)S(1)}, u32[]{:S(2)}, u32[]{:S(2)}) collective-permute-start(bf16[512,128]{1,0:T(8,128)(2,1)S(1)} %get-tuple-element.39), channel_id=1, source_target_pairs={{0,2},{1,3},{2,0},{3,1},{4,6},{5,7},{6,4},{7,5},{8,10},{9,11},{10,... | collective-permute-start | bytes 393224 | tf_op jit(solution)/shard_map/ppermute | solution.py:335
  13.3 0.3 collective-permute-start.8
  13.6 0.5 %shard_map.116.refs_2_ = bf16[912,128]{1,0:T(8,128)(2,1)S(1)} custom-call(s32[32,128]{1,0:T(8,128)S(1)} %get-tuple-element.32.lines.refs_1_.refs_0_, s32[8,128]{1,0:T(8,128)S(1)} %get-tuple-element.33._, bf16[7,512,128]{2,1,0:T(8,128)(2,1)S(1)} %copy-done.2, bf16[16,128]{1,0:T(8,128)(2,1)S(1)} %collective-permute-done.3.shard.refs_0_), custom_call_target="tpu_custom_call" | custom-call | flops 500000000 | bytes 1048576 | tf_op jit(solution)/shard_map/pallas_call | solution.py:323
  14.1 0.3 collective-permute-start.4
  14.4 0.0 copy-done.6
  14.4 2.1 %shard_map.117 = (bf16[896,128]{1,0:T(8,128)(2,1)S(1)}, bf16[3712,512]{1,0:T(8,128)(2,1)S(1)}, bf16[512,3712]{1,0:T(8,128)(2,1)S(1)}, bf16[128,3712]{1,0:T(8,128)(2,1)S(1)}, f32[32,128]{1,0:T(8,128)S(1)}) custom-call(s32[8,128]{1,0:T(8,128)S(1)} %get-tuple-element.31.refs_0_, s32[32,128]{1,0:T(8,128)S(1)} %get-tuple-element.32.lines.refs_1_.refs_0_, ...), custom_call_target="tpu_custom_call" | custom-call | flops 4000000000 | bytes 1048576 | tf_op jit(solution)/shard_map/pallas_call | solution.py:323
  16.5 0.0 collective-permute-done.5.refs_2_.refs_0_.refs_3_
  16.5 0.0 collective-permute-done.6.refs_3_.refs_1_.refs_4_
  16.5 0.0 collective-permute-done.4.refs_1_.refs_2_
  16.5 2.4 %collective-permute-start.9 = (bf16[64,128]{1,0:T(8,128)(2,1)S(1)}, bf16[64,128]{1,0:T(8,128)(2,1)S(1)}, u32[]{:S(2)}, u32[]{:S(2)}) collective-permute-start(bf16[64,128]{1,0:T(8,128)(2,1)S(1)} %shard_map.119.refs_2_), channel_id=1, source_target_pairs={{16,0},{20,4},{24,8},{28,12},{0,16},{4,20},{8,24},{12,28},{17,1},{... | collective-permute-start | bytes 49160 | tf_op jit(solution)/shard_map/ppermute | solution.py:418
  18.9 1.0 %shard_map.120 = (f32[128,512]{1,0:T(8,128)S(1)}, f32[128,512]{1,0:T(8,128)S(1)}) custom-call(bf16[896,128]{1,0:T(8,128)(2,1)S(1)} %get-tuple-element.34.refs_0_.refs_1_, bf16[912,128]{1,0:T(8,128)(2,1)S(1)} %collective-permute-done.4.refs_1_.refs_2_, bf16[3712,512]{1,0:T(8,128)(2,1)S(1)} %get-tuple-element.41.refs_2_.refs_8_.down, ...), custom_call_target="tpu_custom_call" | custom-call | flops 4000000000 | bytes 1048576 | tf_op jit(solution)/shard_map/pallas_call | solution.py:323
  19.9 0.0 copy-start.4
  19.9 0.0 copy-start.7
  19.9 0.5 %shard_map.121 = (f32[128,512]{1,0:T(8,128)S(1)}, f32[128,512]{1,0:T(8,128)S(1)}) custom-call(bf16[400,128]{1,0:T(8,128)(2,1)S(1)} %collective-permute-done.5.refs_2_.refs_0_.refs_3_, bf16[400,128]{1,0:T(8,128)(2,1)S(1)} %collective-permute-done.6.refs_3_.refs_1_.refs_4_, bf16[3712,512]{1,0:T(8,128)(2,1)S(1)} %get-tuple-element.41.refs_2_.refs_8_.down, ...), custom_call_target="tpu_custom_call" | custom-call | flops 4000000000 | bytes 1048576 | tf_op jit(solution)/shard_map/pallas_call | solution.py:323
  20.5 0.0 collective-permute-done.7.refs_0_.refs_5_
  20.5 1.2 %collective-permute-done.8.refs_1_.refs_6_ = bf16[512,128]{1,0:T(8,128)(2,1)S(1)} collective-permute-done((bf16[512,128]{1,0:T(8,128)(2,1)S(1)}, bf16[512,128]{1,0:T(8,128)(2,1)S(1)}, u32[]{:S(2)}, u32[]{:S(2)}) %collective-permute-start.8) | collective-permute-done | bytes 131104 | tf_op jit(solution)/shard_map/ppermute | solution.py:335
  21.7 0.0 collective-permute-done.9.refs_3_
  21.7 1.5 %shard_map.122 = (bf16[128,128]{1,0:T(8,128)(2,1)S(1)}, bf16[128,512]{1,0:T(8,128)(2,1)S(1)}, bf16[128,512]{1,0:T(8,128)(2,1)S(1)}, bf16[512,128]{1,0:T(8,128)(2,1)S(1)}, bf16[512,128]{1,0:T(8,128)(2,1)S(1)}) custom-call(bf16[512,128]{1,0:T(8,128)(2,1)S(1)} %collective-permute-done.7.refs_0_.refs_5_, ...), custom_call_target="tpu_custom_call" | custom-call | flops 4000000000 | bytes 1048576 | tf_op jit(solution)/shard_map/pallas_call | solution.py:323
  23.2 0.5 %shard_map.123 = (bf16[384,128]{1,0:T(8,128)(2,1)S(1)}, bf16[384,128]{1,0:T(8,128)(2,1)S(1)}) custom-call(bf16[128,512]{1,0:T(8,128)(2,1)S(1)} %get-tuple-element.50.low.refs_8_, bf16[128,512]{1,0:T(8,128)(2,1)S(1)} %get-tuple-element.51.grad, bf16[3712,512]{1,0:T(8,128)(2,1)S(1)} %get-tuple-element.41.refs_2_.refs_8_.down, ...), custom_call_target="tpu_custom_call" | custom-call | flops 4000000000 | bytes 1048576 | tf_op jit(solution)/shard_map/pallas_call | solution.py:323
  23.8 1.0 %shard_map.124 = (bf16[896,128]{1,0:T(8,128)(2,1)S(1)}, bf16[896,128]{1,0:T(8,128)(2,1)S(1)}) custom-call(bf16[128,512]{1,0:T(8,128)(2,1)S(1)} %get-tuple-element.50.low.refs_8_, bf16[128,512]{1,0:T(8,128)(2,1)S(1)} %get-tuple-element.51.grad, bf16[3712,512]{1,0:T(8,128)(2,1)S(1)} %get-tuple-element.41.refs_2_.refs_8_.down, ...), custom_call_target="tpu_custom_call" | custom-call | flops 4000000000 | bytes 1048576 | tf_op jit(solution)/shard_map/pallas_call | solution.py:323
  24.8 1.3 %collective-permute-start.13 = (bf16[384,128]{1,0:T(8,128)(2,1)S(1)}, bf16[384,128]{1,0:T(8,128)(2,1)S(1)}, u32[]{:S(2)}, u32[]{:S(2)}) collective-permute-start(bf16[384,128]{1,0:T(8,128)(2,1)S(1)} %get-tuple-element.52._), channel_id=1, source_target_pairs={{0,2},{1,3},{2,0},{3,1},{4,6},{5,7},{6,4},{7,5},{8,10},{9,11},{10,... | collective-permute-start | bytes 294920 | tf_op jit(solution)/shard_map/ppermute | solution.py:335
  26.1 0.2 collective-permute-start.11
  26.4 1.4 %collective-permute-start.12 = (bf16[512,128]{1,0:T(8,128)(2,1)S(1)}, bf16[512,128]{1,0:T(8,128)(2,1)S(1)}, u32[]{:S(2)}, u32[]{:S(2)}) collective-permute-start(bf16[512,128]{1,0:T(8,128)(2,1)S(1)} %get-tuple-element.56), channel_id=1, source_target_pairs={{0,3},{1,2},{2,1},{3,0},{4,7},{5,6},{6,5},{7,4},{8,11},{9,10},{10,... | collective-permute-start | bytes 393224 | tf_op jit(solution)/shard_map/ppermute | solution.py:335
  27.8 0.3 collective-permute-start.14
  28.1 1.0 %collective-permute-start.10 = (bf16[896,128]{1,0:T(8,128)(2,1)S(1)}, bf16[896,128]{1,0:T(8,128)(2,1)S(1)}, u32[]{:S(2)}, u32[]{:S(2)}) collective-permute-start(bf16[896,128]{1,0:T(8,128)(2,1)S(1)} %get-tuple-element.54), channel_id=1, source_target_pairs={{0,1},{1,0},{2,3},{3,2},{4,5},{5,4},{6,7},{7,6},{8,9},{9,8},{10,11... | collective-permute-start | bytes 688136 | tf_op jit(solution)/shard_map/ppermute | solution.py:335
  29.1 2.4 %shard_map.125 = bf16[128,3456]{1,0:T(8,128)(2,1)} custom-call(s32[8,128]{1,0:T(8,128)S(1)} %get-tuple-element.31.refs_0_, bf16[896,128]{1,0:T(8,128)(2,1)S(1)} %get-tuple-element.34.refs_0_.refs_1_, bf16[912,128]{1,0:T(8,128)(2,1)S(1)} %collective-permute-done.4.refs_1_.refs_2_, bf16[400,128]{1,0:T(8,128)(2,1)S(1)} %collective-permute-done.5.refs_2_.refs_0_.refs_3_, ...), custom_call_target="tpu_custom_call" | custom-call | flops 4000000000 | bytes 1048576 | tf_op jit(solution)/shard_map/pallas_call | solution.py:323
  31.5 0.2 collective-permute-done.11.refs_3_
  31.7 4.5 %collective-permute-done.12.refs_4_ = bf16[512,128]{1,0:T(8,128)(2,1)S(1)} collective-permute-done((bf16[512,128]{1,0:T(8,128)(2,1)S(1)}, bf16[512,128]{1,0:T(8,128)(2,1)S(1)}, u32[]{:S(2)}, u32[]{:S(2)}) %collective-permute-start.12) | collective-permute-done | bytes 131104 | tf_op jit(solution)/shard_map/ppermute | solution.py:335
  36.2 0.0 collective-permute-done.10.refs_2_
  36.2 1.5 %scatter.1 = (f32[1,7,512,128]{3,2,1,0:T(8,128)}, f32[3,512,128]{2,1,0:T(8,128)S(1)}) custom-call(s32[32,128]{1,0:T(8,128)S(1)} %get-tuple-element.32.lines.refs_1_.refs_0_, bf16[896,128]{1,0:T(8,128)(2,1)S(1)} %get-tuple-element.53.refs_11_.refs_1_, bf16[896,128]{1,0:T(8,128)(2,1)S(1)} %collective-permute-done.10.refs_2_, ...), custom_call_target="tpu_custom_call" | custom-call | tf_op jit(solution)/shard_map/scatter/pallas_call | solution.py:467
  37.7 0.0 collective-permute-done.14.refs_3_
  37.7 0.0 collective-permute-done.13.refs_2_
  37.7 1.2 %last.1 = f32[1,7,512,128]{3,2,1,0:T(8,128)} custom-call(s32[32,128]{1,0:T(8,128)S(1)} %get-tuple-element.32.lines.refs_1_.refs_0_, f32[3,512,128]{2,1,0:T(8,128)S(1)} %get-tuple-element.57.refs_1_, bf16[384,128]{1,0:T(8,128)(2,1)S(1)} %collective-permute-done.13.refs_2_, ...), custom_call_target="tpu_custom_call", output_to_operand_aliasing={{}: (4, {})} | custom-call | tf_op jit(solution)/shard_map/last/pallas_call | solution.py:479
  (15 shorter events, 0.0 us)
Async XLA Ops:
  0.6 6.4 %copy-start.2 = (bf16[7,512,128]{2,1,0:T(8,128)(2,1)S(1)}, bf16[7,512,128]{2,1,0:T(8,128)(2,1)}, u32[]{:S(2)}) copy-start(bf16[7,512,128]{2,1,0:T(8,128)(2,1)} %refs_3_.1) | copy-start | bytes 2752516
  0.6 6.4 %copy-start.5 = (s32[128,26]{0,1:T(8,128)S(1)}, s32[128,26]{0,1:T(8,128)}, u32[]{:S(2)}) copy-start(s32[128,26]{0,1:T(8,128)} %param.13) | copy-start | bytes 39940
  0.7 6.4 %copy-start.8 = (s32[26]{0:T(128)S(1)}, s32[26]{0:T(128)}, u32[]{:S(2)}) copy-start(s32[26]{0:T(128)} %refs_0_.1) | copy-start | bytes 316
  0.7 6.3 %collective-permute-start.2 = (s32[26,128]{1,0:T(8,128)}, s32[26,128]{1,0:T(8,128)S(1)}, u32[]{:S(2)}, u32[]{:S(2)}) collective-permute-start(s32[26,128]{1,0:T(8,128)} %bitcast.3), channel_id=1, source_target_pairs={{0,3},{1,2},{2,1},{3,0},{4,7},{5,6},{6,5},{7,4},{8,11},{9,10},{10,... | collective-permute-start | bytes 39944 | tf_op jit(solution)/shard_map/ppermute | solution.py:335
  3.3 3.7 %collective-permute-start.1 = (s32[26,128]{1,0:T(8,128)}, s32[26,128]{1,0:T(8,128)S(1)}, u32[]{:S(2)}, u32[]{:S(2)}) collective-permute-start(s32[26,128]{1,0:T(8,128)} %bitcast.4), channel_id=1, source_target_pairs={{0,2},{1,3},{2,0},{3,1},{4,6},{5,7},{6,4},{7,5},{8,10},{9,11},{10,... | collective-permute-start | bytes 39944 | tf_op jit(solution)/shard_map/ppermute | solution.py:335
  3.3 3.7 %collective-permute-start = (s32[26,128]{1,0:T(8,128)}, s32[26,128]{1,0:T(8,128)S(1)}, u32[]{:S(2)}, u32[]{:S(2)}) collective-permute-start(s32[26,128]{1,0:T(8,128)} %bitcast.5), channel_id=1, source_target_pairs={{0,1},{1,0},{2,3},{3,2},{4,5},{5,4},{6,7},{7,6},{8,9},{9,8},{10,11... | collective-permute-start | bytes 39944 | tf_op jit(solution)/shard_map/ppermute | solution.py:335
  3.8 4.5 %collective-permute-start.3 = (bf16[16,128]{1,0:T(8,128)(2,1)}, bf16[16,128]{1,0:T(8,128)(2,1)S(1)}, u32[]{:S(2)}, u32[]{:S(2)}) collective-permute-start(bf16[16,128]{1,0:T(8,128)(2,1)} %param.10), channel_id=1, source_target_pairs={{0,0},{5,1},{10,2},{15,3},{4,4},{1,5},{14,6},{11,7},{8,8},{13,9},{... | collective-permute-start | bytes 12296 | tf_op jit(solution)/shard_map/ppermute | solution.py:346
  6.9 7.4 %copy-start.3 = (bf16[128,3456]{1,0:T(8,128)(2,1)S(1)}, bf16[128,3456]{1,0:T(8,128)(2,1)}, u32[]{:S(2)}) copy-start(bf16[128,3456]{1,0:T(8,128)(2,1)} %refs_6_.3) | copy-start | bytes 2654212
  7.0 7.4 %copy-start = (bf16[3456,512]{1,0:T(8,128)(2,1)S(1)}, bf16[3456,512]{1,0:T(8,128)(2,1)}, u32[]{:S(2)}) copy-start(bf16[3456,512]{1,0:T(8,128)(2,1)} %refs_4_.1) | copy-start | bytes 10616836
  7.0 7.4 %copy-start.1 = (bf16[512,3456]{1,0:T(8,128)(2,1)S(1)}, bf16[512,3456]{1,0:T(8,128)(2,1)}, u32[]{:S(2)}) copy-start(bf16[512,3456]{1,0:T(8,128)(2,1)} %refs_5_.2) | copy-start | bytes 10616836
  7.0 7.4 %copy-start.6 = (f32[3456]{0:T(1024)S(1)}, f32[3456]{0:T(1024)}, u32[]{:S(2)}) copy-start(f32[3456]{0:T(1024)} %param.18) | copy-start | bytes 41476
  8.4 8.1 %collective-permute-start.5 = (bf16[400,128]{1,0:T(8,128)(2,1)S(1)}, bf16[400,128]{1,0:T(8,128)(2,1)S(1)}, u32[]{:S(2)}, u32[]{:S(2)}) collective-permute-start(bf16[400,128]{1,0:T(8,128)(2,1)S(1)} %get-tuple-element.37), channel_id=1, source_target_pairs={{0,2},{1,3},{2,0},{3,1},{4,6},{5,7},{6,4},{7,5},{8,10},{9,11},{10,... | collective-permute-start | bytes 307208 | tf_op jit(solution)/shard_map/ppermute | solution.py:335
  10.5 5.9 %collective-permute-start.6 = (bf16[400,128]{1,0:T(8,128)(2,1)S(1)}, bf16[400,128]{1,0:T(8,128)(2,1)S(1)}, u32[]{:S(2)}, u32[]{:S(2)}) collective-permute-start(bf16[400,128]{1,0:T(8,128)(2,1)S(1)} %get-tuple-element.38), channel_id=1, source_target_pairs={{0,3},{1,2},{2,1},{3,0},{4,7},{5,6},{6,5},{7,4},{8,11},{9,10},{10,... | collective-permute-start | bytes 307208 | tf_op jit(solution)/shard_map/ppermute | solution.py:335
  11.5 9.0 %collective-permute-start.7 = (bf16[512,128]{1,0:T(8,128)(2,1)S(1)}, bf16[512,128]{1,0:T(8,128)(2,1)S(1)}, u32[]{:S(2)}, u32[]{:S(2)}) collective-permute-start(bf16[512,128]{1,0:T(8,128)(2,1)S(1)} %get-tuple-element.39), channel_id=1, source_target_pairs={{0,2},{1,3},{2,0},{3,1},{4,6},{5,7},{6,4},{7,5},{8,10},{9,11},{10,... | collective-permute-start | bytes 393224 | tf_op jit(solution)/shard_map/ppermute | solution.py:335
  13.3 8.4 %collective-permute-start.8 = (bf16[512,128]{1,0:T(8,128)(2,1)S(1)}, bf16[512,128]{1,0:T(8,128)(2,1)S(1)}, u32[]{:S(2)}, u32[]{:S(2)}) collective-permute-start(bf16[512,128]{1,0:T(8,128)(2,1)S(1)} %get-tuple-element.40), channel_id=1, source_target_pairs={{0,3},{1,2},{2,1},{3,0},{4,7},{5,6},{6,5},{7,4},{8,11},{9,10},{10,... | collective-permute-start | bytes 393224 | tf_op jit(solution)/shard_map/ppermute | solution.py:335
  14.1 2.4 %collective-permute-start.4 = (bf16[912,128]{1,0:T(8,128)(2,1)S(1)}, bf16[912,128]{1,0:T(8,128)(2,1)S(1)}, u32[]{:S(2)}, u32[]{:S(2)}) collective-permute-start(bf16[912,128]{1,0:T(8,128)(2,1)S(1)} %shard_map.116.refs_2_), channel_id=1, source_target_pairs={{0,1},{1,0},{2,3},{3,2},{4,5},{5,4},{6,7},{7,6},{8,9},{9,8},{10,11... | collective-permute-start | bytes 700424 | tf_op jit(solution)/shard_map/ppermute | solution.py:335
  16.5 5.2 %collective-permute-start.9 = (bf16[64,128]{1,0:T(8,128)(2,1)S(1)}, bf16[64,128]{1,0:T(8,128)(2,1)S(1)}, u32[]{:S(2)}, u32[]{:S(2)}) collective-permute-start(bf16[64,128]{1,0:T(8,128)(2,1)S(1)} %shard_map.119.refs_2_), channel_id=1, source_target_pairs={{16,0},{20,4},{24,8},{28,12},{0,16},{4,20},{8,24},{12,28},{17,1},{... | collective-permute-start | bytes 49160 | tf_op jit(solution)/shard_map/ppermute | solution.py:418
  19.9 1.8 %copy-start.4 = (bf16[128,128]{1,0:T(8,128)(2,1)S(1)}, bf16[128,128]{1,0:T(8,128)(2,1)}, u32[]{:S(2)}) copy-start(bf16[128,128]{1,0:T(8,128)(2,1)} %refs_5_.3) | copy-start | bytes 98308
  19.9 1.8 %copy-start.7 = (s32[128,16]{0,1:T(8,128)S(1)}, s32[128,16]{0,1:T(8,128)}, u32[]{:S(2)}) copy-start(s32[128,16]{0,1:T(8,128)} %param.11) | copy-start | bytes 24580
  24.8 12.9 %collective-permute-start.13 = (bf16[384,128]{1,0:T(8,128)(2,1)S(1)}, bf16[384,128]{1,0:T(8,128)(2,1)S(1)}, u32[]{:S(2)}, u32[]{:S(2)}) collective-permute-start(bf16[384,128]{1,0:T(8,128)(2,1)S(1)} %get-tuple-element.52._), channel_id=1, source_target_pairs={{0,2},{1,3},{2,0},{3,1},{4,6},{5,7},{6,4},{7,5},{8,10},{9,11},{10,... | collective-permute-start | bytes 294920 | tf_op jit(solution)/shard_map/ppermute | solution.py:335
  26.1 5.5 %collective-permute-start.11 = (bf16[512,128]{1,0:T(8,128)(2,1)S(1)}, bf16[512,128]{1,0:T(8,128)(2,1)S(1)}, u32[]{:S(2)}, u32[]{:S(2)}) collective-permute-start(bf16[512,128]{1,0:T(8,128)(2,1)S(1)} %get-tuple-element.55), channel_id=1, source_target_pairs={{0,2},{1,3},{2,0},{3,1},{4,6},{5,7},{6,4},{7,5},{8,10},{9,11},{10,... | collective-permute-start | bytes 393224 | tf_op jit(solution)/shard_map/ppermute | solution.py:335
  26.4 9.8 %collective-permute-start.12 = (bf16[512,128]{1,0:T(8,128)(2,1)S(1)}, bf16[512,128]{1,0:T(8,128)(2,1)S(1)}, u32[]{:S(2)}, u32[]{:S(2)}) collective-permute-start(bf16[512,128]{1,0:T(8,128)(2,1)S(1)} %get-tuple-element.56), channel_id=1, source_target_pairs={{0,3},{1,2},{2,1},{3,0},{4,7},{5,6},{6,5},{7,4},{8,11},{9,10},{10,... | collective-permute-start | bytes 393224 | tf_op jit(solution)/shard_map/ppermute | solution.py:335
  27.8 9.9 %collective-permute-start.14 = (bf16[384,128]{1,0:T(8,128)(2,1)S(1)}, bf16[384,128]{1,0:T(8,128)(2,1)S(1)}, u32[]{:S(2)}, u32[]{:S(2)}) collective-permute-start(bf16[384,128]{1,0:T(8,128)(2,1)S(1)} %get-tuple-element.58), channel_id=1, source_target_pairs={{0,3},{1,2},{2,1},{3,0},{4,7},{5,6},{6,5},{7,4},{8,11},{9,10},{10,... | collective-permute-start | bytes 294920 | tf_op jit(solution)/shard_map/ppermute | solution.py:335
  28.1 8.1 %collective-permute-start.10 = (bf16[896,128]{1,0:T(8,128)(2,1)S(1)}, bf16[896,128]{1,0:T(8,128)(2,1)S(1)}, u32[]{:S(2)}, u32[]{:S(2)}) collective-permute-start(bf16[896,128]{1,0:T(8,128)(2,1)S(1)} %get-tuple-element.54), channel_id=1, source_target_pairs={{0,1},{1,0},{2,3},{3,2},{4,5},{5,4},{6,7},{7,6},{8,9},{9,8},{10,11... | collective-permute-start | bytes 688136 | tf_op jit(solution)/shard_map/ppermute | solution.py:335

commit v4 on v3

--- a/solution.py
+++ b/solution.py
@@ -164,35 +164,46 @@
     grad_out[...] = grad
 
 
+def counts_kernel(owners, blocks, group, hot_ids, dense, counts, base):
+    batch = dense.shape[0]
+    me = lax.axis_index("table")
+    mine = lax.axis_index("blk")
+    height = group.shape[0] // owners
+    row = lax.broadcasted_iota(jnp.int32, (height, batch), 0)
+    for part in range(-(-blocks // owners)):
+        for k in range(owners):
+            mask = part * owners + (me ^ k)
+            first = jnp.where(mask < blocks, peer(mine, mask, blocks) * height, -height)
+            total = jnp.zeros((height, batch), F32)
+            for i in range(hot_ids.shape[0]):
+                total += jnp.where(hot_ids[i : i + 1, :] - first == row, 1.0, 0.0)
+            begin = (part * owners + k) * height
+            counts[begin : begin + height, :] = total.astype(BF16)
+    pooled = lax.dot_general(
+        counts[: owners * height, :],
+        group[...],
+        (((0,), (0,)), ((), ())),
+        preferred_element_type=F32,
+    )
+    base[...] = dense[...].astype(F32) + pooled
+
+
 def second_kernel(span, grad_span, owners, slots, blocks, *refs):
     far = refs[: owners - NEAR]
     refs = refs[owners - NEAR :]
     held = -(-blocks // owners)
     shards = refs[:held]
-    hot_ids, dense, low_in, grad_in, down, up, bias, cot = refs[held : 8 + held]
+    counts, base, low_in, grad_in, down, up, bias, cot = refs[held : 8 + held]
     front_out, low_out, grad_out = refs[8 + held : 11 + held]
     outs = refs[11 + held :]
-    batch, width = dense.shape
-    me = lax.axis_index("table")
-    mine = lax.axis_index("blk")
-    height = shards[0].shape[0] // owners
-    row = lax.broadcasted_iota(jnp.int32, (height, batch), 0)
-    pooled = None
-    for part in range(held):
-        counts = []
-        for k in range(owners):
-            mask = part * owners + (me ^ k)
-            base = jnp.where(mask < blocks, peer(mine, mask, blocks) * height, -height)
-            total = jnp.zeros((height, batch), F32)
-            for i in range(hot_ids.shape[0]):
-                total += jnp.where(hot_ids[i : i + 1, :] - base == row, 1.0, 0.0)
-            counts.append(total)
-        counts = jnp.concatenate(counts, axis=0).astype(BF16)
-        more = lax.dot_general(
-            counts, shards[part][...], (((0,), (0,)), ((), ())), preferred_element_type=F32
+    batch, width = base.shape
+    pooled = base[...]
+    for part in range(1, held):
+        rows = counts[part * shards[part].shape[0] : (part + 1) * shards[part].shape[0], :]
+        pooled += lax.dot_general(
+            rows, shards[part][...], (((0,), (0,)), ((), ())), preferred_element_type=F32
         )
-        pooled = more if pooled is None else pooled + more
-    front = (dense[...].astype(F32) + pooled).astype(BF16)
+    front = pooled.astype(BF16)
     front_out[...] = front
     low, grad = add_up(front, 0, down, up, cot, low_in[...], grad_in[...])
     for k, ref in enumerate(far, NEAR):
@@ -417,6 +428,15 @@
         pairs = [(peer(b, mask, blocks), b) for b in range(blocks)]
         shards.append(lax.ppermute(group, "blk", pairs))
 
+    counts, base = call(
+        functools.partial(counts_kernel, owners, blocks),
+        [
+            shape(-(-blocks // owners) * owners * height, batch),
+            shape(batch, width, dtype=F32),
+        ],
+        [group, hot_rows, dense],
+        mib=2,
+    )
     sums = [shape(batch, rank, dtype=F32)] * 2
     low, grad = call(
         functools.partial(sums_kernel, (0, slots), range(NEAR), slots),
@@ -434,7 +454,7 @@
         functools.partial(second_kernel, row_spans[1], grad_spans[0], owners, slots, blocks),
         [shape(batch, width), shape(batch, rank), shape(batch, rank)]
         + [shape(grad_spans[0][1] * batch, width)] * far_count,
-        [*far[1], *shards, hot_rows, dense, low, grad, down, up, bias, cot],
+        [*far[1], *shards, counts, base, low, grad, down, up, bias, cot],
         mib=6,
     )
     far_grads = [far_swap(sends)]

time: 39.1 us -> 39 us (level)
    pallas_call x13 -> x14, Pallas kernels: 11.5 us -> 11.7 us  [call(): pl.pallas_call(kernel, out_shape=shapes, in_specs=[VMEM] * len(operands)...]
  transfers between devices with their start and end apart: 15 -> 15, of which waited for: 4 -> 4; matrix products, arithmetic and copies ran while one was open for 0% -> 0% of each run, Pallas kernels for 26% -> 27%
where the time goes in v4:
time: 39 us; the launch traced here: 38.8 us
  starting transfers between devices  17.8 us (46%)
  Pallas kernels  14.4 us (37%)
  waiting for transfers between devices  5.64 us (14%)
  between operations  0.9 us (2%)
    ppermute x13, starting transfers between devices, swap(): return lax.ppermute(array, 'table', [(i, i ^ k) for i in range(owners)])  12.3 us
    pallas_call x14, Pallas kernels, call(): pl.pallas_call(kernel, out_shape=shapes, in_specs=[VMEM] * len(operands)...  11.7 us
    ppermute x13, waiting for transfers between devices, swap(): return lax.ppermute(array, 'table', [(i, i ^ k) for i in range(owners)])  5.59 us
    ppermute x1, starting transfers between devices, on_device(): lax.ppermute(hot_slab, ('blk', 'table'), [(peer(b, t, blocks) * owners +...  3.11 us
    ppermute x1, starting transfers between devices, on_device(): shards.append(lax.ppermute(group, 'blk', pairs))  2.37 us
    pallas_call x1, Pallas kernels, on_device(): pl.pallas_call(functools.partial(scatter_kernel, grad_spans[0], later, ow...  1.52 us
    pallas_call x1, Pallas kernels, on_device(): pl.pallas_call(functools.partial(last_kernel, later, owners, pad), out_sh...  1.2 us
  transfers between devices with their start and end apart: 15, of which 4 were waited for; matrix products, arithmetic and copies ran while one was open for 0% of the time, Pallas kernels for 27%

profile of v4, /device:TPU:1, one launch (start us, length us, event | category | flops | bytes accessed | tf_op | source)
XLA Modules:
  0.0 38.8 jit_solution(7165538662831599081)
XLA Ops:
  0.7 2.7 %collective-permute-start.2 = (s32[26,128]{1,0:T(8,128)}, s32[26,128]{1,0:T(8,128)S(1)}, u32[]{:S(2)}, u32[]{:S(2)}) collective-permute-start(s32[26,128]{1,0:T(8,128)} %bitcast.3), channel_id=1, source_target_pairs={{0,3},{1,2},{2,1},{3,0},{4,7},{5,6},{6,5},{7,4},{8,11},{9,10},{10,... | collective-permute-start | bytes 39944 | tf_op jit(solution)/shard_map/ppermute | solution.py:346
  3.3 0.0 collective-permute-start.1
  3.3 0.5 %collective-permute-start = (s32[26,128]{1,0:T(8,128)}, s32[26,128]{1,0:T(8,128)S(1)}, u32[]{:S(2)}, u32[]{:S(2)}) collective-permute-start(s32[26,128]{1,0:T(8,128)} %bitcast.5), channel_id=1, source_target_pairs={{0,1},{1,0},{2,3},{3,2},{4,5},{5,4},{6,7},{7,6},{8,9},{9,8},{10,11... | collective-permute-start | bytes 39944 | tf_op jit(solution)/shard_map/ppermute | solution.py:346
  3.8 3.1 %collective-permute-start.3 = (bf16[16,128]{1,0:T(8,128)(2,1)}, bf16[16,128]{1,0:T(8,128)(2,1)S(1)}, u32[]{:S(2)}, u32[]{:S(2)}) collective-permute-start(bf16[16,128]{1,0:T(8,128)(2,1)} %param.10), channel_id=1, source_target_pairs={{0,0},{5,1},{10,2},{15,3},{4,4},{1,5},{14,6},{11,7},{8,8},{13,9},{... | collective-permute-start | bytes 12296 | tf_op jit(solution)/shard_map/ppermute | solution.py:357
  7.0 0.0 copy-start
  7.0 0.0 copy-start.1
  7.0 0.0 copy-start.6
  7.0 0.0 collective-permute-done.2.refs_5_
  7.0 0.0 collective-permute-done.1.refs_4_
  7.0 0.0 collective-permute-done.refs_3_
  7.1 1.3 %shard_map.114 = (s32[32,128]{1,0:T(8,128)S(1)}, s32[8,128]{1,0:T(8,128)S(1)}, bf16[400,128]{1,0:T(8,128)(2,1)S(1)}, bf16[400,128]{1,0:T(8,128)(2,1)S(1)}) custom-call(s32[26]{0:T(128)S(1)} %copy-done.8, s32[8,128]{1,0:T(8,128)S(1)} %shard_map.113.refs_1_, s32[26,128]{1,0:T(8,128)S(1)} %bitcast.6, s32[26,128]{1,0:T(8,128)S(1)} %collective-permute-done.refs_3_, ...), custom_call_target="tpu_custom_call" | custom-call | flops 1000000000 | bytes 1048576 | tf_op jit(solution)/shard_map/pallas_call | solution.py:334
  8.3 0.1 collective-permute-done.3.shard.refs_0_
  8.4 2.2 %collective-permute-start.5 = (bf16[400,128]{1,0:T(8,128)(2,1)S(1)}, bf16[400,128]{1,0:T(8,128)(2,1)S(1)}, u32[]{:S(2)}, u32[]{:S(2)}) collective-permute-start(bf16[400,128]{1,0:T(8,128)(2,1)S(1)} %get-tuple-element.39), channel_id=1, source_target_pairs={{0,2},{1,3},{2,0},{3,1},{4,6},{5,7},{6,4},{7,5},{8,10},{9,11},{10,... | collective-permute-start | bytes 307208 | tf_op jit(solution)/shard_map/ppermute | solution.py:346
  10.5 0.4 %collective-permute-start.6 = (bf16[400,128]{1,0:T(8,128)(2,1)S(1)}, bf16[400,128]{1,0:T(8,128)(2,1)S(1)}, u32[]{:S(2)}, u32[]{:S(2)}) collective-permute-start(bf16[400,128]{1,0:T(8,128)(2,1)S(1)} %get-tuple-element.40), channel_id=1, source_target_pairs={{0,3},{1,2},{2,1},{3,0},{4,7},{5,6},{6,5},{7,4},{8,11},{9,10},{10,... | collective-permute-start | bytes 307208 | tf_op jit(solution)/shard_map/ppermute | solution.py:346
  10.9 0.6 %shard_map.115 = (s32[8,128]{1,0:T(8,128)S(1)}, bf16[512,128]{1,0:T(8,128)(2,1)S(1)}, bf16[512,128]{1,0:T(8,128)(2,1)S(1)}) custom-call(s32[32,128]{1,0:T(8,128)S(1)} %get-tuple-element.34.lines.refs_1_.refs_0_, bf16[7,512,128]{2,1,0:T(8,128)(2,1)S(1)} %copy-done.2), custom_call_target="tpu_custom_call" | custom-call | flops 500000000 | bytes 1048576 | tf_op jit(solution)/shard_map/pallas_call | solution.py:334
  11.5 1.8 %collective-permute-start.7 = (bf16[512,128]{1,0:T(8,128)(2,1)S(1)}, bf16[512,128]{1,0:T(8,128)(2,1)S(1)}, u32[]{:S(2)}, u32[]{:S(2)}) collective-permute-start(bf16[512,128]{1,0:T(8,128)(2,1)S(1)} %get-tuple-element.41), channel_id=1, source_target_pairs={{0,2},{1,3},{2,0},{3,1},{4,6},{5,7},{6,4},{7,5},{8,10},{9,11},{10,... | collective-permute-start | bytes 393224 | tf_op jit(solution)/shard_map/ppermute | solution.py:346
  13.3 0.3 collective-permute-start.8
  13.6 0.5 %shard_map.116.refs_2_ = bf16[912,128]{1,0:T(8,128)(2,1)S(1)} custom-call(s32[32,128]{1,0:T(8,128)S(1)} %get-tuple-element.34.lines.refs_1_.refs_0_, s32[8,128]{1,0:T(8,128)S(1)} %get-tuple-element.35._, bf16[7,512,128]{2,1,0:T(8,128)(2,1)S(1)} %copy-done.2, bf16[16,128]{1,0:T(8,128)(2,1)S(1)} %collective-permute-done.3.shard.refs_0_), custom_call_target="tpu_custom_call" | custom-call | flops 500000000 | bytes 1048576 | tf_op jit(solution)/shard_map/pallas_call | solution.py:334
  14.1 0.3 collective-permute-start.4
  14.4 2.1 %shard_map.117 = (bf16[896,128]{1,0:T(8,128)(2,1)S(1)}, bf16[3712,512]{1,0:T(8,128)(2,1)S(1)}, bf16[512,3712]{1,0:T(8,128)(2,1)S(1)}, bf16[128,3712]{1,0:T(8,128)(2,1)S(1)}, f32[32,128]{1,0:T(8,128)S(1)}) custom-call(s32[8,128]{1,0:T(8,128)S(1)} %get-tuple-element.33.refs_0_, s32[32,128]{1,0:T(8,128)S(1)} %get-tuple-element.34.lines.refs_1_.refs_0_, ...), custom_call_target="tpu_custom_call" | custom-call | flops 4000000000 | bytes 1048576 | tf_op jit(solution)/shard_map/pallas_call | solution.py:334
  16.5 0.0 copy-start.4
  16.5 0.0 copy-start.7
  16.5 0.0 collective-permute-done.5.refs_2_.refs_0_.refs_3_
  16.5 0.0 collective-permute-done.6.refs_3_.refs_1_.refs_4_
  16.5 0.0 collective-permute-done.4.refs_1_.refs_2_
  16.5 2.4 %collective-permute-start.9 = (bf16[64,128]{1,0:T(8,128)(2,1)S(1)}, bf16[64,128]{1,0:T(8,128)(2,1)S(1)}, u32[]{:S(2)}, u32[]{:S(2)}) collective-permute-start(bf16[64,128]{1,0:T(8,128)(2,1)S(1)} %shard_map.119.group.refs_2_), channel_id=1, source_target_pairs={{16,0},{20,4},{24,8},{28,12},{0,16},{4,20},{8,24},{12,28},{17,1},{... | collective-permute-start | bytes 49160 | tf_op jit(solution)/shard_map/ppermute | solution.py:429
  18.9 0.3 shard_map.120
  19.2 1.0 %shard_map.121 = (f32[128,512]{1,0:T(8,128)S(1)}, f32[128,512]{1,0:T(8,128)S(1)}) custom-call(bf16[896,128]{1,0:T(8,128)(2,1)S(1)} %get-tuple-element.36.refs_0_.refs_1_, bf16[912,128]{1,0:T(8,128)(2,1)S(1)} %collective-permute-done.4.refs_1_.refs_2_, bf16[3712,512]{1,0:T(8,128)(2,1)S(1)} %get-tuple-element.45.refs_2_.refs_8_.down, ...), custom_call_target="tpu_custom_call" | custom-call | flops 4000000000 | bytes 1048576 | tf_op jit(solution)/shard_map/pallas_call | solution.py:334
  20.3 0.6 %shard_map.122 = (f32[128,512]{1,0:T(8,128)S(1)}, f32[128,512]{1,0:T(8,128)S(1)}) custom-call(bf16[400,128]{1,0:T(8,128)(2,1)S(1)} %collective-permute-done.5.refs_2_.refs_0_.refs_3_, bf16[400,128]{1,0:T(8,128)(2,1)S(1)} %collective-permute-done.6.refs_3_.refs_1_.refs_4_, bf16[3712,512]{1,0:T(8,128)(2,1)S(1)} %get-tuple-element.45.refs_2_.refs_8_.down, ...), custom_call_target="tpu_custom_call" | custom-call | flops 4000000000 | bytes 1048576 | tf_op jit(solution)/shard_map/pallas_call | solution.py:334
  20.8 0.0 collective-permute-done.7.refs_0_.refs_5_
  20.8 0.9 %collective-permute-done.8.refs_1_.refs_6_ = bf16[512,128]{1,0:T(8,128)(2,1)S(1)} collective-permute-done((bf16[512,128]{1,0:T(8,128)(2,1)S(1)}, bf16[512,128]{1,0:T(8,128)(2,1)S(1)}, u32[]{:S(2)}, u32[]{:S(2)}) %collective-permute-start.8) | collective-permute-done | bytes 131104 | tf_op jit(solution)/shard_map/ppermute | solution.py:346
  21.7 0.0 collective-permute-done.9.refs_3_
  21.7 1.4 %shard_map.123 = (bf16[128,128]{1,0:T(8,128)(2,1)S(1)}, bf16[128,512]{1,0:T(8,128)(2,1)S(1)}, bf16[128,512]{1,0:T(8,128)(2,1)S(1)}, bf16[512,128]{1,0:T(8,128)(2,1)S(1)}, bf16[512,128]{1,0:T(8,128)(2,1)S(1)}) custom-call(bf16[512,128]{1,0:T(8,128)(2,1)S(1)} %collective-permute-done.7.refs_0_.refs_5_, ...), custom_call_target="tpu_custom_call" | custom-call | flops 4000000000 | bytes 1048576 | tf_op jit(solution)/shard_map/pallas_call | solution.py:334
  23.1 0.5 %shard_map.124 = (bf16[384,128]{1,0:T(8,128)(2,1)S(1)}, bf16[384,128]{1,0:T(8,128)(2,1)S(1)}) custom-call(bf16[128,512]{1,0:T(8,128)(2,1)S(1)} %get-tuple-element.54.low.refs_8_, bf16[128,512]{1,0:T(8,128)(2,1)S(1)} %get-tuple-element.55.grad, bf16[3712,512]{1,0:T(8,128)(2,1)S(1)} %get-tuple-element.45.refs_2_.refs_8_.down, ...), custom_call_target="tpu_custom_call" | custom-call | flops 4000000000 | bytes 1048576 | tf_op jit(solution)/shard_map/pallas_call | solution.py:334
  23.6 1.0 %shard_map.125 = (bf16[896,128]{1,0:T(8,128)(2,1)S(1)}, bf16[896,128]{1,0:T(8,128)(2,1)S(1)}) custom-call(bf16[128,512]{1,0:T(8,128)(2,1)S(1)} %get-tuple-element.54.low.refs_8_, bf16[128,512]{1,0:T(8,128)(2,1)S(1)} %get-tuple-element.55.grad, bf16[3712,512]{1,0:T(8,128)(2,1)S(1)} %get-tuple-element.45.refs_2_.refs_8_.down, ...), custom_call_target="tpu_custom_call" | custom-call | flops 4000000000 | bytes 1048576 | tf_op jit(solution)/shard_map/pallas_call | solution.py:334
  24.7 1.3 %collective-permute-start.13 = (bf16[384,128]{1,0:T(8,128)(2,1)S(1)}, bf16[384,128]{1,0:T(8,128)(2,1)S(1)}, u32[]{:S(2)}, u32[]{:S(2)}) collective-permute-start(bf16[384,128]{1,0:T(8,128)(2,1)S(1)} %get-tuple-element.56._), channel_id=1, source_target_pairs={{0,2},{1,3},{2,0},{3,1},{4,6},{5,7},{6,4},{7,5},{8,10},{9,11},{10,... | collective-permute-start | bytes 294920 | tf_op jit(solution)/shard_map/ppermute | solution.py:346
  26.0 0.2 collective-permute-start.11
  26.2 1.4 %collective-permute-start.12 = (bf16[512,128]{1,0:T(8,128)(2,1)S(1)}, bf16[512,128]{1,0:T(8,128)(2,1)S(1)}, u32[]{:S(2)}, u32[]{:S(2)}) collective-permute-start(bf16[512,128]{1,0:T(8,128)(2,1)S(1)} %get-tuple-element.60), channel_id=1, source_target_pairs={{0,3},{1,2},{2,1},{3,0},{4,7},{5,6},{6,5},{7,4},{8,11},{9,10},{10,... | collective-permute-start | bytes 393224 | tf_op jit(solution)/shard_map/ppermute | solution.py:346
  27.7 0.3 collective-permute-start.14
  28.0 1.0 %collective-permute-start.10 = (bf16[896,128]{1,0:T(8,128)(2,1)S(1)}, bf16[896,128]{1,0:T(8,128)(2,1)S(1)}, u32[]{:S(2)}, u32[]{:S(2)}) collective-permute-start(bf16[896,128]{1,0:T(8,128)(2,1)S(1)} %get-tuple-element.58), channel_id=1, source_target_pairs={{0,1},{1,0},{2,3},{3,2},{4,5},{5,4},{6,7},{7,6},{8,9},{9,8},{10,11... | collective-permute-start | bytes 688136 | tf_op jit(solution)/shard_map/ppermute | solution.py:346
  28.9 2.4 %shard_map.126 = bf16[128,3456]{1,0:T(8,128)(2,1)} custom-call(s32[8,128]{1,0:T(8,128)S(1)} %get-tuple-element.33.refs_0_, bf16[896,128]{1,0:T(8,128)(2,1)S(1)} %get-tuple-element.36.refs_0_.refs_1_, bf16[912,128]{1,0:T(8,128)(2,1)S(1)} %collective-permute-done.4.refs_1_.refs_2_, bf16[400,128]{1,0:T(8,128)(2,1)S(1)} %collective-permute-done.5.refs_2_.refs_0_.refs_3_, ...), custom_call_target="tpu_custom_call" | custom-call | flops 4000000000 | bytes 1048576 | tf_op jit(solution)/shard_map/pallas_call | solution.py:334
  31.4 0.2 collective-permute-done.11.refs_3_
  31.5 4.5 %collective-permute-done.12.refs_4_ = bf16[512,128]{1,0:T(8,128)(2,1)S(1)} collective-permute-done((bf16[512,128]{1,0:T(8,128)(2,1)S(1)}, bf16[512,128]{1,0:T(8,128)(2,1)S(1)}, u32[]{:S(2)}, u32[]{:S(2)}) %collective-permute-start.12) | collective-permute-done | bytes 131104 | tf_op jit(solution)/shard_map/ppermute | solution.py:346
  36.0 0.0 collective-permute-done.10.refs_2_
  36.0 1.5 %scatter.1 = (f32[1,7,512,128]{3,2,1,0:T(8,128)}, f32[3,512,128]{2,1,0:T(8,128)S(1)}) custom-call(s32[32,128]{1,0:T(8,128)S(1)} %get-tuple-element.34.lines.refs_1_.refs_0_, bf16[896,128]{1,0:T(8,128)(2,1)S(1)} %get-tuple-element.57.refs_11_.refs_1_, bf16[896,128]{1,0:T(8,128)(2,1)S(1)} %collective-permute-done.10.refs_2_, ...), custom_call_target="tpu_custom_call" | custom-call | tf_op jit(solution)/shard_map/scatter/pallas_call | solution.py:487
  37.6 0.0 collective-permute-done.14.refs_3_
  37.6 0.0 collective-permute-done.13.refs_2_
  37.6 1.2 %last.1 = f32[1,7,512,128]{3,2,1,0:T(8,128)} custom-call(s32[32,128]{1,0:T(8,128)S(1)} %get-tuple-element.34.lines.refs_1_.refs_0_, f32[3,512,128]{2,1,0:T(8,128)S(1)} %get-tuple-element.61.refs_1_, bf16[384,128]{1,0:T(8,128)(2,1)S(1)} %collective-permute-done.13.refs_2_, ...), custom_call_target="tpu_custom_call", output_to_operand_aliasing={{}: (4, {})} | custom-call | tf_op jit(solution)/shard_map/last/pallas_call | solution.py:499
  (16 shorter events, 0.0 us)
Async XLA Ops:
  0.6 6.4 %copy-start.2 = (bf16[7,512,128]{2,1,0:T(8,128)(2,1)S(1)}, bf16[7,512,128]{2,1,0:T(8,128)(2,1)}, u32[]{:S(2)}) copy-start(bf16[7,512,128]{2,1,0:T(8,128)(2,1)} %refs_3_.1) | copy-start | bytes 2752516
  0.6 6.4 %copy-start.5 = (s32[128,26]{0,1:T(8,128)S(1)}, s32[128,26]{0,1:T(8,128)}, u32[]{:S(2)}) copy-start(s32[128,26]{0,1:T(8,128)} %param.13) | copy-start | bytes 39940
  0.7 6.4 %copy-start.8 = (s32[26]{0:T(128)S(1)}, s32[26]{0:T(128)}, u32[]{:S(2)}) copy-start(s32[26]{0:T(128)} %refs_0_.1) | copy-start | bytes 316
  0.7 6.3 %collective-permute-start.2 = (s32[26,128]{1,0:T(8,128)}, s32[26,128]{1,0:T(8,128)S(1)}, u32[]{:S(2)}, u32[]{:S(2)}) collective-permute-start(s32[26,128]{1,0:T(8,128)} %bitcast.3), channel_id=1, source_target_pairs={{0,3},{1,2},{2,1},{3,0},{4,7},{5,6},{6,5},{7,4},{8,11},{9,10},{10,... | collective-permute-start | bytes 39944 | tf_op jit(solution)/shard_map/ppermute | solution.py:346
  3.3 3.7 %collective-permute-start.1 = (s32[26,128]{1,0:T(8,128)}, s32[26,128]{1,0:T(8,128)S(1)}, u32[]{:S(2)}, u32[]{:S(2)}) collective-permute-start(s32[26,128]{1,0:T(8,128)} %bitcast.4), channel_id=1, source_target_pairs={{0,2},{1,3},{2,0},{3,1},{4,6},{5,7},{6,4},{7,5},{8,10},{9,11},{10,... | collective-permute-start | bytes 39944 | tf_op jit(solution)/shard_map/ppermute | solution.py:346
  3.3 3.7 %collective-permute-start = (s32[26,128]{1,0:T(8,128)}, s32[26,128]{1,0:T(8,128)S(1)}, u32[]{:S(2)}, u32[]{:S(2)}) collective-permute-start(s32[26,128]{1,0:T(8,128)} %bitcast.5), channel_id=1, source_target_pairs={{0,1},{1,0},{2,3},{3,2},{4,5},{5,4},{6,7},{7,6},{8,9},{9,8},{10,11... | collective-permute-start | bytes 39944 | tf_op jit(solution)/shard_map/ppermute | solution.py:346
  3.8 4.5 %collective-permute-start.3 = (bf16[16,128]{1,0:T(8,128)(2,1)}, bf16[16,128]{1,0:T(8,128)(2,1)S(1)}, u32[]{:S(2)}, u32[]{:S(2)}) collective-permute-start(bf16[16,128]{1,0:T(8,128)(2,1)} %param.10), channel_id=1, source_target_pairs={{0,0},{5,1},{10,2},{15,3},{4,4},{1,5},{14,6},{11,7},{8,8},{13,9},{... | collective-permute-start | bytes 12296 | tf_op jit(solution)/shard_map/ppermute | solution.py:357
  6.9 7.4 %copy-start.3 = (bf16[128,3456]{1,0:T(8,128)(2,1)S(1)}, bf16[128,3456]{1,0:T(8,128)(2,1)}, u32[]{:S(2)}) copy-start(bf16[128,3456]{1,0:T(8,128)(2,1)} %refs_6_.3) | copy-start | bytes 2654212
  7.0 7.4 %copy-start = (bf16[3456,512]{1,0:T(8,128)(2,1)S(1)}, bf16[3456,512]{1,0:T(8,128)(2,1)}, u32[]{:S(2)}) copy-start(bf16[3456,512]{1,0:T(8,128)(2,1)} %refs_4_.1) | copy-start | bytes 10616836
  7.0 7.4 %copy-start.1 = (bf16[512,3456]{1,0:T(8,128)(2,1)S(1)}, bf16[512,3456]{1,0:T(8,128)(2,1)}, u32[]{:S(2)}) copy-start(bf16[512,3456]{1,0:T(8,128)(2,1)} %refs_5_.1) | copy-start | bytes 10616836
  7.0 7.4 %copy-start.6 = (f32[3456]{0:T(1024)S(1)}, f32[3456]{0:T(1024)}, u32[]{:S(2)}) copy-start(f32[3456]{0:T(1024)} %param.18) | copy-start | bytes 41476
  8.4 8.1 %collective-permute-start.5 = (bf16[400,128]{1,0:T(8,128)(2,1)S(1)}, bf16[400,128]{1,0:T(8,128)(2,1)S(1)}, u32[]{:S(2)}, u32[]{:S(2)}) collective-permute-start(bf16[400,128]{1,0:T(8,128)(2,1)S(1)} %get-tuple-element.39), channel_id=1, source_target_pairs={{0,2},{1,3},{2,0},{3,1},{4,6},{5,7},{6,4},{7,5},{8,10},{9,11},{10,... | collective-permute-start | bytes 307208 | tf_op jit(solution)/shard_map/ppermute | solution.py:346
  10.5 6.0 %collective-permute-start.6 = (bf16[400,128]{1,0:T(8,128)(2,1)S(1)}, bf16[400,128]{1,0:T(8,128)(2,1)S(1)}, u32[]{:S(2)}, u32[]{:S(2)}) collective-permute-start(bf16[400,128]{1,0:T(8,128)(2,1)S(1)} %get-tuple-element.40), channel_id=1, source_target_pairs={{0,3},{1,2},{2,1},{3,0},{4,7},{5,6},{6,5},{7,4},{8,11},{9,10},{10,... | collective-permute-start | bytes 307208 | tf_op jit(solution)/shard_map/ppermute | solution.py:346
  11.5 9.3 %collective-permute-start.7 = (bf16[512,128]{1,0:T(8,128)(2,1)S(1)}, bf16[512,128]{1,0:T(8,128)(2,1)S(1)}, u32[]{:S(2)}, u32[]{:S(2)}) collective-permute-start(bf16[512,128]{1,0:T(8,128)(2,1)S(1)} %get-tuple-element.41), channel_id=1, source_target_pairs={{0,2},{1,3},{2,0},{3,1},{4,6},{5,7},{6,4},{7,5},{8,10},{9,11},{10,... | collective-permute-start | bytes 393224 | tf_op jit(solution)/shard_map/ppermute | solution.py:346
  13.3 8.4 %collective-permute-start.8 = (bf16[512,128]{1,0:T(8,128)(2,1)S(1)}, bf16[512,128]{1,0:T(8,128)(2,1)S(1)}, u32[]{:S(2)}, u32[]{:S(2)}) collective-permute-start(bf16[512,128]{1,0:T(8,128)(2,1)S(1)} %get-tuple-element.42), channel_id=1, source_target_pairs={{0,3},{1,2},{2,1},{3,0},{4,7},{5,6},{6,5},{7,4},{8,11},{9,10},{10,... | collective-permute-start | bytes 393224 | tf_op jit(solution)/shard_map/ppermute | solution.py:346
  14.1 2.4 %collective-permute-start.4 = (bf16[912,128]{1,0:T(8,128)(2,1)S(1)}, bf16[912,128]{1,0:T(8,128)(2,1)S(1)}, u32[]{:S(2)}, u32[]{:S(2)}) collective-permute-start(bf16[912,128]{1,0:T(8,128)(2,1)S(1)} %shard_map.116.refs_2_), channel_id=1, source_target_pairs={{0,1},{1,0},{2,3},{3,2},{4,5},{5,4},{6,7},{7,6},{8,9},{9,8},{10,11... | collective-permute-start | bytes 700424 | tf_op jit(solution)/shard_map/ppermute | solution.py:346
  16.5 2.4 %copy-start.4 = (bf16[128,128]{1,0:T(8,128)(2,1)S(1)}, bf16[128,128]{1,0:T(8,128)(2,1)}, u32[]{:S(2)}) copy-start(bf16[128,128]{1,0:T(8,128)(2,1)} %dense.1) | copy-start | bytes 98308
  16.5 2.4 %copy-start.7 = (s32[128,16]{0,1:T(8,128)S(1)}, s32[128,16]{0,1:T(8,128)}, u32[]{:S(2)}) copy-start(s32[128,16]{0,1:T(8,128)} %param.11) | copy-start | bytes 24580
  16.5 5.2 %collective-permute-start.9 = (bf16[64,128]{1,0:T(8,128)(2,1)S(1)}, bf16[64,128]{1,0:T(8,128)(2,1)S(1)}, u32[]{:S(2)}, u32[]{:S(2)}) collective-permute-start(bf16[64,128]{1,0:T(8,128)(2,1)S(1)} %shard_map.119.group.refs_2_), channel_id=1, source_target_pairs={{16,0},{20,4},{24,8},{28,12},{0,16},{4,20},{8,24},{12,28},{17,1},{... | collective-permute-start | bytes 49160 | tf_op jit(solution)/shard_map/ppermute | solution.py:429
  24.7 12.9 %collective-permute-start.13 = (bf16[384,128]{1,0:T(8,128)(2,1)S(1)}, bf16[384,128]{1,0:T(8,128)(2,1)S(1)}, u32[]{:S(2)}, u32[]{:S(2)}) collective-permute-start(bf16[384,128]{1,0:T(8,128)(2,1)S(1)} %get-tuple-element.56._), channel_id=1, source_target_pairs={{0,2},{1,3},{2,0},{3,1},{4,6},{5,7},{6,4},{7,5},{8,10},{9,11},{10,... | collective-permute-start | bytes 294920 | tf_op jit(solution)/shard_map/ppermute | solution.py:346
  26.0 5.5 %collective-permute-start.11 = (bf16[512,128]{1,0:T(8,128)(2,1)S(1)}, bf16[512,128]{1,0:T(8,128)(2,1)S(1)}, u32[]{:S(2)}, u32[]{:S(2)}) collective-permute-start(bf16[512,128]{1,0:T(8,128)(2,1)S(1)} %get-tuple-element.59), channel_id=1, source_target_pairs={{0,2},{1,3},{2,0},{3,1},{4,6},{5,7},{6,4},{7,5},{8,10},{9,11},{10,... | collective-permute-start | bytes 393224 | tf_op jit(solution)/shard_map/ppermute | solution.py:346
  26.2 9.8 %collective-permute-start.12 = (bf16[512,128]{1,0:T(8,128)(2,1)S(1)}, bf16[512,128]{1,0:T(8,128)(2,1)S(1)}, u32[]{:S(2)}, u32[]{:S(2)}) collective-permute-start(bf16[512,128]{1,0:T(8,128)(2,1)S(1)} %get-tuple-element.60), channel_id=1, source_target_pairs={{0,3},{1,2},{2,1},{3,0},{4,7},{5,6},{6,5},{7,4},{8,11},{9,10},{10,... | collective-permute-start | bytes 393224 | tf_op jit(solution)/shard_map/ppermute | solution.py:346
  27.7 9.9 %collective-permute-start.14 = (bf16[384,128]{1,0:T(8,128)(2,1)S(1)}, bf16[384,128]{1,0:T(8,128)(2,1)S(1)}, u32[]{:S(2)}, u32[]{:S(2)}) collective-permute-start(bf16[384,128]{1,0:T(8,128)(2,1)S(1)} %get-tuple-element.62), channel_id=1, source_target_pairs={{0,3},{1,2},{2,1},{3,0},{4,7},{5,6},{6,5},{7,4},{8,11},{9,10},{10,... | collective-permute-start | bytes 294920 | tf_op jit(solution)/shard_map/ppermute | solution.py:346
  28.0 8.1 %collective-permute-start.10 = (bf16[896,128]{1,0:T(8,128)(2,1)S(1)}, bf16[896,128]{1,0:T(8,128)(2,1)S(1)}, u32[]{:S(2)}, u32[]{:S(2)}) collective-permute-start(bf16[896,128]{1,0:T(8,128)(2,1)S(1)} %get-tuple-element.58), channel_id=1, source_target_pairs={{0,1},{1,0},{2,3},{3,2},{4,5},{5,4},{6,7},{7,6},{8,9},{9,8},{10,11... | collective-permute-start | bytes 688136 | tf_op jit(solution)/shard_map/ppermute | solution.py:346

commit v5 on v4

--- a/solution.py
+++ b/solution.py
@@ -11,7 +11,7 @@
 BF16 = jnp.bfloat16
 F32 = jnp.float32
 ROW_PARTS = (3, 4)
-GRAD_PARTS = (4, 3)
+GRAD_PARTS = (5, 2)
 NEAR = 2
 VMEM = pl.BlockSpec(memory_space=pltpu.VMEM)
 SMEM = pl.BlockSpec(memory_space=pltpu.SMEM)
@@ -189,8 +189,9 @@
 
 
 def second_kernel(span, grad_span, owners, slots, blocks, *refs):
-    far = refs[: owners - NEAR]
-    refs = refs[owners - NEAR :]
+    odds = range(NEAR + 1, owners, 2)
+    far = refs[: len(odds)]
+    refs = refs[len(odds) :]
     held = -(-blocks // owners)
     shards = refs[:held]
     counts, base, low_in, grad_in, down, up, bias, cot = refs[held : 8 + held]
@@ -206,14 +207,14 @@
     front = pooled.astype(BF16)
     front_out[...] = front
     low, grad = add_up(front, 0, down, up, cot, low_in[...], grad_in[...])
-    for k, ref in enumerate(far, NEAR):
+    for k, ref in zip(odds, far):
         x = wide(ref, span[1], batch)
         low, grad = add_up(x, (1 + k * slots + span[0]) * width, down, up, cot, low, grad)
     low = low.astype(BF16)
     grad = grad.astype(BF16)
     low_out[...] = low
     grad_out[...] = grad
-    for k, out in enumerate(outs, NEAR):
+    for k, out in zip(range(NEAR, owners, 2), outs):
         begin = 1 + k * slots + grad_span[0]
         grads_to(out, begin, grad_span[1], low, grad, down, up, bias, cot)
 
@@ -450,13 +451,26 @@
         [*far[0], down, up, cot, low, grad],
         mib=6,
     )
+    low, grad = call(
+        functools.partial(sums_kernel, row_spans[1], range(NEAR, owners, 2), slots),
+        sums,
+        [*far[1][::2], down, up, cot, low, grad],
+        mib=6,
+    )
     front, low, grad, *sends = call(
         functools.partial(second_kernel, row_spans[1], grad_spans[0], owners, slots, blocks),
         [shape(batch, width), shape(batch, rank), shape(batch, rank)]
-        + [shape(grad_spans[0][1] * batch, width)] * far_count,
-        [*far[1], *shards, counts, base, low, grad, down, up, bias, cot],
-        mib=6,
-    )
+        + [shape(grad_spans[0][1] * batch, width)] * (far_count // 2),
+        [*far[1][1::2], *shards, counts, base, low, grad, down, up, bias, cot],
+        mib=6,
+    )
+    odds = call(
+        functools.partial(grads_kernel, grad_spans[0], range(NEAR + 1, owners, 2), slots),
+        [shape(grad_spans[0][1] * batch, width)] * (far_count // 2),
+        [low, grad, down, up, bias, cot, front],
+        mib=6,
+    )
+    sends = [array for pair in zip(sends, odds) for array in pair]
     far_grads = [far_swap(sends)]
     sends = call(
         functools.partial(grads_kernel, grad_spans[1], range(NEAR, owners), slots),

time: 39 us -> 41.1 us (1.054)
  the two profiles are of different devices: /device:TPU:1 before, /device:TPU:0 now
where the time goes in v5:
time: 41.1 us; the launch traced here: 40.9 us
  starting transfers between devices  15.5 us (38%)
  Pallas kernels  15 us (36%)
  waiting for transfers between devices  9.65 us (23%)
  between operations  0.83 us (2%)
    pallas_call x16, Pallas kernels, call(): pl.pallas_call(kernel, out_shape=shapes, in_specs=[VMEM] * len(operands)...  12 us
    ppermute x13, starting transfers between devices, swap(): return lax.ppermute(array, 'table', [(i, i ^ k) for i in range(owners)])  11.6 us
    ppermute x13, waiting for transfers between devices, swap(): return lax.ppermute(array, 'table', [(i, i ^ k) for i in range(owners)])  9.64 us
    ppermute x1, starting transfers between devices, on_device(): shards.append(lax.ppermute(group, 'blk', pairs))  2.59 us
    pallas_call x1, Pallas kernels, on_device(): pl.pallas_call(functools.partial(scatter_kernel, grad_spans[0], later, ow...  1.8 us
    ppermute x1, starting transfers between devices, on_device(): lax.ppermute(hot_slab, ('blk', 'table'), [(peer(b, t, blocks) * owners +...  1.33 us
    pallas_call x1, Pallas kernels, on_device(): pl.pallas_call(functools.partial(last_kernel, later, owners, pad), out_sh...  1.11 us
  transfers between devices with their start and end apart: 15, of which 6 were waited for; matrix products, arithmetic and copies ran while one was open for 0% of the time, Pallas kernels for 26%

profile of v5, /device:TPU:0, one launch (start us, length us, event | category | flops | bytes accessed | tf_op | source)
XLA Modules:
  0.0 40.9 jit_solution(13775056384837685281)
XLA Ops:
  0.7 0.6 %collective-permute-start = (s32[26,128]{1,0:T(8,128)}, s32[26,128]{1,0:T(8,128)S(1)}, u32[]{:S(2)}, u32[]{:S(2)}) collective-permute-start(s32[26,128]{1,0:T(8,128)} %bitcast.3), channel_id=1, source_target_pairs={{0,1},{1,0},{2,3},{3,2},{4,5},{5,4},{6,7},{7,6},{8,9},{9,8},{10,11... | collective-permute-start | bytes 39944 | tf_op jit(solution)/shard_map/ppermute | solution.py:347
  1.2 2.6 %collective-permute-start.1 = (s32[26,128]{1,0:T(8,128)}, s32[26,128]{1,0:T(8,128)S(1)}, u32[]{:S(2)}, u32[]{:S(2)}) collective-permute-start(s32[26,128]{1,0:T(8,128)} %bitcast.4), channel_id=1, source_target_pairs={{0,2},{1,3},{2,0},{3,1},{4,6},{5,7},{6,4},{7,5},{8,10},{9,11},{10,... | collective-permute-start | bytes 39944 | tf_op jit(solution)/shard_map/ppermute | solution.py:347
  3.8 0.0 collective-permute-start.2
  3.8 1.3 %collective-permute-start.3 = (bf16[16,128]{1,0:T(8,128)(2,1)}, bf16[16,128]{1,0:T(8,128)(2,1)S(1)}, u32[]{:S(2)}, u32[]{:S(2)}) collective-permute-start(bf16[16,128]{1,0:T(8,128)(2,1)} %param.10), channel_id=1, source_target_pairs={{0,0},{5,1},{10,2},{15,3},{4,4},{1,5},{14,6},{11,7},{8,8},{13,9},{... | collective-permute-start | bytes 12296 | tf_op jit(solution)/shard_map/ppermute | solution.py:358
  5.2 0.0 copy-start.6
  5.2 0.0 collective-permute-done.refs_3_
  5.2 0.5 %collective-permute-done.1.refs_4_ = s32[26,128]{1,0:T(8,128)S(1)} collective-permute-done((s32[26,128]{1,0:T(8,128)}, s32[26,128]{1,0:T(8,128)S(1)}, u32[]{:S(2)}, u32[]{:S(2)}) %collective-permute-start.1) | collective-permute-done | bytes 13344 | tf_op jit(solution)/shard_map/ppermute | solution.py:347
  5.7 1.4 %collective-permute-done.2.refs_5_ = s32[26,128]{1,0:T(8,128)S(1)} collective-permute-done((s32[26,128]{1,0:T(8,128)}, s32[26,128]{1,0:T(8,128)S(1)}, u32[]{:S(2)}, u32[]{:S(2)}) %collective-permute-start.2) | collective-permute-done | bytes 13344 | tf_op jit(solution)/shard_map/ppermute | solution.py:347
  7.2 1.3 %shard_map.114 = (s32[32,128]{1,0:T(8,128)S(1)}, s32[8,128]{1,0:T(8,128)S(1)}, bf16[400,128]{1,0:T(8,128)(2,1)S(1)}, bf16[400,128]{1,0:T(8,128)(2,1)S(1)}) custom-call(s32[26]{0:T(128)S(1)} %copy-done.8, s32[8,128]{1,0:T(8,128)S(1)} %shard_map.113.refs_1_, s32[26,128]{1,0:T(8,128)S(1)} %bitcast.6, s32[26,128]{1,0:T(8,128)S(1)} %collective-permute-done.refs_3_, ...), custom_call_target="tpu_custom_call" | custom-call | flops 1000000000 | bytes 1048576 | tf_op jit(solution)/shard_map/pallas_call | solution.py:335
  8.5 0.6 %shard_map.115 = (s32[8,128]{1,0:T(8,128)S(1)}, bf16[512,128]{1,0:T(8,128)(2,1)S(1)}, bf16[512,128]{1,0:T(8,128)(2,1)S(1)}) custom-call(s32[32,128]{1,0:T(8,128)S(1)} %get-tuple-element.35.lines.refs_1_.refs_0_, bf16[7,512,128]{2,1,0:T(8,128)(2,1)S(1)} %copy-done.2), custom_call_target="tpu_custom_call" | custom-call | flops 500000000 | bytes 1048576 | tf_op jit(solution)/shard_map/pallas_call | solution.py:335
  9.0 0.0 collective-permute-done.3.shard.refs_0_
  9.0 0.5 %shard_map.116.refs_2_ = bf16[912,128]{1,0:T(8,128)(2,1)S(1)} custom-call(s32[32,128]{1,0:T(8,128)S(1)} %get-tuple-element.35.lines.refs_1_.refs_0_, s32[8,128]{1,0:T(8,128)S(1)} %get-tuple-element.36._, bf16[7,512,128]{2,1,0:T(8,128)(2,1)S(1)} %copy-done.2, bf16[16,128]{1,0:T(8,128)(2,1)S(1)} %collective-permute-done.3.shard.refs_0_), custom_call_target="tpu_custom_call" | custom-call | flops 500000000 | bytes 1048576 | tf_op jit(solution)/shard_map/pallas_call | solution.py:335
  9.6 0.5 %collective-permute-start.4 = (bf16[912,128]{1,0:T(8,128)(2,1)S(1)}, bf16[912,128]{1,0:T(8,128)(2,1)S(1)}, u32[]{:S(2)}, u32[]{:S(2)}) collective-permute-start(bf16[912,128]{1,0:T(8,128)(2,1)S(1)} %shard_map.116.refs_2_), channel_id=1, source_target_pairs={{0,1},{1,0},{2,3},{3,2},{4,5},{5,4},{6,7},{7,6},{8,9},{9,8},{10,11... | collective-permute-start | bytes 700424 | tf_op jit(solution)/shard_map/ppermute | solution.py:347
  10.1 2.5 %collective-permute-start.5 = (bf16[400,128]{1,0:T(8,128)(2,1)S(1)}, bf16[400,128]{1,0:T(8,128)(2,1)S(1)}, u32[]{:S(2)}, u32[]{:S(2)}) collective-permute-start(bf16[400,128]{1,0:T(8,128)(2,1)S(1)} %get-tuple-element.40), channel_id=1, source_target_pairs={{0,2},{1,3},{2,0},{3,1},{4,6},{5,7},{6,4},{7,5},{8,10},{9,11},{10,... | collective-permute-start | bytes 307208 | tf_op jit(solution)/shard_map/ppermute | solution.py:347
  12.6 0.0 collective-permute-start.6
  12.6 1.4 %collective-permute-start.7 = (bf16[512,128]{1,0:T(8,128)(2,1)S(1)}, bf16[512,128]{1,0:T(8,128)(2,1)S(1)}, u32[]{:S(2)}, u32[]{:S(2)}) collective-permute-start(bf16[512,128]{1,0:T(8,128)(2,1)S(1)} %get-tuple-element.42), channel_id=1, source_target_pairs={{0,2},{1,3},{2,0},{3,1},{4,6},{5,7},{6,4},{7,5},{8,10},{9,11},{10,... | collective-permute-start | bytes 393224 | tf_op jit(solution)/shard_map/ppermute | solution.py:347
  14.1 0.3 collective-permute-start.8
  14.4 2.1 %shard_map.117 = (bf16[896,128]{1,0:T(8,128)(2,1)S(1)}, bf16[3712,512]{1,0:T(8,128)(2,1)S(1)}, bf16[512,3712]{1,0:T(8,128)(2,1)S(1)}, bf16[128,3712]{1,0:T(8,128)(2,1)S(1)}, f32[32,128]{1,0:T(8,128)S(1)}) custom-call(s32[8,128]{1,0:T(8,128)S(1)} %get-tuple-element.34.refs_0_, s32[32,128]{1,0:T(8,128)S(1)} %get-tuple-element.35.lines.refs_1_.refs_0_, ...), custom_call_target="tpu_custom_call" | custom-call | flops 4000000000 | bytes 1048576 | tf_op jit(solution)/shard_map/pallas_call | solution.py:335
  16.5 0.0 copy-start.4
  16.5 0.0 copy-start.7
  16.5 0.0 collective-permute-done.5.refs_2_.refs_0_.refs_3_
  16.5 1.6 %collective-permute-done.6.refs_3_.refs_1_.refs_4_ = bf16[400,128]{1,0:T(8,128)(2,1)S(1)} collective-permute-done((bf16[400,128]{1,0:T(8,128)(2,1)S(1)}, bf16[400,128]{1,0:T(8,128)(2,1)S(1)}, u32[]{:S(2)}, u32[]{:S(2)}) %collective-permute-start.6) | collective-permute-done | bytes 102432 | tf_op jit(solution)/shard_map/ppermute | solution.py:347
  18.1 0.0 collective-permute-done.4.refs_1_.refs_2_
  18.1 2.6 %collective-permute-start.9 = (bf16[64,128]{1,0:T(8,128)(2,1)S(1)}, bf16[64,128]{1,0:T(8,128)(2,1)S(1)}, u32[]{:S(2)}, u32[]{:S(2)}) collective-permute-start(bf16[64,128]{1,0:T(8,128)(2,1)S(1)} %shard_map.119.group.refs_1_), channel_id=1, source_target_pairs={{16,0},{20,4},{24,8},{28,12},{0,16},{4,20},{8,24},{12,28},{17,1},{... | collective-permute-start | bytes 49160 | tf_op jit(solution)/shard_map/ppermute | solution.py:430
  20.7 0.3 shard_map.120
  21.0 1.0 %shard_map.121 = (f32[128,512]{1,0:T(8,128)S(1)}, f32[128,512]{1,0:T(8,128)S(1)}) custom-call(bf16[896,128]{1,0:T(8,128)(2,1)S(1)} %get-tuple-element.37.refs_0_.refs_1_, bf16[912,128]{1,0:T(8,128)(2,1)S(1)} %collective-permute-done.4.refs_1_.refs_2_, bf16[3712,512]{1,0:T(8,128)(2,1)S(1)} %get-tuple-element.46.refs_2_.refs_1_.refs_7_.down, ...), custom_call_target="tpu_custom_call" | custom-call | flops 4000000000 | bytes 1048576 | tf_op jit(solution)/shard_map/pallas_call | solution.py:335
  22.1 0.6 %shard_map.122 = (f32[128,512]{1,0:T(8,128)S(1)}, f32[128,512]{1,0:T(8,128)S(1)}) custom-call(bf16[400,128]{1,0:T(8,128)(2,1)S(1)} %collective-permute-done.5.refs_2_.refs_0_.refs_3_, bf16[400,128]{1,0:T(8,128)(2,1)S(1)} %collective-permute-done.6.refs_3_.refs_1_.refs_4_, bf16[3712,512]{1,0:T(8,128)(2,1)S(1)} %get-tuple-element.46.refs_2_.refs_1_.refs_7_.down, ...), custom_call_target="tpu_custom_call" | custom-call | flops 4000000000 | bytes 1048576 | tf_op jit(solution)/shard_map/pallas_call | solution.py:335
  22.6 0.0 collective-permute-done.7.refs_0_.refs_5_
  22.6 0.4 shard_map.123
  23.0 0.4 collective-permute-done.8.refs_0_.refs_6_
  23.4 0.0 collective-permute-done.9.refs_2_
  23.4 1.0 %shard_map.124 = (bf16[128,128]{1,0:T(8,128)(2,1)S(1)}, bf16[128,512]{1,0:T(8,128)(2,1)S(1)}, bf16[128,512]{1,0:T(8,128)(2,1)S(1)}, bf16[640,128]{1,0:T(8,128)(2,1)S(1)}) custom-call(bf16[512,128]{1,0:T(8,128)(2,1)S(1)} %collective-permute-done.8.refs_0_.refs_6_, bf16[64,128]{1,0:T(8,128)(2,1)S(1)} %shard_map.119.group.refs_1_, ...), custom_call_target="tpu_custom_call" | custom-call | flops 4000000000 | bytes 1048576 | tf_op jit(solution)/shard_map/pallas_call | solution.py:335
  24.4 0.5 %shard_map.128 = bf16[640,128]{1,0:T(8,128)(2,1)S(1)} custom-call(bf16[128,512]{1,0:T(8,128)(2,1)S(1)} %get-tuple-element.57.low.refs_8_, bf16[128,512]{1,0:T(8,128)(2,1)S(1)} %get-tuple-element.58.grad, bf16[3712,512]{1,0:T(8,128)(2,1)S(1)} %get-tuple-element.46.refs_2_.refs_1_.refs_7_.down, ...), custom_call_target="tpu_custom_call" | custom-call | flops 4000000000 | bytes 1048576 | tf_op jit(solution)/shard_map/pallas_call | solution.py:335
  24.9 0.4 shard_map.125
  25.3 1.0 %shard_map.126 = (bf16[896,128]{1,0:T(8,128)(2,1)S(1)}, bf16[896,128]{1,0:T(8,128)(2,1)S(1)}) custom-call(bf16[128,512]{1,0:T(8,128)(2,1)S(1)} %get-tuple-element.57.low.refs_8_, bf16[128,512]{1,0:T(8,128)(2,1)S(1)} %get-tuple-element.58.grad, bf16[3712,512]{1,0:T(8,128)(2,1)S(1)} %get-tuple-element.46.refs_2_.refs_1_.refs_7_.down, ...), custom_call_target="tpu_custom_call" | custom-call | flops 4000000000 | bytes 1048576 | tf_op jit(solution)/shard_map/pallas_call | solution.py:335
  26.3 1.1 %collective-permute-start.13 = (bf16[256,128]{1,0:T(8,128)(2,1)S(1)}, bf16[256,128]{1,0:T(8,128)(2,1)S(1)}, u32[]{:S(2)}, u32[]{:S(2)}) collective-permute-start(bf16[256,128]{1,0:T(8,128)(2,1)S(1)} %get-tuple-element.59._), channel_id=1, source_target_pairs={{0,2},{1,3},{2,0},{3,1},{4,6},{5,7},{6,4},{7,5},{8,10},{9,11},{10,... | collective-permute-start | bytes 196616 | tf_op jit(solution)/shard_map/ppermute | solution.py:347
  27.4 0.5 %collective-permute-start.12 = (bf16[640,128]{1,0:T(8,128)(2,1)S(1)}, bf16[640,128]{1,0:T(8,128)(2,1)S(1)}, u32[]{:S(2)}, u32[]{:S(2)}) collective-permute-start(bf16[640,128]{1,0:T(8,128)(2,1)S(1)} %shard_map.128), channel_id=1, source_target_pairs={{0,3},{1,2},{2,1},{3,0},{4,7},{5,6},{6,5},{7,4},{8,11},{9,10},{10,... | collective-permute-start | bytes 491528 | tf_op jit(solution)/shard_map/ppermute | solution.py:347
  27.8 0.7 %collective-permute-start.10 = (bf16[896,128]{1,0:T(8,128)(2,1)S(1)}, bf16[896,128]{1,0:T(8,128)(2,1)S(1)}, u32[]{:S(2)}, u32[]{:S(2)}) collective-permute-start(bf16[896,128]{1,0:T(8,128)(2,1)S(1)} %get-tuple-element.61), channel_id=1, source_target_pairs={{0,1},{1,0},{2,3},{3,2},{4,5},{5,4},{6,7},{7,6},{8,9},{9,8},{10,11... | collective-permute-start | bytes 688136 | tf_op jit(solution)/shard_map/ppermute | solution.py:347
  28.5 1.0 %collective-permute-start.11 = (bf16[640,128]{1,0:T(8,128)(2,1)S(1)}, bf16[640,128]{1,0:T(8,128)(2,1)S(1)}, u32[]{:S(2)}, u32[]{:S(2)}) collective-permute-start(bf16[640,128]{1,0:T(8,128)(2,1)S(1)} %get-tuple-element.62), channel_id=1, source_target_pairs={{0,2},{1,3},{2,0},{3,1},{4,6},{5,7},{6,4},{7,5},{8,10},{9,11},{10,... | collective-permute-start | bytes 491528 | tf_op jit(solution)/shard_map/ppermute | solution.py:347
  29.5 0.3 collective-permute-start.14
  29.9 2.4 %shard_map.127 = bf16[128,3456]{1,0:T(8,128)(2,1)} custom-call(s32[8,128]{1,0:T(8,128)S(1)} %get-tuple-element.34.refs_0_, bf16[896,128]{1,0:T(8,128)(2,1)S(1)} %get-tuple-element.37.refs_0_.refs_1_, bf16[912,128]{1,0:T(8,128)(2,1)S(1)} %collective-permute-done.4.refs_1_.refs_2_, bf16[400,128]{1,0:T(8,128)(2,1)S(1)} %collective-permute-done.5.refs_2_.refs_0_.refs_3_, ...), custom_call_target="tpu_custom_call" | custom-call | flops 4000000000 | bytes 1048576 | tf_op jit(solution)/shard_map/pallas_call | solution.py:335
  32.3 1.5 %collective-permute-done.12.refs_4_ = bf16[640,128]{1,0:T(8,128)(2,1)S(1)} collective-permute-done((bf16[640,128]{1,0:T(8,128)(2,1)S(1)}, bf16[640,128]{1,0:T(8,128)(2,1)S(1)}, u32[]{:S(2)}, u32[]{:S(2)}) %collective-permute-start.12) | collective-permute-done | bytes 163872 | tf_op jit(solution)/shard_map/ppermute | solution.py:347
  33.8 4.2 %collective-permute-done.11.refs_3_ = bf16[640,128]{1,0:T(8,128)(2,1)S(1)} collective-permute-done((bf16[640,128]{1,0:T(8,128)(2,1)S(1)}, bf16[640,128]{1,0:T(8,128)(2,1)S(1)}, u32[]{:S(2)}, u32[]{:S(2)}) %collective-permute-start.11) | collective-permute-done | bytes 163872 | tf_op jit(solution)/shard_map/ppermute | solution.py:347
  38.0 0.0 collective-permute-done.10.refs_2_
  38.0 1.8 %scatter.1 = (f32[1,7,512,128]{3,2,1,0:T(8,128)}, f32[2,512,128]{2,1,0:T(8,128)S(1)}) custom-call(s32[32,128]{1,0:T(8,128)S(1)} %get-tuple-element.35.lines.refs_1_.refs_0_, bf16[896,128]{1,0:T(8,128)(2,1)S(1)} %get-tuple-element.60.refs_11_.refs_1_, bf16[896,128]{1,0:T(8,128)(2,1)S(1)} %collective-permute-done.10.refs_2_, ...), custom_call_target="tpu_custom_call" | custom-call | tf_op jit(solution)/shard_map/scatter/pallas_call | solution.py:501
  39.8 0.0 collective-permute-done.13.refs_2_
  39.8 0.0 collective-permute-done.14.refs_3_
  39.8 1.1 %last.1 = f32[1,7,512,128]{3,2,1,0:T(8,128)} custom-call(s32[32,128]{1,0:T(8,128)S(1)} %get-tuple-element.35.lines.refs_1_.refs_0_, f32[2,512,128]{2,1,0:T(8,128)S(1)} %get-tuple-element.63.refs_1_, bf16[256,128]{1,0:T(8,128)(2,1)S(1)} %collective-permute-done.13.refs_2_, ...), custom_call_target="tpu_custom_call", output_to_operand_aliasing={{}: (4, {})} | custom-call | tf_op jit(solution)/shard_map/last/pallas_call | solution.py:513
  (18 shorter events, 0.0 us)
Async XLA Ops:
  0.6 6.5 %copy-start.2 = (bf16[7,512,128]{2,1,0:T(8,128)(2,1)S(1)}, bf16[7,512,128]{2,1,0:T(8,128)(2,1)}, u32[]{:S(2)}) copy-start(bf16[7,512,128]{2,1,0:T(8,128)(2,1)} %refs_3_.1) | copy-start | bytes 2752516
  0.6 6.5 %copy-start.5 = (s32[128,26]{0,1:T(8,128)S(1)}, s32[128,26]{0,1:T(8,128)}, u32[]{:S(2)}) copy-start(s32[128,26]{0,1:T(8,128)} %param.13) | copy-start | bytes 39940
  0.7 6.5 %copy-start.8 = (s32[26]{0:T(128)S(1)}, s32[26]{0:T(128)}, u32[]{:S(2)}) copy-start(s32[26]{0:T(128)} %refs_0_.1) | copy-start | bytes 316
  0.7 4.5 %collective-permute-start = (s32[26,128]{1,0:T(8,128)}, s32[26,128]{1,0:T(8,128)S(1)}, u32[]{:S(2)}, u32[]{:S(2)}) collective-permute-start(s32[26,128]{1,0:T(8,128)} %bitcast.3), channel_id=1, source_target_pairs={{0,1},{1,0},{2,3},{3,2},{4,5},{5,4},{6,7},{7,6},{8,9},{9,8},{10,11... | collective-permute-start | bytes 39944 | tf_op jit(solution)/shard_map/ppermute | solution.py:347
  1.2 4.5 %collective-permute-start.1 = (s32[26,128]{1,0:T(8,128)}, s32[26,128]{1,0:T(8,128)S(1)}, u32[]{:S(2)}, u32[]{:S(2)}) collective-permute-start(s32[26,128]{1,0:T(8,128)} %bitcast.4), channel_id=1, source_target_pairs={{0,2},{1,3},{2,0},{3,1},{4,6},{5,7},{6,4},{7,5},{8,10},{9,11},{10,... | collective-permute-start | bytes 39944 | tf_op jit(solution)/shard_map/ppermute | solution.py:347
  3.8 3.4 %collective-permute-start.2 = (s32[26,128]{1,0:T(8,128)}, s32[26,128]{1,0:T(8,128)S(1)}, u32[]{:S(2)}, u32[]{:S(2)}) collective-permute-start(s32[26,128]{1,0:T(8,128)} %bitcast.5), channel_id=1, source_target_pairs={{0,3},{1,2},{2,1},{3,0},{4,7},{5,6},{6,5},{7,4},{8,11},{9,10},{10,... | collective-permute-start | bytes 39944 | tf_op jit(solution)/shard_map/ppermute | solution.py:347
  3.8 5.2 %collective-permute-start.3 = (bf16[16,128]{1,0:T(8,128)(2,1)}, bf16[16,128]{1,0:T(8,128)(2,1)S(1)}, u32[]{:S(2)}, u32[]{:S(2)}) collective-permute-start(bf16[16,128]{1,0:T(8,128)(2,1)} %param.10), channel_id=1, source_target_pairs={{0,0},{5,1},{10,2},{15,3},{4,4},{1,5},{14,6},{11,7},{8,8},{13,9},{... | collective-permute-start | bytes 12296 | tf_op jit(solution)/shard_map/ppermute | solution.py:358
  5.2 9.2 %copy-start.3 = (bf16[128,3456]{1,0:T(8,128)(2,1)S(1)}, bf16[128,3456]{1,0:T(8,128)(2,1)}, u32[]{:S(2)}) copy-start(bf16[128,3456]{1,0:T(8,128)(2,1)} %refs_6_.3) | copy-start | bytes 2654212
  5.2 9.2 %copy-start = (bf16[3456,512]{1,0:T(8,128)(2,1)S(1)}, bf16[3456,512]{1,0:T(8,128)(2,1)}, u32[]{:S(2)}) copy-start(bf16[3456,512]{1,0:T(8,128)(2,1)} %refs_4_.1) | copy-start | bytes 10616836
  5.2 9.2 %copy-start.1 = (bf16[512,3456]{1,0:T(8,128)(2,1)S(1)}, bf16[512,3456]{1,0:T(8,128)(2,1)}, u32[]{:S(2)}) copy-start(bf16[512,3456]{1,0:T(8,128)(2,1)} %refs_5_.1) | copy-start | bytes 10616836
  5.2 9.2 %copy-start.6 = (f32[3456]{0:T(1024)S(1)}, f32[3456]{0:T(1024)}, u32[]{:S(2)}) copy-start(f32[3456]{0:T(1024)} %param.18) | copy-start | bytes 41476
  9.6 8.5 %collective-permute-start.4 = (bf16[912,128]{1,0:T(8,128)(2,1)S(1)}, bf16[912,128]{1,0:T(8,128)(2,1)S(1)}, u32[]{:S(2)}, u32[]{:S(2)}) collective-permute-start(bf16[912,128]{1,0:T(8,128)(2,1)S(1)} %shard_map.116.refs_2_), channel_id=1, source_target_pairs={{0,1},{1,0},{2,3},{3,2},{4,5},{5,4},{6,7},{7,6},{8,9},{9,8},{10,11... | collective-permute-start | bytes 700424 | tf_op jit(solution)/shard_map/ppermute | solution.py:347
  10.1 6.4 %collective-permute-start.5 = (bf16[400,128]{1,0:T(8,128)(2,1)S(1)}, bf16[400,128]{1,0:T(8,128)(2,1)S(1)}, u32[]{:S(2)}, u32[]{:S(2)}) collective-permute-start(bf16[400,128]{1,0:T(8,128)(2,1)S(1)} %get-tuple-element.40), channel_id=1, source_target_pairs={{0,2},{1,3},{2,0},{3,1},{4,6},{5,7},{6,4},{7,5},{8,10},{9,11},{10,... | collective-permute-start | bytes 307208 | tf_op jit(solution)/shard_map/ppermute | solution.py:347
  12.6 5.5 %collective-permute-start.6 = (bf16[400,128]{1,0:T(8,128)(2,1)S(1)}, bf16[400,128]{1,0:T(8,128)(2,1)S(1)}, u32[]{:S(2)}, u32[]{:S(2)}) collective-permute-start(bf16[400,128]{1,0:T(8,128)(2,1)S(1)} %get-tuple-element.41), channel_id=1, source_target_pairs={{0,3},{1,2},{2,1},{3,0},{4,7},{5,6},{6,5},{7,4},{8,11},{9,10},{10,... | collective-permute-start | bytes 307208 | tf_op jit(solution)/shard_map/ppermute | solution.py:347
  12.6 10.0 %collective-permute-start.7 = (bf16[512,128]{1,0:T(8,128)(2,1)S(1)}, bf16[512,128]{1,0:T(8,128)(2,1)S(1)}, u32[]{:S(2)}, u32[]{:S(2)}) collective-permute-start(bf16[512,128]{1,0:T(8,128)(2,1)S(1)} %get-tuple-element.42), channel_id=1, source_target_pairs={{0,2},{1,3},{2,0},{3,1},{4,6},{5,7},{6,4},{7,5},{8,10},{9,11},{10,... | collective-permute-start | bytes 393224 | tf_op jit(solution)/shard_map/ppermute | solution.py:347
  14.1 9.4 %collective-permute-start.8 = (bf16[512,128]{1,0:T(8,128)(2,1)S(1)}, bf16[512,128]{1,0:T(8,128)(2,1)S(1)}, u32[]{:S(2)}, u32[]{:S(2)}) collective-permute-start(bf16[512,128]{1,0:T(8,128)(2,1)S(1)} %get-tuple-element.43), channel_id=1, source_target_pairs={{0,3},{1,2},{2,1},{3,0},{4,7},{5,6},{6,5},{7,4},{8,11},{9,10},{10,... | collective-permute-start | bytes 393224 | tf_op jit(solution)/shard_map/ppermute | solution.py:347
  16.5 4.2 %copy-start.4 = (bf16[128,128]{1,0:T(8,128)(2,1)S(1)}, bf16[128,128]{1,0:T(8,128)(2,1)}, u32[]{:S(2)}) copy-start(bf16[128,128]{1,0:T(8,128)(2,1)} %dense.1) | copy-start | bytes 98308
  16.5 4.2 %copy-start.7 = (s32[128,16]{0,1:T(8,128)S(1)}, s32[128,16]{0,1:T(8,128)}, u32[]{:S(2)}) copy-start(s32[128,16]{0,1:T(8,128)} %param.11) | copy-start | bytes 24580
  18.1 5.3 %collective-permute-start.9 = (bf16[64,128]{1,0:T(8,128)(2,1)S(1)}, bf16[64,128]{1,0:T(8,128)(2,1)S(1)}, u32[]{:S(2)}, u32[]{:S(2)}) collective-permute-start(bf16[64,128]{1,0:T(8,128)(2,1)S(1)} %shard_map.119.group.refs_1_), channel_id=1, source_target_pairs={{16,0},{20,4},{24,8},{28,12},{0,16},{4,20},{8,24},{12,28},{17,1},{... | collective-permute-start | bytes 49160 | tf_op jit(solution)/shard_map/ppermute | solution.py:430
  26.3 13.5 %collective-permute-start.13 = (bf16[256,128]{1,0:T(8,128)(2,1)S(1)}, bf16[256,128]{1,0:T(8,128)(2,1)S(1)}, u32[]{:S(2)}, u32[]{:S(2)}) collective-permute-start(bf16[256,128]{1,0:T(8,128)(2,1)S(1)} %get-tuple-element.59._), channel_id=1, source_target_pairs={{0,2},{1,3},{2,0},{3,1},{4,6},{5,7},{6,4},{7,5},{8,10},{9,11},{10,... | collective-permute-start | bytes 196616 | tf_op jit(solution)/shard_map/ppermute | solution.py:347
  27.4 6.4 %collective-permute-start.12 = (bf16[640,128]{1,0:T(8,128)(2,1)S(1)}, bf16[640,128]{1,0:T(8,128)(2,1)S(1)}, u32[]{:S(2)}, u32[]{:S(2)}) collective-permute-start(bf16[640,128]{1,0:T(8,128)(2,1)S(1)} %shard_map.128), channel_id=1, source_target_pairs={{0,3},{1,2},{2,1},{3,0},{4,7},{5,6},{6,5},{7,4},{8,11},{9,10},{10,... | collective-permute-start | bytes 491528 | tf_op jit(solution)/shard_map/ppermute | solution.py:347
  27.8 10.2 %collective-permute-start.10 = (bf16[896,128]{1,0:T(8,128)(2,1)S(1)}, bf16[896,128]{1,0:T(8,128)(2,1)S(1)}, u32[]{:S(2)}, u32[]{:S(2)}) collective-permute-start(bf16[896,128]{1,0:T(8,128)(2,1)S(1)} %get-tuple-element.61), channel_id=1, source_target_pairs={{0,1},{1,0},{2,3},{3,2},{4,5},{5,4},{6,7},{7,6},{8,9},{9,8},{10,11... | collective-permute-start | bytes 688136 | tf_op jit(solution)/shard_map/ppermute | solution.py:347
  28.5 9.5 %collective-permute-start.11 = (bf16[640,128]{1,0:T(8,128)(2,1)S(1)}, bf16[640,128]{1,0:T(8,128)(2,1)S(1)}, u32[]{:S(2)}, u32[]{:S(2)}) collective-permute-start(bf16[640,128]{1,0:T(8,128)(2,1)S(1)} %get-tuple-element.62), channel_id=1, source_target_pairs={{0,2},{1,3},{2,0},{3,1},{4,6},{5,7},{6,4},{7,5},{8,10},{9,11},{10,... | collective-permute-start | bytes 491528 | tf_op jit(solution)/shard_map/ppermute | solution.py:347
  29.5 10.3 %collective-permute-start.14 = (bf16[256,128]{1,0:T(8,128)(2,1)S(1)}, bf16[256,128]{1,0:T(8,128)(2,1)S(1)}, u32[]{:S(2)}, u32[]{:S(2)}) collective-permute-start(bf16[256,128]{1,0:T(8,128)(2,1)S(1)} %get-tuple-element.64), channel_id=1, source_target_pairs={{0,3},{1,2},{2,1},{3,0},{4,7},{5,6},{6,5},{7,4},{8,11},{9,10},{10,... | collective-permute-start | bytes 196616 | tf_op jit(solution)/shard_map/ppermute | solution.py:347

commit v6 on v5

--- a/solution.py
+++ b/solution.py
@@ -266,41 +266,26 @@
     )
 
 
-def scatter_kernel(span, later, owners, pad, *refs):
+def near_scatter_kernel(slots, pad, *refs):
     lines = refs[0]
-    near = refs[1 : 1 + NEAR]
-    far = refs[1 + NEAR : 1 + owners]
-    out, rest, held, sems = refs[1 + owners :]
-    rows = out.shape[2]
+    near, out = refs[1:-1], refs[-1]
     batch = lines.shape[1]
-    first, count = span
-    copies = []
-    for step in range(count):
-        slot = first + step
+    for slot in range(slots):
         grads = [ref[slot * batch : (slot + 1) * batch, :] for ref in near]
-        grads += [ref[step * batch : (step + 1) * batch, :] for ref in far]
-        held[step] = summed(lines, range(owners), slot, grads, pad, rows)
-        copies.append(pltpu.make_async_copy(held.at[step], out.at[0, slot], sems.at[step]))
-        copies[-1].start()
-    for step in range(later[1]):
-        slot = later[0] + step
-        grads = [ref[slot * batch : (slot + 1) * batch, :] for ref in near]
-        rest[step] = summed(lines, range(NEAR), slot, grads, pad, rows)
-    for copy in copies:
-        copy.wait()
-
-
-def last_kernel(span, owners, pad, *refs):
-    lines, rest = refs[:2]
+        out[slot] = summed(lines, range(NEAR), slot, grads, pad, out.shape[1])
+
+
+def far_scatter_kernel(span, owners, pad, *refs):
+    lines, near = refs[:2]
     far = refs[2 : 2 + owners - NEAR]
-    out, held, sems = refs[3 + owners - NEAR :]
+    out, held, sems = refs[-3:]
     rows = out.shape[2]
     batch = lines.shape[1]
     copies = []
     for step in range(span[1]):
         slot = span[0] + step
         grads = [ref[step * batch : (step + 1) * batch, :] for ref in far]
-        held[step] = rest[step] + summed(lines, range(NEAR, owners), slot, grads, pad, rows)
+        held[step] = near[slot] + summed(lines, range(NEAR, owners), slot, grads, pad, rows)
         copies.append(pltpu.make_async_copy(held.at[step], out.at[0, slot], sems.at[step]))
         copies[-1].start()
     for copy in copies:
@@ -496,33 +481,30 @@
         mib=6,
     )
 
-    (first, count), later = grad_spans
-    grads_shape = shape(1, slots, table_rows, width, dtype=F32)
-    table_grad, rest = pl.pallas_call(
-        functools.partial(scatter_kernel, grad_spans[0], later, owners, pad),
-        out_shape=[grads_shape, shape(later[1], table_rows, width, dtype=F32)],
-        in_specs=[VMEM] * (1 + owners),
-        out_specs=[pl.BlockSpec(memory_space=pl.ANY), VMEM],
-        scratch_shapes=[
-            pltpu.VMEM((count, table_rows, width), F32),
-            pltpu.SemaphoreType.DMA((count,)),
-        ],
-        compiler_params=pltpu.CompilerParams(vmem_limit_bytes=6 << 20),
-        name="scatter",
-    )(lines, *near_grads, *far_grads[0])
-    table_grad = pl.pallas_call(
-        functools.partial(last_kernel, later, owners, pad),
-        out_shape=grads_shape,
-        in_specs=[VMEM] * (2 + far_count) + [pl.BlockSpec(memory_space=pl.ANY)],
-        out_specs=pl.BlockSpec(memory_space=pl.ANY),
-        scratch_shapes=[
-            pltpu.VMEM((later[1], table_rows, width), F32),
-            pltpu.SemaphoreType.DMA((later[1],)),
-        ],
-        input_output_aliases={2 + far_count: 0},
-        compiler_params=pltpu.CompilerParams(vmem_limit_bytes=6 << 20),
-        name="last",
-    )(lines, rest, *far_grads[1], table_grad)
+    (near_sums,) = call(
+        functools.partial(near_scatter_kernel, slots, pad),
+        [shape(slots, table_rows, width, dtype=F32)],
+        [lines, *near_grads],
+        mib=6,
+    )
+    table_grad = []
+    for chunk, (first, count) in enumerate(grad_spans):
+        table_grad = [
+            pl.pallas_call(
+                functools.partial(far_scatter_kernel, (first, count), owners, pad),
+                out_shape=shape(1, slots, table_rows, width, dtype=F32),
+                in_specs=[VMEM] * (2 + far_count)
+                + [pl.BlockSpec(memory_space=pl.ANY)] * len(table_grad),
+                out_specs=pl.BlockSpec(memory_space=pl.ANY),
+                scratch_shapes=[
+                    pltpu.VMEM((count, table_rows, width), F32),
+                    pltpu.SemaphoreType.DMA((count,)),
+                ],
+                input_output_aliases={2 + far_count: 0} if table_grad else {},
+                compiler_params=pltpu.CompilerParams(vmem_limit_bytes=6 << 20),
+            )(lines, near_sums, *far_grads[chunk], *table_grad)
+        ]
+    (table_grad,) = table_grad
     return crossed, table_grad
 
 

time: 41.1 us -> 40.7 us (level)
  waiting for transfers between devices: 9.65 us -> 9.01 us
    ppermute x13, waiting for transfers between devices: 9.64 us -> 9 us  [swap(): return lax.ppermute(array, 'table', [(i, i ^ k) for i in range(owners)])]
    pallas_call x16 -> x17, Pallas kernels: 12 us -> 12.7 us  [call(): pl.pallas_call(kernel, out_shape=shapes, in_specs=[VMEM] * len(operands)...]
    pallas_call x2, Pallas kernels: 2.91 us -> 2.49 us  [on_device(): pl.pallas_call(functools.partial(far_scatter_kernel, (first, count), owne...]
where the time goes in v6:
time: 40.7 us; the launch traced here: 40.5 us
  starting transfers between devices  15.5 us (38%)
  Pallas kernels  15.2 us (37%)
  waiting for transfers between devices  9.01 us (22%)
  between operations  0.83 us (2%)
    pallas_call x17, Pallas kernels, call(): pl.pallas_call(kernel, out_shape=shapes, in_specs=[VMEM] * len(operands)...  12.7 us
    ppermute x13, starting transfers between devices, swap(): return lax.ppermute(array, 'table', [(i, i ^ k) for i in range(owners)])  11.6 us
    ppermute x13, waiting for transfers between devices, swap(): return lax.ppermute(array, 'table', [(i, i ^ k) for i in range(owners)])  9 us
    ppermute x1, starting transfers between devices, on_device(): shards.append(lax.ppermute(group, 'blk', pairs))  2.59 us
    pallas_call x2, Pallas kernels, on_device(): pl.pallas_call(functools.partial(far_scatter_kernel, (first, count), owne...  2.49 us
    ppermute x1, starting transfers between devices, on_device(): lax.ppermute(hot_slab, ('blk', 'table'), [(peer(b, t, blocks) * owners +...  1.33 us
  transfers between devices with their start and end apart: 15, of which 6 were waited for; matrix products, arithmetic and copies ran while one was open for 0% of the time, Pallas kernels for 26%

profile of v6, /device:TPU:0, one launch (start us, length us, event | category | flops | bytes accessed | tf_op | source)
XLA Modules:
  0.0 40.5 jit_solution(11361657903871463548)
XLA Ops:
  0.7 0.6 %collective-permute-start = (s32[26,128]{1,0:T(8,128)}, s32[26,128]{1,0:T(8,128)S(1)}, u32[]{:S(2)}, u32[]{:S(2)}) collective-permute-start(s32[26,128]{1,0:T(8,128)} %bitcast.3), channel_id=1, source_target_pairs={{0,1},{1,0},{2,3},{3,2},{4,5},{5,4},{6,7},{7,6},{8,9},{9,8},{10,11... | collective-permute-start | bytes 39944 | tf_op jit(solution)/shard_map/ppermute | solution.py:332
  1.2 2.6 %collective-permute-start.1 = (s32[26,128]{1,0:T(8,128)}, s32[26,128]{1,0:T(8,128)S(1)}, u32[]{:S(2)}, u32[]{:S(2)}) collective-permute-start(s32[26,128]{1,0:T(8,128)} %bitcast.4), channel_id=1, source_target_pairs={{0,2},{1,3},{2,0},{3,1},{4,6},{5,7},{6,4},{7,5},{8,10},{9,11},{10,... | collective-permute-start | bytes 39944 | tf_op jit(solution)/shard_map/ppermute | solution.py:332
  3.8 0.0 collective-permute-start.2
  3.8 1.3 %collective-permute-start.3 = (bf16[16,128]{1,0:T(8,128)(2,1)}, bf16[16,128]{1,0:T(8,128)(2,1)S(1)}, u32[]{:S(2)}, u32[]{:S(2)}) collective-permute-start(bf16[16,128]{1,0:T(8,128)(2,1)} %param.10), channel_id=1, source_target_pairs={{0,0},{5,1},{10,2},{15,3},{4,4},{1,5},{14,6},{11,7},{8,8},{13,9},{... | collective-permute-start | bytes 12296 | tf_op jit(solution)/shard_map/ppermute | solution.py:343
  5.2 0.0 copy-start.6
  5.2 0.0 collective-permute-done.refs_3_
  5.2 0.5 %collective-permute-done.1.refs_4_ = s32[26,128]{1,0:T(8,128)S(1)} collective-permute-done((s32[26,128]{1,0:T(8,128)}, s32[26,128]{1,0:T(8,128)S(1)}, u32[]{:S(2)}, u32[]{:S(2)}) %collective-permute-start.1) | collective-permute-done | bytes 13344 | tf_op jit(solution)/shard_map/ppermute | solution.py:332
  5.7 1.4 %collective-permute-done.2.refs_5_ = s32[26,128]{1,0:T(8,128)S(1)} collective-permute-done((s32[26,128]{1,0:T(8,128)}, s32[26,128]{1,0:T(8,128)S(1)}, u32[]{:S(2)}, u32[]{:S(2)}) %collective-permute-start.2) | collective-permute-done | bytes 13344 | tf_op jit(solution)/shard_map/ppermute | solution.py:332
  7.2 1.3 %shard_map.114 = (s32[32,128]{1,0:T(8,128)S(1)}, s32[8,128]{1,0:T(8,128)S(1)}, bf16[400,128]{1,0:T(8,128)(2,1)S(1)}, bf16[400,128]{1,0:T(8,128)(2,1)S(1)}) custom-call(s32[26]{0:T(128)S(1)} %copy-done.8, s32[8,128]{1,0:T(8,128)S(1)} %shard_map.113.refs_1_, s32[26,128]{1,0:T(8,128)S(1)} %bitcast.6, s32[26,128]{1,0:T(8,128)S(1)} %collective-permute-done.refs_3_, ...), custom_call_target="tpu_custom_call" | custom-call | flops 1000000000 | bytes 1048576 | tf_op jit(solution)/shard_map/pallas_call | solution.py:320
  8.5 0.6 %shard_map.115 = (s32[8,128]{1,0:T(8,128)S(1)}, bf16[512,128]{1,0:T(8,128)(2,1)S(1)}, bf16[512,128]{1,0:T(8,128)(2,1)S(1)}) custom-call(s32[32,128]{1,0:T(8,128)S(1)} %get-tuple-element.33.lines.refs_1_.refs_0_, bf16[7,512,128]{2,1,0:T(8,128)(2,1)S(1)} %copy-done.2), custom_call_target="tpu_custom_call" | custom-call | flops 500000000 | bytes 1048576 | tf_op jit(solution)/shard_map/pallas_call | solution.py:320
  9.0 0.0 collective-permute-done.3.shard.refs_0_
  9.0 0.5 %shard_map.116.refs_2_ = bf16[912,128]{1,0:T(8,128)(2,1)S(1)} custom-call(s32[32,128]{1,0:T(8,128)S(1)} %get-tuple-element.33.lines.refs_1_.refs_0_, s32[8,128]{1,0:T(8,128)S(1)} %get-tuple-element.34._, bf16[7,512,128]{2,1,0:T(8,128)(2,1)S(1)} %copy-done.2, bf16[16,128]{1,0:T(8,128)(2,1)S(1)} %collective-permute-done.3.shard.refs_0_), custom_call_target="tpu_custom_call" | custom-call | flops 500000000 | bytes 1048576 | tf_op jit(solution)/shard_map/pallas_call | solution.py:320
  9.6 0.5 %collective-permute-start.4 = (bf16[912,128]{1,0:T(8,128)(2,1)S(1)}, bf16[912,128]{1,0:T(8,128)(2,1)S(1)}, u32[]{:S(2)}, u32[]{:S(2)}) collective-permute-start(bf16[912,128]{1,0:T(8,128)(2,1)S(1)} %shard_map.116.refs_2_), channel_id=1, source_target_pairs={{0,1},{1,0},{2,3},{3,2},{4,5},{5,4},{6,7},{7,6},{8,9},{9,8},{10,11... | collective-permute-start | bytes 700424 | tf_op jit(solution)/shard_map/ppermute | solution.py:332
  10.1 2.5 %collective-permute-start.5 = (bf16[400,128]{1,0:T(8,128)(2,1)S(1)}, bf16[400,128]{1,0:T(8,128)(2,1)S(1)}, u32[]{:S(2)}, u32[]{:S(2)}) collective-permute-start(bf16[400,128]{1,0:T(8,128)(2,1)S(1)} %get-tuple-element.38), channel_id=1, source_target_pairs={{0,2},{1,3},{2,0},{3,1},{4,6},{5,7},{6,4},{7,5},{8,10},{9,11},{10,... | collective-permute-start | bytes 307208 | tf_op jit(solution)/shard_map/ppermute | solution.py:332
  12.6 0.0 collective-permute-start.6
  12.6 1.4 %collective-permute-start.7 = (bf16[512,128]{1,0:T(8,128)(2,1)S(1)}, bf16[512,128]{1,0:T(8,128)(2,1)S(1)}, u32[]{:S(2)}, u32[]{:S(2)}) collective-permute-start(bf16[512,128]{1,0:T(8,128)(2,1)S(1)} %get-tuple-element.40), channel_id=1, source_target_pairs={{0,2},{1,3},{2,0},{3,1},{4,6},{5,7},{6,4},{7,5},{8,10},{9,11},{10,... | collective-permute-start | bytes 393224 | tf_op jit(solution)/shard_map/ppermute | solution.py:332
  14.1 0.3 collective-permute-start.8
  14.4 2.1 %shard_map.117 = (bf16[896,128]{1,0:T(8,128)(2,1)S(1)}, bf16[3712,512]{1,0:T(8,128)(2,1)S(1)}, bf16[512,3712]{1,0:T(8,128)(2,1)S(1)}, bf16[128,3712]{1,0:T(8,128)(2,1)S(1)}, f32[32,128]{1,0:T(8,128)S(1)}) custom-call(s32[8,128]{1,0:T(8,128)S(1)} %get-tuple-element.32.refs_0_, s32[32,128]{1,0:T(8,128)S(1)} %get-tuple-element.33.lines.refs_1_.refs_0_, ...), custom_call_target="tpu_custom_call" | custom-call | flops 4000000000 | bytes 1048576 | tf_op jit(solution)/shard_map/pallas_call | solution.py:320
  16.5 0.0 copy-start.4
  16.5 0.0 copy-start.7
  16.5 0.0 collective-permute-done.5.refs_2_.refs_0_.refs_3_
  16.5 1.6 %collective-permute-done.6.refs_3_.refs_1_.refs_4_ = bf16[400,128]{1,0:T(8,128)(2,1)S(1)} collective-permute-done((bf16[400,128]{1,0:T(8,128)(2,1)S(1)}, bf16[400,128]{1,0:T(8,128)(2,1)S(1)}, u32[]{:S(2)}, u32[]{:S(2)}) %collective-permute-start.6) | collective-permute-done | bytes 102432 | tf_op jit(solution)/shard_map/ppermute | solution.py:332
  18.1 0.0 collective-permute-done.4.refs_1_.refs_2_
  18.1 2.6 %collective-permute-start.9 = (bf16[64,128]{1,0:T(8,128)(2,1)S(1)}, bf16[64,128]{1,0:T(8,128)(2,1)S(1)}, u32[]{:S(2)}, u32[]{:S(2)}) collective-permute-start(bf16[64,128]{1,0:T(8,128)(2,1)S(1)} %shard_map.119.group.refs_1_), channel_id=1, source_target_pairs={{16,0},{20,4},{24,8},{28,12},{0,16},{4,20},{8,24},{12,28},{17,1},{... | collective-permute-start | bytes 49160 | tf_op jit(solution)/shard_map/ppermute | solution.py:415
  20.7 0.3 shard_map.120
  21.0 1.0 %shard_map.121 = (f32[128,512]{1,0:T(8,128)S(1)}, f32[128,512]{1,0:T(8,128)S(1)}) custom-call(bf16[896,128]{1,0:T(8,128)(2,1)S(1)} %get-tuple-element.35.refs_0_.refs_1_, bf16[912,128]{1,0:T(8,128)(2,1)S(1)} %collective-permute-done.4.refs_1_.refs_2_, bf16[3712,512]{1,0:T(8,128)(2,1)S(1)} %get-tuple-element.44.refs_2_.refs_1_.refs_7_.down, ...), custom_call_target="tpu_custom_call" | custom-call | flops 4000000000 | bytes 1048576 | tf_op jit(solution)/shard_map/pallas_call | solution.py:320
  22.1 0.6 %shard_map.122 = (f32[128,512]{1,0:T(8,128)S(1)}, f32[128,512]{1,0:T(8,128)S(1)}) custom-call(bf16[400,128]{1,0:T(8,128)(2,1)S(1)} %collective-permute-done.5.refs_2_.refs_0_.refs_3_, bf16[400,128]{1,0:T(8,128)(2,1)S(1)} %collective-permute-done.6.refs_3_.refs_1_.refs_4_, bf16[3712,512]{1,0:T(8,128)(2,1)S(1)} %get-tuple-element.44.refs_2_.refs_1_.refs_7_.down, ...), custom_call_target="tpu_custom_call" | custom-call | flops 4000000000 | bytes 1048576 | tf_op jit(solution)/shard_map/pallas_call | solution.py:320
  22.6 0.0 collective-permute-done.7.refs_0_.refs_5_
  22.6 0.4 shard_map.123
  23.0 0.4 collective-permute-done.8.refs_0_.refs_6_
  23.4 0.0 collective-permute-done.9.refs_2_
  23.4 1.0 %shard_map.124 = (bf16[128,128]{1,0:T(8,128)(2,1)S(1)}, bf16[128,512]{1,0:T(8,128)(2,1)S(1)}, bf16[128,512]{1,0:T(8,128)(2,1)S(1)}, bf16[640,128]{1,0:T(8,128)(2,1)S(1)}) custom-call(bf16[512,128]{1,0:T(8,128)(2,1)S(1)} %collective-permute-done.8.refs_0_.refs_6_, bf16[64,128]{1,0:T(8,128)(2,1)S(1)} %shard_map.119.group.refs_1_, ...), custom_call_target="tpu_custom_call" | custom-call | flops 4000000000 | bytes 1048576 | tf_op jit(solution)/shard_map/pallas_call | solution.py:320
  24.4 0.5 %shard_map.129 = bf16[640,128]{1,0:T(8,128)(2,1)S(1)} custom-call(bf16[128,512]{1,0:T(8,128)(2,1)S(1)} %get-tuple-element.55.low.refs_8_, bf16[128,512]{1,0:T(8,128)(2,1)S(1)} %get-tuple-element.56.grad, bf16[3712,512]{1,0:T(8,128)(2,1)S(1)} %get-tuple-element.44.refs_2_.refs_1_.refs_7_.down, ...), custom_call_target="tpu_custom_call" | custom-call | flops 4000000000 | bytes 1048576 | tf_op jit(solution)/shard_map/pallas_call | solution.py:320
  24.9 0.4 shard_map.125
  25.3 1.0 %shard_map.126 = (bf16[896,128]{1,0:T(8,128)(2,1)S(1)}, bf16[896,128]{1,0:T(8,128)(2,1)S(1)}) custom-call(bf16[128,512]{1,0:T(8,128)(2,1)S(1)} %get-tuple-element.55.low.refs_8_, bf16[128,512]{1,0:T(8,128)(2,1)S(1)} %get-tuple-element.56.grad, bf16[3712,512]{1,0:T(8,128)(2,1)S(1)} %get-tuple-element.44.refs_2_.refs_1_.refs_7_.down, ...), custom_call_target="tpu_custom_call" | custom-call | flops 4000000000 | bytes 1048576 | tf_op jit(solution)/shard_map/pallas_call | solution.py:320
  26.3 1.1 %collective-permute-start.11 = (bf16[256,128]{1,0:T(8,128)(2,1)S(1)}, bf16[256,128]{1,0:T(8,128)(2,1)S(1)}, u32[]{:S(2)}, u32[]{:S(2)}) collective-permute-start(bf16[256,128]{1,0:T(8,128)(2,1)S(1)} %get-tuple-element.57._), channel_id=1, source_target_pairs={{0,2},{1,3},{2,0},{3,1},{4,6},{5,7},{6,4},{7,5},{8,10},{9,11},{10,... | collective-permute-start | bytes 196616 | tf_op jit(solution)/shard_map/ppermute | solution.py:332
  27.4 0.5 %collective-permute-start.14 = (bf16[640,128]{1,0:T(8,128)(2,1)S(1)}, bf16[640,128]{1,0:T(8,128)(2,1)S(1)}, u32[]{:S(2)}, u32[]{:S(2)}) collective-permute-start(bf16[640,128]{1,0:T(8,128)(2,1)S(1)} %shard_map.129), channel_id=1, source_target_pairs={{0,3},{1,2},{2,1},{3,0},{4,7},{5,6},{6,5},{7,4},{8,11},{9,10},{10,... | collective-permute-start | bytes 491528 | tf_op jit(solution)/shard_map/ppermute | solution.py:332
  27.8 0.7 %collective-permute-start.10 = (bf16[896,128]{1,0:T(8,128)(2,1)S(1)}, bf16[896,128]{1,0:T(8,128)(2,1)S(1)}, u32[]{:S(2)}, u32[]{:S(2)}) collective-permute-start(bf16[896,128]{1,0:T(8,128)(2,1)S(1)} %get-tuple-element.59), channel_id=1, source_target_pairs={{0,1},{1,0},{2,3},{3,2},{4,5},{5,4},{6,7},{7,6},{8,9},{9,8},{10,11... | collective-permute-start | bytes 688136 | tf_op jit(solution)/shard_map/ppermute | solution.py:332
  28.5 1.0 %collective-permute-start.13 = (bf16[640,128]{1,0:T(8,128)(2,1)S(1)}, bf16[640,128]{1,0:T(8,128)(2,1)S(1)}, u32[]{:S(2)}, u32[]{:S(2)}) collective-permute-start(bf16[640,128]{1,0:T(8,128)(2,1)S(1)} %get-tuple-element.61), channel_id=1, source_target_pairs={{0,2},{1,3},{2,0},{3,1},{4,6},{5,7},{6,4},{7,5},{8,10},{9,11},{10,... | collective-permute-start | bytes 491528 | tf_op jit(solution)/shard_map/ppermute | solution.py:332
  29.5 0.3 collective-permute-start.12
  29.9 2.4 %shard_map.127 = bf16[128,3456]{1,0:T(8,128)(2,1)} custom-call(s32[8,128]{1,0:T(8,128)S(1)} %get-tuple-element.32.refs_0_, bf16[896,128]{1,0:T(8,128)(2,1)S(1)} %get-tuple-element.35.refs_0_.refs_1_, bf16[912,128]{1,0:T(8,128)(2,1)S(1)} %collective-permute-done.4.refs_1_.refs_2_, bf16[400,128]{1,0:T(8,128)(2,1)S(1)} %collective-permute-done.5.refs_2_.refs_0_.refs_3_, ...), custom_call_target="tpu_custom_call" | custom-call | flops 4000000000 | bytes 1048576 | tf_op jit(solution)/shard_map/pallas_call | solution.py:320
  32.3 0.0 collective-permute-done.10.refs_2_
  32.3 0.6 %shard_map.128.refs_1_ = f32[7,512,128]{2,1,0:T(8,128)S(1)} custom-call(s32[32,128]{1,0:T(8,128)S(1)} %get-tuple-element.33.lines.refs_1_.refs_0_, bf16[896,128]{1,0:T(8,128)(2,1)S(1)} %get-tuple-element.58.refs_11_.refs_1_, bf16[896,128]{1,0:T(8,128)(2,1)S(1)} %collective-permute-done.10.refs_2_), custom_call_target="tpu_custom_call" | custom-call | flops 4000000000 | bytes 1048576 | tf_op jit(solution)/shard_map/pallas_call | solution.py:320
  33.0 0.9 %collective-permute-done.14.refs_3_ = bf16[640,128]{1,0:T(8,128)(2,1)S(1)} collective-permute-done((bf16[640,128]{1,0:T(8,128)(2,1)S(1)}, bf16[640,128]{1,0:T(8,128)(2,1)S(1)}, u32[]{:S(2)}, u32[]{:S(2)}) %collective-permute-start.14) | collective-permute-done | bytes 163872 | tf_op jit(solution)/shard_map/ppermute | solution.py:332
  33.8 4.2 %collective-permute-done.13.refs_2_ = bf16[640,128]{1,0:T(8,128)(2,1)S(1)} collective-permute-done((bf16[640,128]{1,0:T(8,128)(2,1)S(1)}, bf16[640,128]{1,0:T(8,128)(2,1)S(1)}, u32[]{:S(2)}, u32[]{:S(2)}) %collective-permute-start.13) | collective-permute-done | bytes 163872 | tf_op jit(solution)/shard_map/ppermute | solution.py:332
  38.0 1.4 %shard_map.130.refs_4_ = f32[1,7,512,128]{3,2,1,0:T(8,128)} custom-call(s32[32,128]{1,0:T(8,128)S(1)} %get-tuple-element.33.lines.refs_1_.refs_0_, f32[7,512,128]{2,1,0:T(8,128)S(1)} %shard_map.128.refs_1_, bf16[640,128]{1,0:T(8,128)(2,1)S(1)} %collective-permute-done.13.refs_2_, bf16[640,128]{1,0:T(8,128)(2,1)S(1)} %collective-permute-done.14.refs_3_), custom_call_target="tpu_custom_call" | custom-call | tf_op jit(solution)/shard_map/pallas_call | solution.py:493
  39.4 0.0 collective-permute-done.12.refs_3_
  39.4 1.1 %shard_map.131 = f32[1,7,512,128]{3,2,1,0:T(8,128)} custom-call(s32[32,128]{1,0:T(8,128)S(1)} %get-tuple-element.33.lines.refs_1_.refs_0_, f32[7,512,128]{2,1,0:T(8,128)S(1)} %shard_map.128.refs_1_, bf16[256,128]{1,0:T(8,128)(2,1)S(1)} %collective-permute-done.11.refs_2_, ...), custom_call_target="tpu_custom_call", output_to_operand_aliasing={{}: (4, {})} | custom-call | tf_op jit(solution)/shard_map/pallas_call | solution.py:493
  (19 shorter events, 0.0 us)
Async XLA Ops:
  0.6 6.5 %copy-start.2 = (bf16[7,512,128]{2,1,0:T(8,128)(2,1)S(1)}, bf16[7,512,128]{2,1,0:T(8,128)(2,1)}, u32[]{:S(2)}) copy-start(bf16[7,512,128]{2,1,0:T(8,128)(2,1)} %refs_3_.1) | copy-start | bytes 2752516
  0.6 6.5 %copy-start.5 = (s32[128,26]{0,1:T(8,128)S(1)}, s32[128,26]{0,1:T(8,128)}, u32[]{:S(2)}) copy-start(s32[128,26]{0,1:T(8,128)} %param.13) | copy-start | bytes 39940
  0.7 6.5 %copy-start.8 = (s32[26]{0:T(128)S(1)}, s32[26]{0:T(128)}, u32[]{:S(2)}) copy-start(s32[26]{0:T(128)} %refs_0_.1) | copy-start | bytes 316
  0.7 4.5 %collective-permute-start = (s32[26,128]{1,0:T(8,128)}, s32[26,128]{1,0:T(8,128)S(1)}, u32[]{:S(2)}, u32[]{:S(2)}) collective-permute-start(s32[26,128]{1,0:T(8,128)} %bitcast.3), channel_id=1, source_target_pairs={{0,1},{1,0},{2,3},{3,2},{4,5},{5,4},{6,7},{7,6},{8,9},{9,8},{10,11... | collective-permute-start | bytes 39944 | tf_op jit(solution)/shard_map/ppermute | solution.py:332
  1.2 4.5 %collective-permute-start.1 = (s32[26,128]{1,0:T(8,128)}, s32[26,128]{1,0:T(8,128)S(1)}, u32[]{:S(2)}, u32[]{:S(2)}) collective-permute-start(s32[26,128]{1,0:T(8,128)} %bitcast.4), channel_id=1, source_target_pairs={{0,2},{1,3},{2,0},{3,1},{4,6},{5,7},{6,4},{7,5},{8,10},{9,11},{10,... | collective-permute-start | bytes 39944 | tf_op jit(solution)/shard_map/ppermute | solution.py:332
  3.8 3.4 %collective-permute-start.2 = (s32[26,128]{1,0:T(8,128)}, s32[26,128]{1,0:T(8,128)S(1)}, u32[]{:S(2)}, u32[]{:S(2)}) collective-permute-start(s32[26,128]{1,0:T(8,128)} %bitcast.5), channel_id=1, source_target_pairs={{0,3},{1,2},{2,1},{3,0},{4,7},{5,6},{6,5},{7,4},{8,11},{9,10},{10,... | collective-permute-start | bytes 39944 | tf_op jit(solution)/shard_map/ppermute | solution.py:332
  3.8 5.2 %collective-permute-start.3 = (bf16[16,128]{1,0:T(8,128)(2,1)}, bf16[16,128]{1,0:T(8,128)(2,1)S(1)}, u32[]{:S(2)}, u32[]{:S(2)}) collective-permute-start(bf16[16,128]{1,0:T(8,128)(2,1)} %param.10), channel_id=1, source_target_pairs={{0,0},{5,1},{10,2},{15,3},{4,4},{1,5},{14,6},{11,7},{8,8},{13,9},{... | collective-permute-start | bytes 12296 | tf_op jit(solution)/shard_map/ppermute | solution.py:343
  5.2 9.2 %copy-start.3 = (bf16[128,3456]{1,0:T(8,128)(2,1)S(1)}, bf16[128,3456]{1,0:T(8,128)(2,1)}, u32[]{:S(2)}) copy-start(bf16[128,3456]{1,0:T(8,128)(2,1)} %refs_6_.3) | copy-start | bytes 2654212
  5.2 9.2 %copy-start = (bf16[3456,512]{1,0:T(8,128)(2,1)S(1)}, bf16[3456,512]{1,0:T(8,128)(2,1)}, u32[]{:S(2)}) copy-start(bf16[3456,512]{1,0:T(8,128)(2,1)} %refs_4_.1) | copy-start | bytes 10616836
  5.2 9.2 %copy-start.1 = (bf16[512,3456]{1,0:T(8,128)(2,1)S(1)}, bf16[512,3456]{1,0:T(8,128)(2,1)}, u32[]{:S(2)}) copy-start(bf16[512,3456]{1,0:T(8,128)(2,1)} %refs_5_.1) | copy-start | bytes 10616836
  5.2 9.2 %copy-start.6 = (f32[3456]{0:T(1024)S(1)}, f32[3456]{0:T(1024)}, u32[]{:S(2)}) copy-start(f32[3456]{0:T(1024)} %param.18) | copy-start | bytes 41476
  9.6 8.5 %collective-permute-start.4 = (bf16[912,128]{1,0:T(8,128)(2,1)S(1)}, bf16[912,128]{1,0:T(8,128)(2,1)S(1)}, u32[]{:S(2)}, u32[]{:S(2)}) collective-permute-start(bf16[912,128]{1,0:T(8,128)(2,1)S(1)} %shard_map.116.refs_2_), channel_id=1, source_target_pairs={{0,1},{1,0},{2,3},{3,2},{4,5},{5,4},{6,7},{7,6},{8,9},{9,8},{10,11... | collective-permute-start | bytes 700424 | tf_op jit(solution)/shard_map/ppermute | solution.py:332
  10.1 6.4 %collective-permute-start.5 = (bf16[400,128]{1,0:T(8,128)(2,1)S(1)}, bf16[400,128]{1,0:T(8,128)(2,1)S(1)}, u32[]{:S(2)}, u32[]{:S(2)}) collective-permute-start(bf16[400,128]{1,0:T(8,128)(2,1)S(1)} %get-tuple-element.38), channel_id=1, source_target_pairs={{0,2},{1,3},{2,0},{3,1},{4,6},{5,7},{6,4},{7,5},{8,10},{9,11},{10,... | collective-permute-start | bytes 307208 | tf_op jit(solution)/shard_map/ppermute | solution.py:332
  12.6 5.5 %collective-permute-start.6 = (bf16[400,128]{1,0:T(8,128)(2,1)S(1)}, bf16[400,128]{1,0:T(8,128)(2,1)S(1)}, u32[]{:S(2)}, u32[]{:S(2)}) collective-permute-start(bf16[400,128]{1,0:T(8,128)(2,1)S(1)} %get-tuple-element.39), channel_id=1, source_target_pairs={{0,3},{1,2},{2,1},{3,0},{4,7},{5,6},{6,5},{7,4},{8,11},{9,10},{10,... | collective-permute-start | bytes 307208 | tf_op jit(solution)/shard_map/ppermute | solution.py:332
  12.6 10.0 %collective-permute-start.7 = (bf16[512,128]{1,0:T(8,128)(2,1)S(1)}, bf16[512,128]{1,0:T(8,128)(2,1)S(1)}, u32[]{:S(2)}, u32[]{:S(2)}) collective-permute-start(bf16[512,128]{1,0:T(8,128)(2,1)S(1)} %get-tuple-element.40), channel_id=1, source_target_pairs={{0,2},{1,3},{2,0},{3,1},{4,6},{5,7},{6,4},{7,5},{8,10},{9,11},{10,... | collective-permute-start | bytes 393224 | tf_op jit(solution)/shard_map/ppermute | solution.py:332
  14.1 9.4 %collective-permute-start.8 = (bf16[512,128]{1,0:T(8,128)(2,1)S(1)}, bf16[512,128]{1,0:T(8,128)(2,1)S(1)}, u32[]{:S(2)}, u32[]{:S(2)}) collective-permute-start(bf16[512,128]{1,0:T(8,128)(2,1)S(1)} %get-tuple-element.41), channel_id=1, source_target_pairs={{0,3},{1,2},{2,1},{3,0},{4,7},{5,6},{6,5},{7,4},{8,11},{9,10},{10,... | collective-permute-start | bytes 393224 | tf_op jit(solution)/shard_map/ppermute | solution.py:332
  16.5 4.2 %copy-start.4 = (bf16[128,128]{1,0:T(8,128)(2,1)S(1)}, bf16[128,128]{1,0:T(8,128)(2,1)}, u32[]{:S(2)}) copy-start(bf16[128,128]{1,0:T(8,128)(2,1)} %dense.1) | copy-start | bytes 98308
  16.5 4.2 %copy-start.7 = (s32[128,16]{0,1:T(8,128)S(1)}, s32[128,16]{0,1:T(8,128)}, u32[]{:S(2)}) copy-start(s32[128,16]{0,1:T(8,128)} %param.11) | copy-start | bytes 24580
  18.1 5.3 %collective-permute-start.9 = (bf16[64,128]{1,0:T(8,128)(2,1)S(1)}, bf16[64,128]{1,0:T(8,128)(2,1)S(1)}, u32[]{:S(2)}, u32[]{:S(2)}) collective-permute-start(bf16[64,128]{1,0:T(8,128)(2,1)S(1)} %shard_map.119.group.refs_1_), channel_id=1, source_target_pairs={{16,0},{20,4},{24,8},{28,12},{0,16},{4,20},{8,24},{12,28},{17,1},{... | collective-permute-start | bytes 49160 | tf_op jit(solution)/shard_map/ppermute | solution.py:415
  26.3 13.1 %collective-permute-start.11 = (bf16[256,128]{1,0:T(8,128)(2,1)S(1)}, bf16[256,128]{1,0:T(8,128)(2,1)S(1)}, u32[]{:S(2)}, u32[]{:S(2)}) collective-permute-start(bf16[256,128]{1,0:T(8,128)(2,1)S(1)} %get-tuple-element.57._), channel_id=1, source_target_pairs={{0,2},{1,3},{2,0},{3,1},{4,6},{5,7},{6,4},{7,5},{8,10},{9,11},{10,... | collective-permute-start | bytes 196616 | tf_op jit(solution)/shard_map/ppermute | solution.py:332
  27.4 6.4 %collective-permute-start.14 = (bf16[640,128]{1,0:T(8,128)(2,1)S(1)}, bf16[640,128]{1,0:T(8,128)(2,1)S(1)}, u32[]{:S(2)}, u32[]{:S(2)}) collective-permute-start(bf16[640,128]{1,0:T(8,128)(2,1)S(1)} %shard_map.129), channel_id=1, source_target_pairs={{0,3},{1,2},{2,1},{3,0},{4,7},{5,6},{6,5},{7,4},{8,11},{9,10},{10,... | collective-permute-start | bytes 491528 | tf_op jit(solution)/shard_map/ppermute | solution.py:332
  27.8 4.5 %collective-permute-start.10 = (bf16[896,128]{1,0:T(8,128)(2,1)S(1)}, bf16[896,128]{1,0:T(8,128)(2,1)S(1)}, u32[]{:S(2)}, u32[]{:S(2)}) collective-permute-start(bf16[896,128]{1,0:T(8,128)(2,1)S(1)} %get-tuple-element.59), channel_id=1, source_target_pairs={{0,1},{1,0},{2,3},{3,2},{4,5},{5,4},{6,7},{7,6},{8,9},{9,8},{10,11... | collective-permute-start | bytes 688136 | tf_op jit(solution)/shard_map/ppermute | solution.py:332
  28.5 9.5 %collective-permute-start.13 = (bf16[640,128]{1,0:T(8,128)(2,1)S(1)}, bf16[640,128]{1,0:T(8,128)(2,1)S(1)}, u32[]{:S(2)}, u32[]{:S(2)}) collective-permute-start(bf16[640,128]{1,0:T(8,128)(2,1)S(1)} %get-tuple-element.61), channel_id=1, source_target_pairs={{0,2},{1,3},{2,0},{3,1},{4,6},{5,7},{6,4},{7,5},{8,10},{9,11},{10,... | collective-permute-start | bytes 491528 | tf_op jit(solution)/shard_map/ppermute | solution.py:332
  29.5 9.9 %collective-permute-start.12 = (bf16[256,128]{1,0:T(8,128)(2,1)S(1)}, bf16[256,128]{1,0:T(8,128)(2,1)S(1)}, u32[]{:S(2)}, u32[]{:S(2)}) collective-permute-start(bf16[256,128]{1,0:T(8,128)(2,1)S(1)} %get-tuple-element.60), channel_id=1, source_target_pairs={{0,3},{1,2},{2,1},{3,0},{4,7},{5,6},{6,5},{7,4},{8,11},{9,10},{10,... | collective-permute-start | bytes 196616 | tf_op jit(solution)/shard_map/ppermute | solution.py:332

commit v7 on v6

--- a/solution.py
+++ b/solution.py
@@ -254,9 +254,9 @@
         out[:, (table + 1) * width : (table + 2) * width] = held[meta[1, table]]
 
 
-def summed(lines, masks, slot, grads, pad, rows):
+def summed(lines, masks, slot, grads, pad, rows, first=0):
     batch = lines.shape[1]
-    position = lax.broadcasted_iota(jnp.int32, (rows, batch), 0)
+    position = lax.broadcasted_iota(jnp.int32, (rows, batch), 0) + first
     picks = [
         jnp.where(position == lines[k * pad + slot : k * pad + slot + 1, :], 1.0, 0.0).astype(BF16)
         for k in masks
@@ -285,9 +285,17 @@
     for step in range(span[1]):
         slot = span[0] + step
         grads = [ref[step * batch : (step + 1) * batch, :] for ref in far]
-        held[step] = near[slot] + summed(lines, range(NEAR, owners), slot, grads, pad, rows)
-        copies.append(pltpu.make_async_copy(held.at[step], out.at[0, slot], sems.at[step]))
-        copies[-1].start()
+        half = rows // 2
+        for part in range(2):
+            here = slice(part * half, (part + 1) * half)
+            more = summed(lines, range(NEAR, owners), slot, grads, pad, half, part * half)
+            held[step, here, :] = near[slot, here, :] + more
+            copies.append(
+                pltpu.make_async_copy(
+                    held.at[step, here], out.at[0, slot, here], sems.at[2 * step + part]
+                )
+            )
+            copies[-1].start()
     for copy in copies:
         copy.wait()
 
@@ -498,7 +506,7 @@
                 out_specs=pl.BlockSpec(memory_space=pl.ANY),
                 scratch_shapes=[
                     pltpu.VMEM((count, table_rows, width), F32),
-                    pltpu.SemaphoreType.DMA((count,)),
+                    pltpu.SemaphoreType.DMA((2 * count,)),
                 ],
                 input_output_aliases={2 + far_count: 0} if table_grad else {},
                 compiler_params=pltpu.CompilerParams(vmem_limit_bytes=6 << 20),

time: 40.7 us -> 40.6 us (level)
  no operation moved by 1% of the time
where the time goes in v7:
time: 40.6 us; the launch traced here: 40.4 us
  starting transfers between devices  15.5 us (38%)
  Pallas kernels  15.1 us (37%)
  waiting for transfers between devices  9.01 us (22%)
  between operations  0.83 us (2%)
    pallas_call x17, Pallas kernels, call(): pl.pallas_call(kernel, out_shape=shapes, in_specs=[VMEM] * len(operands)...  12.7 us
    ppermute x13, starting transfers between devices, swap(): return lax.ppermute(array, 'table', [(i, i ^ k) for i in range(owners)])  11.6 us
    ppermute x13, waiting for transfers between devices, swap(): return lax.ppermute(array, 'table', [(i, i ^ k) for i in range(owners)])  9 us
    ppermute x1, starting transfers between devices, on_device(): shards.append(lax.ppermute(group, 'blk', pairs))  2.59 us
    pallas_call x2, Pallas kernels, on_device(): pl.pallas_call(functools.partial(far_scatter_kernel, (first, count), owne...  2.4 us
    ppermute x1, starting transfers between devices, on_device(): lax.ppermute(hot_slab, ('blk', 'table'), [(peer(b, t, blocks) * owners +...  1.33 us
  transfers between devices with their start and end apart: 15, of which 6 were waited for; matrix products, arithmetic and copies ran while one was open for 0% of the time, Pallas kernels for 26%

profile of v7, /device:TPU:0, one launch (start us, length us, event | category | flops | bytes accessed | tf_op | source)
XLA Modules:
  0.0 40.4 jit_solution(3302429590460046258)
XLA Ops:
  0.7 0.6 %collective-permute-start = (s32[26,128]{1,0:T(8,128)}, s32[26,128]{1,0:T(8,128)S(1)}, u32[]{:S(2)}, u32[]{:S(2)}) collective-permute-start(s32[26,128]{1,0:T(8,128)} %bitcast.3), channel_id=1, source_target_pairs={{0,1},{1,0},{2,3},{3,2},{4,5},{5,4},{6,7},{7,6},{8,9},{9,8},{10,11... | collective-permute-start | bytes 39944 | tf_op jit(solution)/shard_map/ppermute | solution.py:340
  1.2 2.6 %collective-permute-start.1 = (s32[26,128]{1,0:T(8,128)}, s32[26,128]{1,0:T(8,128)S(1)}, u32[]{:S(2)}, u32[]{:S(2)}) collective-permute-start(s32[26,128]{1,0:T(8,128)} %bitcast.4), channel_id=1, source_target_pairs={{0,2},{1,3},{2,0},{3,1},{4,6},{5,7},{6,4},{7,5},{8,10},{9,11},{10,... | collective-permute-start | bytes 39944 | tf_op jit(solution)/shard_map/ppermute | solution.py:340
  3.8 0.0 collective-permute-start.2
  3.8 1.3 %collective-permute-start.3 = (bf16[16,128]{1,0:T(8,128)(2,1)}, bf16[16,128]{1,0:T(8,128)(2,1)S(1)}, u32[]{:S(2)}, u32[]{:S(2)}) collective-permute-start(bf16[16,128]{1,0:T(8,128)(2,1)} %param.10), channel_id=1, source_target_pairs={{0,0},{5,1},{10,2},{15,3},{4,4},{1,5},{14,6},{11,7},{8,8},{13,9},{... | collective-permute-start | bytes 12296 | tf_op jit(solution)/shard_map/ppermute | solution.py:351
  5.2 0.0 copy-start.6
  5.2 0.0 collective-permute-done.refs_3_
  5.2 0.5 %collective-permute-done.1.refs_4_ = s32[26,128]{1,0:T(8,128)S(1)} collective-permute-done((s32[26,128]{1,0:T(8,128)}, s32[26,128]{1,0:T(8,128)S(1)}, u32[]{:S(2)}, u32[]{:S(2)}) %collective-permute-start.1) | collective-permute-done | bytes 13344 | tf_op jit(solution)/shard_map/ppermute | solution.py:340
  5.7 1.4 %collective-permute-done.2.refs_5_ = s32[26,128]{1,0:T(8,128)S(1)} collective-permute-done((s32[26,128]{1,0:T(8,128)}, s32[26,128]{1,0:T(8,128)S(1)}, u32[]{:S(2)}, u32[]{:S(2)}) %collective-permute-start.2) | collective-permute-done | bytes 13344 | tf_op jit(solution)/shard_map/ppermute | solution.py:340
  7.2 1.3 %shard_map.114 = (s32[32,128]{1,0:T(8,128)S(1)}, s32[8,128]{1,0:T(8,128)S(1)}, bf16[400,128]{1,0:T(8,128)(2,1)S(1)}, bf16[400,128]{1,0:T(8,128)(2,1)S(1)}) custom-call(s32[26]{0:T(128)S(1)} %copy-done.8, s32[8,128]{1,0:T(8,128)S(1)} %shard_map.113.refs_1_, s32[26,128]{1,0:T(8,128)S(1)} %bitcast.6, s32[26,128]{1,0:T(8,128)S(1)} %collective-permute-done.refs_3_, ...), custom_call_target="tpu_custom_call" | custom-call | flops 1000000000 | bytes 1048576 | tf_op jit(solution)/shard_map/pallas_call | solution.py:328
  8.5 0.6 %shard_map.115 = (s32[8,128]{1,0:T(8,128)S(1)}, bf16[512,128]{1,0:T(8,128)(2,1)S(1)}, bf16[512,128]{1,0:T(8,128)(2,1)S(1)}) custom-call(s32[32,128]{1,0:T(8,128)S(1)} %get-tuple-element.33.lines.refs_1_.refs_0_, bf16[7,512,128]{2,1,0:T(8,128)(2,1)S(1)} %copy-done.2), custom_call_target="tpu_custom_call" | custom-call | flops 500000000 | bytes 1048576 | tf_op jit(solution)/shard_map/pallas_call | solution.py:328
  9.0 0.0 collective-permute-done.3.shard.refs_0_
  9.0 0.5 %shard_map.116.refs_2_ = bf16[912,128]{1,0:T(8,128)(2,1)S(1)} custom-call(s32[32,128]{1,0:T(8,128)S(1)} %get-tuple-element.33.lines.refs_1_.refs_0_, s32[8,128]{1,0:T(8,128)S(1)} %get-tuple-element.34._, bf16[7,512,128]{2,1,0:T(8,128)(2,1)S(1)} %copy-done.2, bf16[16,128]{1,0:T(8,128)(2,1)S(1)} %collective-permute-done.3.shard.refs_0_), custom_call_target="tpu_custom_call" | custom-call | flops 500000000 | bytes 1048576 | tf_op jit(solution)/shard_map/pallas_call | solution.py:328
  9.6 0.5 %collective-permute-start.4 = (bf16[912,128]{1,0:T(8,128)(2,1)S(1)}, bf16[912,128]{1,0:T(8,128)(2,1)S(1)}, u32[]{:S(2)}, u32[]{:S(2)}) collective-permute-start(bf16[912,128]{1,0:T(8,128)(2,1)S(1)} %shard_map.116.refs_2_), channel_id=1, source_target_pairs={{0,1},{1,0},{2,3},{3,2},{4,5},{5,4},{6,7},{7,6},{8,9},{9,8},{10,11... | collective-permute-start | bytes 700424 | tf_op jit(solution)/shard_map/ppermute | solution.py:340
  10.1 2.5 %collective-permute-start.5 = (bf16[400,128]{1,0:T(8,128)(2,1)S(1)}, bf16[400,128]{1,0:T(8,128)(2,1)S(1)}, u32[]{:S(2)}, u32[]{:S(2)}) collective-permute-start(bf16[400,128]{1,0:T(8,128)(2,1)S(1)} %get-tuple-element.38), channel_id=1, source_target_pairs={{0,2},{1,3},{2,0},{3,1},{4,6},{5,7},{6,4},{7,5},{8,10},{9,11},{10,... | collective-permute-start | bytes 307208 | tf_op jit(solution)/shard_map/ppermute | solution.py:340
  12.6 0.0 collective-permute-start.6
  12.6 1.4 %collective-permute-start.7 = (bf16[512,128]{1,0:T(8,128)(2,1)S(1)}, bf16[512,128]{1,0:T(8,128)(2,1)S(1)}, u32[]{:S(2)}, u32[]{:S(2)}) collective-permute-start(bf16[512,128]{1,0:T(8,128)(2,1)S(1)} %get-tuple-element.40), channel_id=1, source_target_pairs={{0,2},{1,3},{2,0},{3,1},{4,6},{5,7},{6,4},{7,5},{8,10},{9,11},{10,... | collective-permute-start | bytes 393224 | tf_op jit(solution)/shard_map/ppermute | solution.py:340
  14.1 0.3 collective-permute-start.8
  14.4 2.1 %shard_map.117 = (bf16[896,128]{1,0:T(8,128)(2,1)S(1)}, bf16[3712,512]{1,0:T(8,128)(2,1)S(1)}, bf16[512,3712]{1,0:T(8,128)(2,1)S(1)}, bf16[128,3712]{1,0:T(8,128)(2,1)S(1)}, f32[32,128]{1,0:T(8,128)S(1)}) custom-call(s32[8,128]{1,0:T(8,128)S(1)} %get-tuple-element.32.refs_0_, s32[32,128]{1,0:T(8,128)S(1)} %get-tuple-element.33.lines.refs_1_.refs_0_, ...), custom_call_target="tpu_custom_call" | custom-call | flops 4000000000 | bytes 1048576 | tf_op jit(solution)/shard_map/pallas_call | solution.py:328
  16.5 0.0 copy-start.4
  16.5 0.0 copy-start.7
  16.5 0.0 collective-permute-done.5.refs_2_.refs_0_.refs_3_
  16.5 1.6 %collective-permute-done.6.refs_3_.refs_1_.refs_4_ = bf16[400,128]{1,0:T(8,128)(2,1)S(1)} collective-permute-done((bf16[400,128]{1,0:T(8,128)(2,1)S(1)}, bf16[400,128]{1,0:T(8,128)(2,1)S(1)}, u32[]{:S(2)}, u32[]{:S(2)}) %collective-permute-start.6) | collective-permute-done | bytes 102432 | tf_op jit(solution)/shard_map/ppermute | solution.py:340
  18.1 0.0 collective-permute-done.4.refs_1_.refs_2_
  18.1 2.6 %collective-permute-start.9 = (bf16[64,128]{1,0:T(8,128)(2,1)S(1)}, bf16[64,128]{1,0:T(8,128)(2,1)S(1)}, u32[]{:S(2)}, u32[]{:S(2)}) collective-permute-start(bf16[64,128]{1,0:T(8,128)(2,1)S(1)} %shard_map.119.group.refs_1_), channel_id=1, source_target_pairs={{16,0},{20,4},{24,8},{28,12},{0,16},{4,20},{8,24},{12,28},{17,1},{... | collective-permute-start | bytes 49160 | tf_op jit(solution)/shard_map/ppermute | solution.py:423
  20.7 0.3 shard_map.120
  21.0 1.0 %shard_map.121 = (f32[128,512]{1,0:T(8,128)S(1)}, f32[128,512]{1,0:T(8,128)S(1)}) custom-call(bf16[896,128]{1,0:T(8,128)(2,1)S(1)} %get-tuple-element.35.refs_0_.refs_1_, bf16[912,128]{1,0:T(8,128)(2,1)S(1)} %collective-permute-done.4.refs_1_.refs_2_, bf16[3712,512]{1,0:T(8,128)(2,1)S(1)} %get-tuple-element.44.refs_2_.refs_1_.refs_7_.down, ...), custom_call_target="tpu_custom_call" | custom-call | flops 4000000000 | bytes 1048576 | tf_op jit(solution)/shard_map/pallas_call | solution.py:328
  22.1 0.6 %shard_map.122 = (f32[128,512]{1,0:T(8,128)S(1)}, f32[128,512]{1,0:T(8,128)S(1)}) custom-call(bf16[400,128]{1,0:T(8,128)(2,1)S(1)} %collective-permute-done.5.refs_2_.refs_0_.refs_3_, bf16[400,128]{1,0:T(8,128)(2,1)S(1)} %collective-permute-done.6.refs_3_.refs_1_.refs_4_, bf16[3712,512]{1,0:T(8,128)(2,1)S(1)} %get-tuple-element.44.refs_2_.refs_1_.refs_7_.down, ...), custom_call_target="tpu_custom_call" | custom-call | flops 4000000000 | bytes 1048576 | tf_op jit(solution)/shard_map/pallas_call | solution.py:328
  22.6 0.0 collective-permute-done.7.refs_0_.refs_5_
  22.6 0.4 shard_map.123
  23.0 0.4 collective-permute-done.8.refs_0_.refs_6_
  23.4 0.0 collective-permute-done.9.refs_2_
  23.4 1.0 %shard_map.124 = (bf16[128,128]{1,0:T(8,128)(2,1)S(1)}, bf16[128,512]{1,0:T(8,128)(2,1)S(1)}, bf16[128,512]{1,0:T(8,128)(2,1)S(1)}, bf16[640,128]{1,0:T(8,128)(2,1)S(1)}) custom-call(bf16[512,128]{1,0:T(8,128)(2,1)S(1)} %collective-permute-done.8.refs_0_.refs_6_, bf16[64,128]{1,0:T(8,128)(2,1)S(1)} %shard_map.119.group.refs_1_, ...), custom_call_target="tpu_custom_call" | custom-call | flops 4000000000 | bytes 1048576 | tf_op jit(solution)/shard_map/pallas_call | solution.py:328
  24.4 0.5 %shard_map.129 = bf16[640,128]{1,0:T(8,128)(2,1)S(1)} custom-call(bf16[128,512]{1,0:T(8,128)(2,1)S(1)} %get-tuple-element.55.low.refs_8_, bf16[128,512]{1,0:T(8,128)(2,1)S(1)} %get-tuple-element.56.grad, bf16[3712,512]{1,0:T(8,128)(2,1)S(1)} %get-tuple-element.44.refs_2_.refs_1_.refs_7_.down, ...), custom_call_target="tpu_custom_call" | custom-call | flops 4000000000 | bytes 1048576 | tf_op jit(solution)/shard_map/pallas_call | solution.py:328
  24.9 0.4 shard_map.125
  25.3 1.0 %shard_map.126 = (bf16[896,128]{1,0:T(8,128)(2,1)S(1)}, bf16[896,128]{1,0:T(8,128)(2,1)S(1)}) custom-call(bf16[128,512]{1,0:T(8,128)(2,1)S(1)} %get-tuple-element.55.low.refs_8_, bf16[128,512]{1,0:T(8,128)(2,1)S(1)} %get-tuple-element.56.grad, bf16[3712,512]{1,0:T(8,128)(2,1)S(1)} %get-tuple-element.44.refs_2_.refs_1_.refs_7_.down, ...), custom_call_target="tpu_custom_call" | custom-call | flops 4000000000 | bytes 1048576 | tf_op jit(solution)/shard_map/pallas_call | solution.py:328
  26.3 1.1 %collective-permute-start.11 = (bf16[256,128]{1,0:T(8,128)(2,1)S(1)}, bf16[256,128]{1,0:T(8,128)(2,1)S(1)}, u32[]{:S(2)}, u32[]{:S(2)}) collective-permute-start(bf16[256,128]{1,0:T(8,128)(2,1)S(1)} %get-tuple-element.57._), channel_id=1, source_target_pairs={{0,2},{1,3},{2,0},{3,1},{4,6},{5,7},{6,4},{7,5},{8,10},{9,11},{10,... | collective-permute-start | bytes 196616 | tf_op jit(solution)/shard_map/ppermute | solution.py:340
  27.4 0.5 %collective-permute-start.14 = (bf16[640,128]{1,0:T(8,128)(2,1)S(1)}, bf16[640,128]{1,0:T(8,128)(2,1)S(1)}, u32[]{:S(2)}, u32[]{:S(2)}) collective-permute-start(bf16[640,128]{1,0:T(8,128)(2,1)S(1)} %shard_map.129), channel_id=1, source_target_pairs={{0,3},{1,2},{2,1},{3,0},{4,7},{5,6},{6,5},{7,4},{8,11},{9,10},{10,... | collective-permute-start | bytes 491528 | tf_op jit(solution)/shard_map/ppermute | solution.py:340
  27.8 0.7 %collective-permute-start.10 = (bf16[896,128]{1,0:T(8,128)(2,1)S(1)}, bf16[896,128]{1,0:T(8,128)(2,1)S(1)}, u32[]{:S(2)}, u32[]{:S(2)}) collective-permute-start(bf16[896,128]{1,0:T(8,128)(2,1)S(1)} %get-tuple-element.59), channel_id=1, source_target_pairs={{0,1},{1,0},{2,3},{3,2},{4,5},{5,4},{6,7},{7,6},{8,9},{9,8},{10,11... | collective-permute-start | bytes 688136 | tf_op jit(solution)/shard_map/ppermute | solution.py:340
  28.5 1.0 %collective-permute-start.13 = (bf16[640,128]{1,0:T(8,128)(2,1)S(1)}, bf16[640,128]{1,0:T(8,128)(2,1)S(1)}, u32[]{:S(2)}, u32[]{:S(2)}) collective-permute-start(bf16[640,128]{1,0:T(8,128)(2,1)S(1)} %get-tuple-element.61), channel_id=1, source_target_pairs={{0,2},{1,3},{2,0},{3,1},{4,6},{5,7},{6,4},{7,5},{8,10},{9,11},{10,... | collective-permute-start | bytes 491528 | tf_op jit(solution)/shard_map/ppermute | solution.py:340
  29.5 0.3 collective-permute-start.12
  29.9 2.4 %shard_map.127 = bf16[128,3456]{1,0:T(8,128)(2,1)} custom-call(s32[8,128]{1,0:T(8,128)S(1)} %get-tuple-element.32.refs_0_, bf16[896,128]{1,0:T(8,128)(2,1)S(1)} %get-tuple-element.35.refs_0_.refs_1_, bf16[912,128]{1,0:T(8,128)(2,1)S(1)} %collective-permute-done.4.refs_1_.refs_2_, bf16[400,128]{1,0:T(8,128)(2,1)S(1)} %collective-permute-done.5.refs_2_.refs_0_.refs_3_, ...), custom_call_target="tpu_custom_call" | custom-call | flops 4000000000 | bytes 1048576 | tf_op jit(solution)/shard_map/pallas_call | solution.py:328
  32.3 0.6 %shard_map.128.refs_1_ = f32[7,512,128]{2,1,0:T(8,128)S(1)} custom-call(s32[32,128]{1,0:T(8,128)S(1)} %get-tuple-element.33.lines.refs_1_.refs_0_, bf16[896,128]{1,0:T(8,128)(2,1)S(1)} %get-tuple-element.58.refs_11_.refs_1_, bf16[896,128]{1,0:T(8,128)(2,1)S(1)} %collective-permute-done.10.refs_2_), custom_call_target="tpu_custom_call" | custom-call | flops 4000000000 | bytes 1048576 | tf_op jit(solution)/shard_map/pallas_call | solution.py:328
  33.0 0.9 %collective-permute-done.14.refs_3_ = bf16[640,128]{1,0:T(8,128)(2,1)S(1)} collective-permute-done((bf16[640,128]{1,0:T(8,128)(2,1)S(1)}, bf16[640,128]{1,0:T(8,128)(2,1)S(1)}, u32[]{:S(2)}, u32[]{:S(2)}) %collective-permute-start.14) | collective-permute-done | bytes 163872 | tf_op jit(solution)/shard_map/ppermute | solution.py:340
  33.8 4.2 %collective-permute-done.13.refs_2_ = bf16[640,128]{1,0:T(8,128)(2,1)S(1)} collective-permute-done((bf16[640,128]{1,0:T(8,128)(2,1)S(1)}, bf16[640,128]{1,0:T(8,128)(2,1)S(1)}, u32[]{:S(2)}, u32[]{:S(2)}) %collective-permute-start.13) | collective-permute-done | bytes 163872 | tf_op jit(solution)/shard_map/ppermute | solution.py:340
  38.0 1.3 %shard_map.130.refs_4_ = f32[1,7,512,128]{3,2,1,0:T(8,128)} custom-call(s32[32,128]{1,0:T(8,128)S(1)} %get-tuple-element.33.lines.refs_1_.refs_0_, f32[7,512,128]{2,1,0:T(8,128)S(1)} %shard_map.128.refs_1_, bf16[640,128]{1,0:T(8,128)(2,1)S(1)} %collective-permute-done.13.refs_2_, bf16[640,128]{1,0:T(8,128)(2,1)S(1)} %collective-permute-done.14.refs_3_), custom_call_target="tpu_custom_call" | custom-call | tf_op jit(solution)/shard_map/pallas_call | solution.py:501
  39.4 0.0 collective-permute-done.11.refs_2_
  39.4 0.0 collective-permute-done.12.refs_3_
  39.4 1.1 %shard_map.131 = f32[1,7,512,128]{3,2,1,0:T(8,128)} custom-call(s32[32,128]{1,0:T(8,128)S(1)} %get-tuple-element.33.lines.refs_1_.refs_0_, f32[7,512,128]{2,1,0:T(8,128)S(1)} %shard_map.128.refs_1_, bf16[256,128]{1,0:T(8,128)(2,1)S(1)} %collective-permute-done.11.refs_2_, ...), custom_call_target="tpu_custom_call", output_to_operand_aliasing={{}: (4, {})} | custom-call | tf_op jit(solution)/shard_map/pallas_call | solution.py:501
  (19 shorter events, 0.0 us)
Async XLA Ops:
  0.6 6.5 %copy-start.2 = (bf16[7,512,128]{2,1,0:T(8,128)(2,1)S(1)}, bf16[7,512,128]{2,1,0:T(8,128)(2,1)}, u32[]{:S(2)}) copy-start(bf16[7,512,128]{2,1,0:T(8,128)(2,1)} %refs_3_.1) | copy-start | bytes 2752516
  0.6 6.5 %copy-start.5 = (s32[128,26]{0,1:T(8,128)S(1)}, s32[128,26]{0,1:T(8,128)}, u32[]{:S(2)}) copy-start(s32[128,26]{0,1:T(8,128)} %param.13) | copy-start | bytes 39940
  0.7 6.5 %copy-start.8 = (s32[26]{0:T(128)S(1)}, s32[26]{0:T(128)}, u32[]{:S(2)}) copy-start(s32[26]{0:T(128)} %refs_0_.1) | copy-start | bytes 316
  0.7 4.5 %collective-permute-start = (s32[26,128]{1,0:T(8,128)}, s32[26,128]{1,0:T(8,128)S(1)}, u32[]{:S(2)}, u32[]{:S(2)}) collective-permute-start(s32[26,128]{1,0:T(8,128)} %bitcast.3), channel_id=1, source_target_pairs={{0,1},{1,0},{2,3},{3,2},{4,5},{5,4},{6,7},{7,6},{8,9},{9,8},{10,11... | collective-permute-start | bytes 39944 | tf_op jit(solution)/shard_map/ppermute | solution.py:340
  1.2 4.5 %collective-permute-start.1 = (s32[26,128]{1,0:T(8,128)}, s32[26,128]{1,0:T(8,128)S(1)}, u32[]{:S(2)}, u32[]{:S(2)}) collective-permute-start(s32[26,128]{1,0:T(8,128)} %bitcast.4), channel_id=1, source_target_pairs={{0,2},{1,3},{2,0},{3,1},{4,6},{5,7},{6,4},{7,5},{8,10},{9,11},{10,... | collective-permute-start | bytes 39944 | tf_op jit(solution)/shard_map/ppermute | solution.py:340
  3.8 3.4 %collective-permute-start.2 = (s32[26,128]{1,0:T(8,128)}, s32[26,128]{1,0:T(8,128)S(1)}, u32[]{:S(2)}, u32[]{:S(2)}) collective-permute-start(s32[26,128]{1,0:T(8,128)} %bitcast.5), channel_id=1, source_target_pairs={{0,3},{1,2},{2,1},{3,0},{4,7},{5,6},{6,5},{7,4},{8,11},{9,10},{10,... | collective-permute-start | bytes 39944 | tf_op jit(solution)/shard_map/ppermute | solution.py:340
  3.8 5.2 %collective-permute-start.3 = (bf16[16,128]{1,0:T(8,128)(2,1)}, bf16[16,128]{1,0:T(8,128)(2,1)S(1)}, u32[]{:S(2)}, u32[]{:S(2)}) collective-permute-start(bf16[16,128]{1,0:T(8,128)(2,1)} %param.10), channel_id=1, source_target_pairs={{0,0},{5,1},{10,2},{15,3},{4,4},{1,5},{14,6},{11,7},{8,8},{13,9},{... | collective-permute-start | bytes 12296 | tf_op jit(solution)/shard_map/ppermute | solution.py:351
  5.2 9.2 %copy-start.3 = (bf16[128,3456]{1,0:T(8,128)(2,1)S(1)}, bf16[128,3456]{1,0:T(8,128)(2,1)}, u32[]{:S(2)}) copy-start(bf16[128,3456]{1,0:T(8,128)(2,1)} %refs_6_.3) | copy-start | bytes 2654212
  5.2 9.2 %copy-start = (bf16[3456,512]{1,0:T(8,128)(2,1)S(1)}, bf16[3456,512]{1,0:T(8,128)(2,1)}, u32[]{:S(2)}) copy-start(bf16[3456,512]{1,0:T(8,128)(2,1)} %refs_4_.1) | copy-start | bytes 10616836
  5.2 9.2 %copy-start.1 = (bf16[512,3456]{1,0:T(8,128)(2,1)S(1)}, bf16[512,3456]{1,0:T(8,128)(2,1)}, u32[]{:S(2)}) copy-start(bf16[512,3456]{1,0:T(8,128)(2,1)} %refs_5_.1) | copy-start | bytes 10616836
  5.2 9.2 %copy-start.6 = (f32[3456]{0:T(1024)S(1)}, f32[3456]{0:T(1024)}, u32[]{:S(2)}) copy-start(f32[3456]{0:T(1024)} %param.18) | copy-start | bytes 41476
  9.6 8.5 %collective-permute-start.4 = (bf16[912,128]{1,0:T(8,128)(2,1)S(1)}, bf16[912,128]{1,0:T(8,128)(2,1)S(1)}, u32[]{:S(2)}, u32[]{:S(2)}) collective-permute-start(bf16[912,128]{1,0:T(8,128)(2,1)S(1)} %shard_map.116.refs_2_), channel_id=1, source_target_pairs={{0,1},{1,0},{2,3},{3,2},{4,5},{5,4},{6,7},{7,6},{8,9},{9,8},{10,11... | collective-permute-start | bytes 700424 | tf_op jit(solution)/shard_map/ppermute | solution.py:340
  10.1 6.4 %collective-permute-start.5 = (bf16[400,128]{1,0:T(8,128)(2,1)S(1)}, bf16[400,128]{1,0:T(8,128)(2,1)S(1)}, u32[]{:S(2)}, u32[]{:S(2)}) collective-permute-start(bf16[400,128]{1,0:T(8,128)(2,1)S(1)} %get-tuple-element.38), channel_id=1, source_target_pairs={{0,2},{1,3},{2,0},{3,1},{4,6},{5,7},{6,4},{7,5},{8,10},{9,11},{10,... | collective-permute-start | bytes 307208 | tf_op jit(solution)/shard_map/ppermute | solution.py:340
  12.6 5.5 %collective-permute-start.6 = (bf16[400,128]{1,0:T(8,128)(2,1)S(1)}, bf16[400,128]{1,0:T(8,128)(2,1)S(1)}, u32[]{:S(2)}, u32[]{:S(2)}) collective-permute-start(bf16[400,128]{1,0:T(8,128)(2,1)S(1)} %get-tuple-element.39), channel_id=1, source_target_pairs={{0,3},{1,2},{2,1},{3,0},{4,7},{5,6},{6,5},{7,4},{8,11},{9,10},{10,... | collective-permute-start | bytes 307208 | tf_op jit(solution)/shard_map/ppermute | solution.py:340
  12.6 10.0 %collective-permute-start.7 = (bf16[512,128]{1,0:T(8,128)(2,1)S(1)}, bf16[512,128]{1,0:T(8,128)(2,1)S(1)}, u32[]{:S(2)}, u32[]{:S(2)}) collective-permute-start(bf16[512,128]{1,0:T(8,128)(2,1)S(1)} %get-tuple-element.40), channel_id=1, source_target_pairs={{0,2},{1,3},{2,0},{3,1},{4,6},{5,7},{6,4},{7,5},{8,10},{9,11},{10,... | collective-permute-start | bytes 393224 | tf_op jit(solution)/shard_map/ppermute | solution.py:340
  14.1 9.4 %collective-permute-start.8 = (bf16[512,128]{1,0:T(8,128)(2,1)S(1)}, bf16[512,128]{1,0:T(8,128)(2,1)S(1)}, u32[]{:S(2)}, u32[]{:S(2)}) collective-permute-start(bf16[512,128]{1,0:T(8,128)(2,1)S(1)} %get-tuple-element.41), channel_id=1, source_target_pairs={{0,3},{1,2},{2,1},{3,0},{4,7},{5,6},{6,5},{7,4},{8,11},{9,10},{10,... | collective-permute-start | bytes 393224 | tf_op jit(solution)/shard_map/ppermute | solution.py:340
  16.5 4.2 %copy-start.4 = (bf16[128,128]{1,0:T(8,128)(2,1)S(1)}, bf16[128,128]{1,0:T(8,128)(2,1)}, u32[]{:S(2)}) copy-start(bf16[128,128]{1,0:T(8,128)(2,1)} %dense.1) | copy-start | bytes 98308
  16.5 4.2 %copy-start.7 = (s32[128,16]{0,1:T(8,128)S(1)}, s32[128,16]{0,1:T(8,128)}, u32[]{:S(2)}) copy-start(s32[128,16]{0,1:T(8,128)} %param.11) | copy-start | bytes 24580
  18.1 5.3 %collective-permute-start.9 = (bf16[64,128]{1,0:T(8,128)(2,1)S(1)}, bf16[64,128]{1,0:T(8,128)(2,1)S(1)}, u32[]{:S(2)}, u32[]{:S(2)}) collective-permute-start(bf16[64,128]{1,0:T(8,128)(2,1)S(1)} %shard_map.119.group.refs_1_), channel_id=1, source_target_pairs={{16,0},{20,4},{24,8},{28,12},{0,16},{4,20},{8,24},{12,28},{17,1},{... | collective-permute-start | bytes 49160 | tf_op jit(solution)/shard_map/ppermute | solution.py:423
  26.3 13.0 %collective-permute-start.11 = (bf16[256,128]{1,0:T(8,128)(2,1)S(1)}, bf16[256,128]{1,0:T(8,128)(2,1)S(1)}, u32[]{:S(2)}, u32[]{:S(2)}) collective-permute-start(bf16[256,128]{1,0:T(8,128)(2,1)S(1)} %get-tuple-element.57._), channel_id=1, source_target_pairs={{0,2},{1,3},{2,0},{3,1},{4,6},{5,7},{6,4},{7,5},{8,10},{9,11},{10,... | collective-permute-start | bytes 196616 | tf_op jit(solution)/shard_map/ppermute | solution.py:340
  27.4 6.4 %collective-permute-start.14 = (bf16[640,128]{1,0:T(8,128)(2,1)S(1)}, bf16[640,128]{1,0:T(8,128)(2,1)S(1)}, u32[]{:S(2)}, u32[]{:S(2)}) collective-permute-start(bf16[640,128]{1,0:T(8,128)(2,1)S(1)} %shard_map.129), channel_id=1, source_target_pairs={{0,3},{1,2},{2,1},{3,0},{4,7},{5,6},{6,5},{7,4},{8,11},{9,10},{10,... | collective-permute-start | bytes 491528 | tf_op jit(solution)/shard_map/ppermute | solution.py:340
  27.8 4.5 %collective-permute-start.10 = (bf16[896,128]{1,0:T(8,128)(2,1)S(1)}, bf16[896,128]{1,0:T(8,128)(2,1)S(1)}, u32[]{:S(2)}, u32[]{:S(2)}) collective-permute-start(bf16[896,128]{1,0:T(8,128)(2,1)S(1)} %get-tuple-element.59), channel_id=1, source_target_pairs={{0,1},{1,0},{2,3},{3,2},{4,5},{5,4},{6,7},{7,6},{8,9},{9,8},{10,11... | collective-permute-start | bytes 688136 | tf_op jit(solution)/shard_map/ppermute | solution.py:340
  28.5 9.5 %collective-permute-start.13 = (bf16[640,128]{1,0:T(8,128)(2,1)S(1)}, bf16[640,128]{1,0:T(8,128)(2,1)S(1)}, u32[]{:S(2)}, u32[]{:S(2)}) collective-permute-start(bf16[640,128]{1,0:T(8,128)(2,1)S(1)} %get-tuple-element.61), channel_id=1, source_target_pairs={{0,2},{1,3},{2,0},{3,1},{4,6},{5,7},{6,4},{7,5},{8,10},{9,11},{10,... | collective-permute-start | bytes 491528 | tf_op jit(solution)/shard_map/ppermute | solution.py:340
  29.5 9.8 %collective-permute-start.12 = (bf16[256,128]{1,0:T(8,128)(2,1)S(1)}, bf16[256,128]{1,0:T(8,128)(2,1)S(1)}, u32[]{:S(2)}, u32[]{:S(2)}) collective-permute-start(bf16[256,128]{1,0:T(8,128)(2,1)S(1)} %get-tuple-element.60), channel_id=1, source_target_pairs={{0,3},{1,2},{2,1},{3,0},{4,7},{5,6},{6,5},{7,4},{8,11},{9,10},{10,... | collective-permute-start | bytes 196616 | tf_op jit(solution)/shard_map/ppermute | solution.py:340
